TPU v7x, 32 devices: a whole 2x2x4 slice. The times are simulated.
32 devices in a mesh: tile: 8 (over z, x), chan: 4 (over y, core).
Axes of the slice: x: 2, y: 2, z: 4, core: 2. Of those that a mesh axis runs over, the one named last changes fastest.
Arguments:
- tokens: bfloat16 [512, 512], P('tile', 'chan'), may hold values from -6 to 6
- cell_source: int32 [8, 64], replicated, may hold values from 0 to 511, as said below
- gain: float32 [512], P('chan'), may hold values from 0.5 to 1.5
- shift: float32 [512], P('chan'), may hold values from -3 to 3
- weight: bfloat16 [27, 512, 512], P(None, None, 'chan'), may hold values from -0.0546875 to 0.0546875
- bias: float32 [512], P('chan'), may hold values from -3 to 3
- cotangent: bfloat16 [8, 2, 8, 16, 512], P('tile', None, None, None, 'chan'), may hold values from -6 to 6
Outputs:
- decoded: bfloat16 [8, 2, 8, 16, 512], P('tile', None, None, None, 'chan')
- token_grad: bfloat16 [512, 512], P('tile', 'chan')
Inputs may be any that keep to these rules, and one draw needn't show every extreme that they name: `cell_source`: every token fills exactly one cell. Token t is held by owner t // 64. A tile takes either none or exactly 16 of its cells from an owner, and those 16 tokens are consecutive in the owner's order starting at a multiple of 16; the set of differences (tile - owner) mod 8 from which a tile takes cells is the same for every tile.
All inputs are finite; a program needn't handle non-finite values.
Results may differ from a plain program's by a relative error of at most 0.0041.
Values may be sent and summed in bfloat16 or wider, within the bound.
No kernel may reach another device: no remote copies, remote signals or barrier semaphores. Data moves between devices by JAX's collectives and lax.ppermute only.
A program may use at most 64 MiB of HBM per device.

v0:
```python
import jax
import jax.numpy as jnp
from jax import lax
from jax.sharding import PartitionSpec as P

CHANNELS = 512
GROUPS = 32
FRAMES = 2
TILE_H = 4
TILE_W = 8


def extended(cells, sides, width):
    for axis, dim in sides:
        count = lax.axis_size(axis)
        ends = count - 1
        head = lax.slice_in_dim(cells, 0, width, axis=dim)
        tail = lax.slice_in_dim(cells, cells.shape[dim] - width, cells.shape[dim], axis=dim)
        cells = jnp.concatenate(
            [
                lax.ppermute(tail, axis, [(i, (i + 1) % count) for i in range(ends)]),
                cells,
                lax.ppermute(head, axis, [((i + 1) % count, i) for i in range(ends)]),
            ],
            axis=dim,
        )
    return cells


def passed_along(block, axis, distance):
    devices = range(lax.axis_size(axis))
    route = [(i - distance, i) for i in devices if i - distance in devices]
    return lax.ppermute(block, axis, route)


def normalize(values, gain, shift):
    group = CHANNELS // GROUPS
    grouped = values.reshape(values.shape[0], values.shape[1], values.shape[2] // group, group)
    center = jnp.mean(grouped, axis=(1, 3), keepdims=True)
    centred = grouped - center
    spread = jnp.mean(centred * centred, axis=(1, 3), keepdims=True)
    normed = (centred * lax.rsqrt(spread + 1e-06)).reshape(values.shape) * gain + shift
    return jax.nn.silu(normed)


def edge_mask(length, kind):
    across = min(lax.axis_size("tile"), 16)
    column = lax.axis_index("tile") % across
    left_keep = (column != 0).astype(kind)
    right_keep = (column != across - 1).astype(kind)
    places = jnp.arange(length)
    return jnp.where(
        places == 0, left_keep, jnp.where(places == length - 1, right_keep, jnp.ones((), kind))
    )


def add_rims(values):
    across = min(lax.axis_size("tile"), 16)
    widened = extended(values, (("tile", 2),), 1)
    widened = widened * edge_mask(widened.shape[2], widened.dtype)[None, None, :, None]
    above = passed_along(widened[:, -1:], "tile", across)
    below = passed_along(widened[:, :1], "tile", -across)
    return jnp.concatenate([above, widened, below], axis=1)


def remove_rims(gradient):
    across = min(lax.axis_size("tile"), 16)
    from_below = passed_along(gradient[:, :1], "tile", -across)
    from_above = passed_along(gradient[:, -1:], "tile", across)
    inner = gradient[:, 1:-1]
    inner = inner.at[:, :1].add(from_above).at[:, -1:].add(from_below)
    outer = extended(inner, (("tile", 2),), 1)
    keeping = edge_mask(outer.shape[2], outer.dtype)
    middle = inner[:, :, 1:-1]
    middle = middle.at[:, :, :1].add(outer[:, :, :1] * keeping[0])
    middle = middle.at[:, :, -1:].add(outer[:, :, -1:] * keeping[-1])
    return middle


def widen_channels(values):
    return lax.all_gather(values, "chan", axis=3, tiled=True)


def narrow_channels(values):
    return lax.psum_scatter(values, "chan", scatter_dimension=3, tiled=True)


def local(tokens, cell_source, gain, shift, weight, bias, cotangent):
    members = lax.axis_size("tile")
    device = lax.axis_index("tile")
    tile_cells, my_channels = tokens.shape
    capacity = max(2, tile_cells // (members // 2))
    owners = cell_source // tile_cells
    is_mine = owners == device
    places = jnp.arange(tile_cells, dtype=jnp.int32)[None, :]
    chosen = jnp.argsort(jnp.where(is_mine, places, places + tile_cells), axis=1)[:, :capacity]
    usable = jnp.take_along_axis(is_mine, chosen, axis=1)
    local_rows = jnp.where(
        usable, jnp.take_along_axis(cell_source, chosen, axis=1) - device * tile_cells, 0
    )
    outgoing = tokens[local_rows] * usable[:, :, None].astype(tokens.dtype)
    incoming = lax.all_to_all(outgoing, "tile", split_axis=0, concat_axis=0, tiled=True)
    my_sources = lax.dynamic_index_in_dim(cell_source, device, 0, keepdims=False)
    senders = my_sources // tile_cells
    earlier = jnp.arange(tile_cells)[None, :] < jnp.arange(tile_cells)[:, None]
    arrival = jnp.sum((senders[:, None] == senders[None, :]) & earlier, axis=1)
    arrival = jnp.minimum(arrival, capacity - 1)
    arrived = incoming[senders, arrival]
    features = arrived.astype(jnp.float32).reshape(1, tile_cells, my_channels)
    activated = normalize(features, gain, shift).astype(jnp.bfloat16)
    activated = activated.reshape(FRAMES, TILE_H, TILE_W, my_channels)
    surrounded = add_rims(widen_channels(activated))
    upsampled = jnp.repeat(jnp.repeat(surrounded, 2, axis=1), 2, axis=2)[:, 1:-1, 1:-1]
    time_padded = jnp.concatenate([upsampled[:1], upsampled[:1], upsampled], axis=0)
    out_h = 2 * TILE_H
    out_w = 2 * TILE_W
    summed = jnp.zeros((FRAMES * out_h * out_w, my_channels), jnp.float32)
    for offset in range(27):
        time_lag, row_shift, col_shift = (offset // 9, offset // 3 % 3, offset % 3)
        window = time_padded[
            time_lag : time_lag + FRAMES,
            row_shift : row_shift + out_h,
            col_shift : col_shift + out_w,
        ]
        summed = summed + jnp.dot(
            window.reshape(-1, window.shape[-1]), weight[offset], preferred_element_type=jnp.float32
        )
    decoded = (summed + bias).astype(jnp.bfloat16).reshape(1, FRAMES, out_h, out_w, my_channels)
    grads = cotangent.reshape(-1, my_channels)
    accum = jnp.zeros(time_padded.shape, jnp.float32)
    for offset in range(27):
        time_lag, row_shift, col_shift = (offset // 9, offset // 3 % 3, offset % 3)
        term = jnp.dot(grads, weight[offset].T, preferred_element_type=jnp.float32)
        accum = accum.at[
            time_lag : time_lag + FRAMES,
            row_shift : row_shift + out_h,
            col_shift : col_shift + out_w,
        ].add(term.reshape(FRAMES, out_h, out_w, -1))
    frames_back = accum[2:].at[0].add(accum[0] + accum[1])
    spread_back = jnp.pad(frames_back, ((0, 0), (1, 1), (1, 1), (0, 0)))
    folded = spread_back.reshape(FRAMES, TILE_H + 2, 2, TILE_W + 2, 2, -1).sum(axis=(2, 4))
    adjoint = narrow_channels(remove_rims(folded))
    unused, pullback = jax.vjp(lambda values: normalize(values, gain, shift), features)
    (d_features,) = pullback(adjoint.reshape(1, tile_cells, my_channels))
    rounded_back = d_features[0].astype(jnp.bfloat16)
    returning = (
        jnp.zeros((members, capacity, my_channels), jnp.bfloat16)
        .at[senders, arrival]
        .set(rounded_back)
    )
    returned = lax.all_to_all(returning, "tile", split_axis=0, concat_axis=0, tiled=True)
    token_grad = (
        jnp.zeros((tile_cells, my_channels), jnp.bfloat16)
        .at[local_rows]
        .add(returned * usable[:, :, None].astype(jnp.bfloat16))
    )
    return (decoded, token_grad)


def solution(mesh):
    in_specs = (
        P("tile", "chan"),
        P(),
        P("chan"),
        P("chan"),
        P(None, None, "chan"),
        P("chan"),
        P("tile", None, None, None, "chan"),
    )
    out_specs = (P("tile", None, None, None, "chan"), P("tile", "chan"))
    return jax.shard_map(local, mesh=mesh, in_specs=in_specs, out_specs=out_specs, check_vma=False)
```

profile of v0, /device:TPU:0, one launch (start us, length us, event | category | flops | bytes accessed | tf_op | source)
XLA Modules:
  0.0 188.4 jit_solution(2758177810722119204)
XLA Ops:
  9.1 1.1 convolution_add_fusion.25
  11.4 1.1 convolution_add_fusion.24
  13.3 1.1 fusion.7
  14.5 1.1 convolution_add_fusion.22
  17.1 3.1 %convolution_add_fusion.21 = f32[2,8,16,512]{3,2,1,0:T(8,128)S(1)} fusion(f32[4,10,18,512]{3,2,1,0:T(8,128)S(1)} %scatter-add.120, s32[]{:T(128)} %bitcast.77, s32[]{:T(128)} %bitcast.78, s32[]{:T(128)} %bitcast.79, bf16[27,512,128]{2,1,0:T(8,128)(2,1)} %param.75, bf16[1,2,8,16,128]{4,3,2,1,0:T(8,128)(2,1)S(1)} %copy-done), kind=kOutput, calls=%fused_computation.34 | convolution fusion | flops 33685504 | bytes 1246720 | tf_op jit(solution)/shard_map/dot_general | solution.py:133
  20.2 2.8 %scatter-add.121 = f32[4,10,18,512]{3,2,1,0:T(8,128)S(1)} dynamic-update-slice(f32[4,10,18,512]{3,2,1,0:T(8,128)S(1)} %scatter-add.120, f32[2,8,16,512]{3,2,1,0:T(8,128)S(1)} %convolution_add_fusion.21, s32[]{:T(128)} %bitcast.77, s32[]{:T(128)} %bitcast.78, s32[]{:T(128)} %bitcast.79, s32[]{:T(128)} %constant.1101.clone.1) | dynamic-update-slice | bytes 1048580 | tf_op jit(solution)/shard_map/scatter-add | solution.py:138
  23.1 1.2 fusion.6
  24.2 1.1 convolution_add_fusion.19
  26.2 1.1 convolution_add_fusion.18
  28.2 1.1 fusion.5
  29.3 1.1 convolution_add_fusion.16
  31.3 1.1 convolution_add_fusion.15
  33.2 1.1 fusion.4
  34.4 1.1 convolution_add_fusion.13
  36.4 1.1 convolution_add_fusion.12
  38.3 1.1 fusion.3
  39.5 1.1 convolution_add_fusion.10
  41.5 1.1 convolution_add_fusion.9
  43.4 1.1 fusion.2
  44.6 1.1 convolution_add_fusion.7
  46.6 1.1 convolution_add_fusion.6
  48.5 1.1 fusion.1
  49.7 1.1 convolution_add_fusion.4
  51.7 1.1 convolution_add_fusion.3
  53.6 1.1 fusion
  54.8 1.1 convolution_add_fusion.1
  56.7 1.1 convolution_add_fusion
  64.2 1.5 gather_fusion.2
  67.4 7.3 %all-to-all-start = ((bf16[8,16,128]{2,1,0:T(8,128)(2,1)}), bf16[8,16,128]{2,1,0:T(8,128)(2,1)S(1)}, u32[]{:S(2)}, u32[]{:S(2)}) async-start(bf16[8,16,128]{2,1,0:T(8,128)(2,1)} %broadcast_multiply_fusion.1), calls=%async_computation | async-start | bytes 65536 | tf_op jit(solution)/shard_map/all_to_all | solution.py:102
  75.9 3.7 %collective-permute-start.6 = (f32[2,4,1,512]{3,0,2,1:T(2,128)S(1)}, f32[2,4,1,512]{3,0,2,1:T(2,128)S(1)}, u32[]{:S(2)}, u32[]{:S(2)}) collective-permute-start(f32[2,4,1,512]{3,0,2,1:T(2,128)S(1)} %get-tuple-element.427), channel_id=1, source_target_pairs={{0,4},{4,8},{8,12},{12,16},{16,20},{20,24},{24,28},{1,5},{5,9},{9,... | collective-permute-start | bytes 49160 | tf_op jit(solution)/shard_map/ppermute | solution.py:21
  79.7 1.3 collective-permute-start.7
  81.8 3.5 %collective-permute-done.7 = f32[2,4,1,512]{3,0,2,1:T(2,128)S(1)} collective-permute-done((f32[2,4,1,512]{3,0,2,1:T(2,128)S(1)}, f32[2,4,1,512]{3,0,2,1:T(2,128)S(1)}, u32[]{:S(2)}, u32[]{:S(2)}) %collective-permute-start.7) | collective-permute-done | bytes 16416 | tf_op jit(solution)/shard_map/ppermute | solution.py:23
  86.0 7.6 %copy.221 = f32[2,4,8,512]{0,2,1,3:T(8,128)} copy(f32[2,4,8,512]{3,0,2,1:T(2,128)S(1)} %fusion.170) | data formatting | bytes 262144
  93.5 8.8 %reshape.1951 = f32[512,64]{1,0:T(8,128)} reshape(f32[512,4,8,2]{3,2,1,0:T(8,128)} %bitcast.419) | data formatting | bytes 262144
  103.9 19.5 %reduce-scatter.4.cloned.1.call-done = f32[128,64]{1,0:T(8,128)} async-done(((f32[512,64]{1,0:T(8,128)}), f32[128,64]{1,0:T(8,128)}) %reduce-scatter.4.cloned.1.call-update) | async-done | bytes 32784
  123.4 3.0 %reshape.1952 = f32[128,4,8,2]{3,2,1,0:T(8,128)S(1)} reshape(f32[128,64]{1,0:T(8,128)} %reduce-scatter.4.cloned.1.call-done) | data formatting | bytes 65536
  126.4 1.3 copy.191
  128.4 5.3 %all_gather.3 = bf16[2,4,8,512]{3,2,1,0:T(8,128)(2,1)S(1)} all-gather(bf16[2,4,8,128]{3,2,1,0:T(8,128)(2,1)S(1)} %get-tuple-element.433), channel_id=1, replica_groups=mesh['tile'=8,'chan'=4] {'chan'}, dimensions={3}, use_global_device_ids=true | all-gather | bytes 81920 | tf_op jit(solution)/shard_map/all_gather | solution.py:81
  133.7 3.4 %collective-permute-start = (bf16[2,4,1,512]{3,2,1,0:T(2,128)(2,1)S(1)}, bf16[2,4,1,512]{3,2,1,0:T(2,128)(2,1)S(1)}, u32[]{:S(2)}, u32[]{:S(2)}) collective-permute-start(bf16[2,4,1,512]{3,2,1,0:T(2,128)(2,1)S(1)} %get-tuple-element.430), channel_id=1, source_target_pairs={{0,4},{4,8},{8,12},{12,16},{16,20},{20,24},{24,28},{1,5},{5,9},{9,... | collective-permute-start | bytes 24584 | tf_op jit(solution)/shard_map/ppermute | solution.py:21
  137.0 1.3 collective-permute-start.1
  138.5 4.2 %collective-permute-done.1 = bf16[2,4,1,512]{3,2,1,0:T(2,128)(2,1)S(1)} collective-permute-done((bf16[2,4,1,512]{3,2,1,0:T(2,128)(2,1)S(1)}, bf16[2,4,1,512]{3,2,1,0:T(2,128)(2,1)S(1)}, u32[]{:S(2)}, u32[]{:S(2)}) %collective-permute-start.1) | collective-permute-done | bytes 8224 | tf_op jit(solution)/shard_map/ppermute | solution.py:23
  144.8 7.6 %scatter_fusion = bf16[8,16,128]{2,1,0:T(8,128)(2,1)} fusion(bf16[8,16,128]{2,1,0:T(8,128)(2,1)} %broadcast_in_dim.114, s32[64]{0:T(128)S(1)} %get-tuple-element.391, bf16[64,128]{1,0:T(8,128)(2,1)S(1)} %fusion.167), kind=kCustom, calls=%fused_computation.4 | custom fusion | bytes 49664 | tf_op jit(solution)/shard_map/scatter | solution.py:149
  152.3 5.4 %all-to-all-start.1 = ((bf16[8,16,128]{2,1,0:T(8,128)(2,1)}), bf16[8,16,128]{2,1,0:T(8,128)(2,1)S(1)}, u32[]{:S(2)}, u32[]{:S(2)}) async-start(bf16[8,16,128]{2,1,0:T(8,128)(2,1)} %scatter_fusion), calls=%async_computation.1 | async-start | bytes 65536 | tf_op jit(solution)/shard_map/all_to_all | solution.py:151
  158.8 2.9 %pad_maximum_fusion.1 = (bf16[2,8,16,512]{3,0,2,1:T(2,128)(2,1)S(1)}, bf16[2,8,16,512]{3,0,2,1:T(2,128)(2,1)S(1)}, bf16[2,8,16,512]{3,0,2,1:T(2,128)(2,1)S(1)}, ...) fusion(bf16[1,10,18,512]{3,0,2,1:T(2,128)(2,1)S(1)} %slice.1624), kind=kLoop, calls=%fused_computation.97 | loop fusion | flops 2621440 | bytes 1495040 | tf_op jit(solution)/shard_map/concatenate | solution.py:114
  161.8 2.5 %slice_maximum_fusion = (bf16[2,8,16,512]{3,0,2,1:T(2,128)(2,1)S(1)}, bf16[2,8,16,512]{3,0,2,1:T(2,128)(2,1)S(1)}, bf16[2,8,16,512]{3,0,2,1:T(2,128)(2,1)S(1)}, bf16[2,8,16,512]{3,0,2,1:T(2,128)(2,1)S(1)}) fusion(bf16[1,10,18,512]{3,0,2,1:T(2,128)(2,1)S(1)} %slice.1624), kind=kLoop, calls=%fused_computation.98 | loop fusion | flops 2097152 | bytes 1232896 | tf_op jit(solution)/shard_map/concatenate | solution.py:114
  164.3 2.6 %fusion.185 = (bf16[2,8,16,512]{3,0,2,1:T(2,128)(2,1)S(1)}, bf16[2,8,16,512]{3,0,2,1:T(2,128)(2,1)S(1)}, bf16[2,8,16,512]{3,0,2,1:T(2,128)(2,1)S(1)}, bf16[2,8,1...) fusion(bf16[2,12,20,512]{3,0,2,1:T(2,128)(2,1)S(1)} %bitcast.422), kind=kLoop, calls=%fused_computation.332 | loop fusion | bytes 4718592 | tf_op jit(solution)/shard_map/slice | solution.py:120
  166.8 5.1 %pad_maximum_fusion = (bf16[2,8,16,512]{3,0,2,1:T(2,128)(2,1)S(1)}, bf16[2,8,16,512]{3,0,2,1:T(2,128)(2,1)S(1)}, bf16[2,8,16,512]{3,0,2,1:T(2,128)(2,1)S(1)}, bf...) fusion(bf16[2,10,18,512]{3,0,2,1:T(2,128)(2,1)S(1)} %slice.1641, ...), kind=kLoop, calls=%fused_computation.96 | loop fusion | flops 4718592 | bytes 2912256 | tf_op jit(solution)/shard_map/concatenate | solution.py:114
  179.7 1.8 scatter_custom_fusion.1
  (178 shorter events, 39.4 us)
Async XLA Ops:
  7.2 0.8 copy-start
  58.8 3.1 %copy-start.1 = (s32[8,64]{1,0:T(8,128)S(1)}, s32[8,64]{1,0:T(8,128)}, u32[]{:S(2)}) copy-start(s32[8,64]{1,0:T(8,128)} %param.72) | copy-start | bytes 6148
  59.9 6.1 %copy-start.3 = (bf16[64,128]{1,0:T(8,128)(2,1)S(1)}, bf16[64,128]{1,0:T(8,128)(2,1)}, u32[]{:S(2)}) copy-start(bf16[64,128]{1,0:T(8,128)(2,1)} %param.71) | copy-start | bytes 49156
  60.5 15.3 %collective-permute-start.4 = (f32[2,1,10,512]{3,0,2,1:T(2,128)S(1)}, f32[2,1,10,512]{3,0,2,1:T(2,128)S(1)}, u32[]{:S(2)}, u32[]{:S(2)}) collective-permute-start(f32[2,1,10,512]{3,0,2,1:T(2,128)S(1)} %get-tuple-element.425), channel_id=1, source_target_pairs={} | collective-permute-start | bytes 122888 | tf_op jit(solution)/shard_map/ppermute | solution.py:33
  61.2 14.7 %collective-permute-start.5 = (f32[2,1,10,512]{3,0,2,1:T(2,128)S(1)}, f32[2,1,10,512]{3,0,2,1:T(2,128)S(1)}, u32[]{:S(2)}, u32[]{:S(2)}) collective-permute-start(f32[2,1,10,512]{3,0,2,1:T(2,128)S(1)} %get-tuple-element.424), channel_id=1, source_target_pairs={} | collective-permute-start | bytes 122888 | tf_op jit(solution)/shard_map/ppermute | solution.py:33
  67.4 34.9 %all-to-all-start = ((bf16[8,16,128]{2,1,0:T(8,128)(2,1)}), bf16[8,16,128]{2,1,0:T(8,128)(2,1)S(1)}, u32[]{:S(2)}, u32[]{:S(2)}) async-start(bf16[8,16,128]{2,1,0:T(8,128)(2,1)} %broadcast_multiply_fusion.1), calls=%async_computation | async-start | bytes 65536 | tf_op jit(solution)/shard_map/all_to_all | solution.py:102
  74.7 48.7 %reduce-scatter.4.cloned.1.call-start = ((), (), s32[]{:S(2)}) async-start(), calls=%async_computation.3 | async-start | bytes 327680
  75.9 5.1 %collective-permute-start.6 = (f32[2,4,1,512]{3,0,2,1:T(2,128)S(1)}, f32[2,4,1,512]{3,0,2,1:T(2,128)S(1)}, u32[]{:S(2)}, u32[]{:S(2)}) collective-permute-start(f32[2,4,1,512]{3,0,2,1:T(2,128)S(1)} %get-tuple-element.427), channel_id=1, source_target_pairs={{0,4},{4,8},{8,12},{12,16},{16,20},{20,24},{24,28},{1,5},{5,9},{9,... | collective-permute-start | bytes 49160 | tf_op jit(solution)/shard_map/ppermute | solution.py:21
  79.7 5.6 %collective-permute-start.7 = (f32[2,4,1,512]{3,0,2,1:T(2,128)S(1)}, f32[2,4,1,512]{3,0,2,1:T(2,128)S(1)}, u32[]{:S(2)}, u32[]{:S(2)}) collective-permute-start(f32[2,4,1,512]{3,0,2,1:T(2,128)S(1)} %get-tuple-element.426), channel_id=1, source_target_pairs={{4,0},{8,4},{12,8},{16,12},{20,16},{24,20},{28,24},{5,1},{9,5},{13... | collective-permute-start | bytes 49160 | tf_op jit(solution)/shard_map/ppermute | solution.py:23
  102.3 25.4 %copy-start.4 = (f32[128]{0:T(128)S(1)}, f32[128]{0:T(128)}, u32[]{:S(2)}) copy-start(f32[128]{0:T(128)} %param.74) | copy-start | bytes 1540
  102.3 25.4 %copy-start.5 = (f32[128]{0:T(128)S(1)}, f32[128]{0:T(128)}, u32[]{:S(2)}) copy-start(f32[128]{0:T(128)} %param.73) | copy-start | bytes 1540
  133.7 4.8 %collective-permute-start = (bf16[2,4,1,512]{3,2,1,0:T(2,128)(2,1)S(1)}, bf16[2,4,1,512]{3,2,1,0:T(2,128)(2,1)S(1)}, u32[]{:S(2)}, u32[]{:S(2)}) collective-permute-start(bf16[2,4,1,512]{3,2,1,0:T(2,128)(2,1)S(1)} %get-tuple-element.430), channel_id=1, source_target_pairs={{0,4},{4,8},{8,12},{12,16},{16,20},{20,24},{24,28},{1,5},{5,9},{9,... | collective-permute-start | bytes 24584 | tf_op jit(solution)/shard_map/ppermute | solution.py:21
  137.0 5.6 %collective-permute-start.1 = (bf16[2,4,1,512]{3,2,1,0:T(2,128)(2,1)S(1)}, bf16[2,4,1,512]{3,2,1,0:T(2,128)(2,1)S(1)}, u32[]{:S(2)}, u32[]{:S(2)}) collective-permute-start(bf16[2,4,1,512]{3,2,1,0:T(2,128)(2,1)S(1)} %get-tuple-element.431), channel_id=1, source_target_pairs={{4,0},{8,4},{12,8},{16,12},{20,16},{24,20},{28,24},{5,1},{9,5},{13... | collective-permute-start | bytes 24584 | tf_op jit(solution)/shard_map/ppermute | solution.py:23
  142.8 14.9 %collective-permute-start.2 = (bf16[2,1,10,512]{3,2,1,0:T(8,128)(2,1)S(1)}, bf16[2,1,10,512]{3,2,1,0:T(8,128)(2,1)S(1)}, u32[]{:S(2)}, u32[]{:S(2)}) collective-permute-start(bf16[2,1,10,512]{3,2,1,0:T(8,128)(2,1)S(1)} %get-tuple-element.428), channel_id=1, source_target_pairs={} | collective-permute-start | bytes 61448 | tf_op jit(solution)/shard_map/ppermute | solution.py:33
  143.4 14.3 %collective-permute-start.3 = (bf16[2,1,10,512]{3,2,1,0:T(8,128)(2,1)S(1)}, bf16[2,1,10,512]{3,2,1,0:T(8,128)(2,1)S(1)}, u32[]{:S(2)}, u32[]{:S(2)}) collective-permute-start(bf16[2,1,10,512]{3,2,1,0:T(8,128)(2,1)S(1)} %get-tuple-element.429), channel_id=1, source_target_pairs={} | collective-permute-start | bytes 61448 | tf_op jit(solution)/shard_map/ppermute | solution.py:33
  152.3 27.3 %all-to-all-start.1 = ((bf16[8,16,128]{2,1,0:T(8,128)(2,1)}), bf16[8,16,128]{2,1,0:T(8,128)(2,1)S(1)}, u32[]{:S(2)}, u32[]{:S(2)}) async-start(bf16[8,16,128]{2,1,0:T(8,128)(2,1)} %scatter_fusion), calls=%async_computation.1 | async-start | bytes 65536 | tf_op jit(solution)/shard_map/all_to_all | solution.py:151
  164.2 7.8 %copy-start.2 = (bf16[27,512,128]{2,1,0:T(8,128)(2,1)S(1)}, bf16[27,512,128]{2,1,0:T(8,128)(2,1)}, u32[]{:S(2)}) copy-start(bf16[27,512,128]{2,1,0:T(8,128)(2,1)} %param.75) | copy-start | bytes 10616836
  176.3 2.4 %copy-start.6 = (f32[128]{0:T(128)S(1)}, f32[128]{0:T(128)}, u32[]{:S(2)}) copy-start(f32[128]{0:T(128)} %param.76) | copy-start | bytes 1540
Sparse Core Ops, SparseCore 0:
  102.4 20.9 reduce-scatter.3
where the time goes:
time: 190 us; the launch traced here: 188 us
  local copies, waits for them, and re-layouts  58.9 us (31%)
  matrix products  39.1 us (21%)
  waiting for transfers between devices  27.3 us (14%)
  starting transfers between devices  25.1 us (13%)
  other arithmetic  17.4 us (9%)
  between operations  15.3 us (8%)
  blocking collectives  5.26 us (3%)
    dot_general x27, matrix products, local(): term = jnp.dot(grads, weight[offset].T, preferred_element_type=jnp.float32)  32.7 us
    unnamed x18, local copies, waits for them, and re-layouts  20.7 us
    unnamed x2, waiting for transfers between devices  19.5 us
    scatter-add x19, local copies, waits for them, and re-layouts, local(): accum = accum.at[time_lag:time_lag + FRAMES, row_shift:row_shift + out_h,...  17 us
    concatenate x3, other arithmetic, local(): jnp.concatenate([upsampled[:1], upsampled[:1], upsampled], axis=0)  10.5 us
    ppermute x2, waiting for transfers between devices, extended(): lax.ppermute(head, axis, [((i + 1) % count, i) for i in range(ends)])  7.69 us
    scatter x1, local copies, waits for them, and re-layouts, local(): returning = jnp.zeros((members, capacity, my_channels), jnp.bfloat16).at[...  7.56 us
    all_to_all x1, starting transfers between devices, local(): lax.all_to_all(outgoing, 'tile', split_axis=0, concat_axis=0, tiled=True)  7.25 us
  transfers between devices with their start and end apart: 11, of which 4 were waited for; matrix products, arithmetic and copies ran while one was open for 29% of the time, Pallas kernels for 0%

commit v1 on v0

v1 whole, which is shorter than its diff:
```python
import functools

import jax
import jax.numpy as jnp
from jax import lax
from jax.experimental import pallas as pl
from jax.experimental.pallas import tpu as pltpu
from jax.sharding import PartitionSpec as P

CHANNELS = 512
GROUP = 16
FRAMES = 2
TILE_H = 4
TILE_W = 8
CELLS = FRAMES * TILE_H * TILE_W
ROWS = FRAMES * TILE_H
EPS = 1e-06
F32 = jnp.float32
BF16 = jnp.bfloat16
VMEM = pl.BlockSpec(memory_space=pltpu.VMEM)
HIGHEST = lax.Precision.HIGHEST


def call(kernel, outs, args, scratch=(), flops=0):
    moved = sum(a.size * a.dtype.itemsize for a in args)
    moved += sum(o.size * o.dtype.itemsize for o in outs)
    return pl.pallas_call(
        kernel,
        out_shape=outs,
        in_specs=[VMEM] * len(args),
        out_specs=[VMEM] * len(outs),
        scratch_shapes=list(scratch),
        compiler_params=pltpu.CompilerParams(vmem_limit_bytes=48 * 2**20),
        cost_estimate=pl.CostEstimate(flops=flops, bytes_accessed=moved, transcendentals=0),
    )(*args)


def across_tiles():
    return min(lax.axis_size("tile"), 16)


def along_row(block, step):
    count, across = lax.axis_size("tile"), across_tiles()
    route = [(i, i + step) for i in range(count) if 0 <= i % across + step < across]
    return lax.ppermute(block, "tile", route)


def along_column(block, step):
    count, across = lax.axis_size("tile"), across_tiles()
    route = [(i, i + step * across) for i in range(count) if 0 <= i + step * across < count]
    return lax.ppermute(block, "tile", route)


def row_index(shape):
    return lax.broadcasted_iota(jnp.int32, shape, 0)


def from_row_above(x):
    keep = row_index(x.shape) % TILE_H != 0
    return jnp.where(keep, pltpu.roll(x, 1, 0), 0.0)


def from_row_below(x):
    keep = row_index(x.shape) % TILE_H != TILE_H - 1
    return jnp.where(keep, pltpu.roll(x, x.shape[0] - 1, 0), 0.0)


def dgrad_kernel(multi, *refs):
    if multi:
        e_ref, l_ref, r_ref, a_ref, b_ref, w_ref, out_ref, grid, sides = refs
    else:
        e_ref, l_ref, r_ref, w_ref, out_ref, grid, sides = refs
    wide = 2 * TILE_W
    grid[...] = e_ref[...].astype(F32)
    sides[: 2 * ROWS] = l_ref[...].astype(F32)
    sides[2 * ROWS :] = r_ref[...].astype(F32)

    def column(p, x):
        if x < 0:
            return sides[pl.ds(p, ROWS, stride=2), :]
        if x >= wide:
            return sides[pl.ds(2 * ROWS + p, ROWS, stride=2), :]
        return grid[pl.ds(p * wide + x, ROWS, stride=2 * wide), :]

    columns = [[column(p, x) for x in range(-1, wide + 1)] for p in range(2)]

    def fold(parts, e):
        pairs = [parts[2 * s + 2 - e] + parts[2 * s + 3 - e] for s in range(TILE_W)]
        return jnp.concatenate(pairs, axis=0)

    total = jnp.zeros((CELLS, CHANNELS), F32)
    latest = []
    for e in range(3):
        even, odd = fold(columns[0], e), fold(columns[1], e)
        below, above = from_row_below(even), from_row_above(odd)
        if multi:
            low = [b_ref[x].astype(F32) for x in range(wide + 2)]
            high = [a_ref[x].astype(F32) for x in range(wide + 2)]
            below, above = below + fold(low, e), above + fold(high, e)
        for b, folded in enumerate((odd + below, even + odd, above + even)):
            tap = 3 * b + e
            first = row_index(folded.shape) % ROWS < TILE_H
            both = folded + pltpu.roll(folded, CELLS - TILE_H, 0)
            both = jnp.where(first, both, 0.0).astype(BF16)
            latest.append((folded.astype(BF16), tap + 18))
            total = total + contract(both, tap, both, tap + 9, w_ref)
            if len(latest) == 2:
                (x, i), (y, j) = latest
                total = total + contract(x, i, y, j, w_ref)
                latest = []
    for x, i in latest:
        total = total + lax.dot_general(
            x, w_ref[i], (((1,), (1,)), ((), ())), preferred_element_type=F32
        )
    out_ref[...] = total


def contract(x, i, y, j, w_ref):
    left = jnp.concatenate([x, y], axis=1)
    right = jnp.concatenate([w_ref[i], w_ref[j]], axis=1)
    return lax.dot_general(left, right, (((1,), (1,)), ((), ())), preferred_element_type=F32)


def group_mean(sums):
    lanes = sums.shape[1]
    left = lax.broadcasted_iota(jnp.int32, (lanes, lanes), 0) // GROUP
    right = lax.broadcasted_iota(jnp.int32, (lanes, lanes), 1) // GROUP
    same = (left == right).astype(F32)
    whole = jnp.dot(sums, same, preferred_element_type=F32, precision=HIGHEST)
    return whole * (1.0 / (CELLS * GROUP))


def column_sums(x):
    return jnp.sum(x, axis=0, keepdims=True)


def norm_kernel(members, across, swapped, neighbours, peers, *refs):
    pieces = refs[:-12]
    source_ref, gain_ref, shift_ref, partial_ref = refs[-12:-8]
    mine_ref, hat_ref, slope_ref, scale_ref = refs[-8:-4]
    sends, own_ref = refs[-4:-1], refs[-1]
    tile = lax.axis_index("tile")
    chan = lax.axis_index("chan")
    tokens = jnp.concatenate([p[...] for p in pieces], axis=0) if len(pieces) > 1 else pieces[0][...]
    total = tokens.shape[0]
    own = total // members
    lanes = tokens.shape[1]
    source = source_ref[...]
    lane = lax.broadcasted_iota(jnp.int32, source.shape, 1)
    gain, shift = gain_ref[...], shift_ref[...]
    place = lax.broadcasted_iota(jnp.int32, (CELLS, total), 1)
    columns, there = [], []
    for dr, dc in neighbours:
        col, row = tile % across + dc, tile // across + dr
        there.append((col >= 0) & (col < across) & (row >= 0) & (row < members // across))
        wanted = jnp.sum(
            jnp.where(lane == tile + dr * across + dc, source, 0), axis=1, keepdims=True
        )
        if swapped:
            wanted = wanted ^ (tile * own)
        columns.append((place == wanted).astype(BF16))
    chosen = jnp.concatenate(columns, axis=0)
    features = jnp.dot(chosen, tokens, preferred_element_type=F32)
    features = [features[i * CELLS : (i + 1) * CELLS] for i in range(len(neighbours))]
    means = group_mean(stacked([column_sums(f) for f in features]))
    centred = [f - means[i : i + 1] for i, f in enumerate(features)]
    spreads = group_mean(stacked([column_sums(c * c) for c in centred]))
    scales = lax.rsqrt(spreads + EPS)
    blocks = {}
    for i, (dr, dc) in enumerate(neighbours):
        c = centred[i]
        if dc == -1:
            c = c[-ROWS:]
        elif dc == 1:
            c = c[:ROWS]
        hat = c * scales[i : i + 1]
        value = hat * gain + shift
        gate = 1.0 / (1.0 + jnp.exp(-value))
        active = value * gate
        if (dr, dc) == (0, 0):
            hat_ref[...] = hat
            slope_ref[...] = gate * (1.0 + value * (1.0 - gate)) * gain
            scale_ref[...] = scales[i : i + 1]
        else:
            active = jnp.where(there[i], active, 0.0)
        blocks[dr, dc] = active
    parts = [blocks[0, dc] for dc in (-1, 0, 1)]
    if len(neighbours) == 9:
        rows = CELLS + 2 * ROWS
        line = row_index((rows, lanes)) % TILE_H
        for dr, take, keep in ((-1, rows - TILE_H + 1, 0), (1, TILE_H - 1, TILE_H - 1)):
            block = jnp.concatenate([blocks[dr, dc] for dc in (-1, 0, 1)], axis=0)
            parts.append(jnp.where(line == keep, pltpu.roll(block, take, 0), 0.0))
    packed = jnp.concatenate(parts, axis=0).astype(BF16)
    own_ref[...] = packed
    size = packed.shape[0]
    for k, send in enumerate(sends):
        send[:size] = packed
        begin = pl.multiple_of((chan ^ (k + 1)) * lanes, 128)
        send[size:] = partial_ref[:, pl.ds(begin, lanes)].astype(BF16)
    mine_ref[...] = partial_ref[:, pl.ds(pl.multiple_of(chan * lanes, 128), lanes)]


def stacked(rows):
    lanes = rows[0].shape[1]
    pad = -len(rows) % 8
    if pad:
        rows = rows + [jnp.zeros((pad, lanes), F32)]
    return jnp.concatenate(rows, axis=0)


def back_kernel(own, capacity, size, *refs):
    mine_ref, hat_ref, slope_ref, scale_ref, source_ref = refs[:5]
    received, out_ref = refs[5:-1], refs[-1]
    tile = lax.axis_index("tile")
    grad = mine_ref[...]
    for r in received:
        grad = grad + r[size:].astype(F32)
    grad = grad * slope_ref[...]
    hat = hat_ref[...]
    means = group_mean(stacked([column_sums(grad), column_sums(grad * hat)]))
    result = scale_ref[...] * (grad - means[0:1] - hat * means[1:2])
    source = source_ref[pl.ds(tile, 1), :]
    slot = source // own * capacity + source % capacity
    place = row_index((out_ref.shape[0], CELLS))
    chosen = (place == slot).astype(BF16)
    packed = jnp.dot(chosen, result.astype(BF16), preferred_element_type=F32)
    out_ref[...] = packed.astype(BF16)


def conv_kernel(multi, *refs):
    own_ref, r1_ref, r2_ref, r3_ref, w_ref, bias_ref, out_ref, grid = refs
    chan = lax.axis_index("chan")
    rows = CELLS + 2 * ROWS
    lanes = own_ref.shape[1]
    size = own_ref.shape[0]
    grid_in = []
    received = [own_ref[...], r1_ref[:size], r2_ref[:size], r3_ref[:size]]
    for c in range(4):
        piece = received[3]
        for k in range(3):
            piece = jnp.where(chan ^ k == c, received[k], piece)
        grid_in.append(piece)
    cells = jnp.concatenate(grid_in, axis=1).astype(F32)
    line = row_index(cells.shape) % ROWS < TILE_H
    early = jnp.where(line, cells, pltpu.roll(cells, TILE_H, 0)).astype(BF16)
    cells = cells.astype(BF16)

    def products(taps, begin):
        x = cells[begin : begin + rows]
        y = early[begin : begin + rows]
        made = {}
        for at in range(0, len(taps), 2):
            pair = taps[at : at + 2]
            acc = None
            for a, left in ((0, y), (9, y), (18, x)):
                right = jnp.concatenate([w_ref[a + t] for t in pair], axis=1)
                term = jnp.dot(left, right, preferred_element_type=F32)
                acc = term if acc is None else acc + term
            for n, t in enumerate(pair):
                made[t] = acc[:, n * lanes : (n + 1) * lanes]
        return made

    def spread(made, b, q):
        first, middle, last = (made[3 * b + e] for e in range(3))
        if q == 0:
            return first[:CELLS] + middle[ROWS:-ROWS] + last[ROWS:-ROWS]
        return first[ROWS:-ROWS] + middle[ROWS:-ROWS] + last[2 * ROWS :]

    made = products(list(range(9)), 0)
    if multi:
        made_above = products([0, 1, 2], rows)
        made_below = products([6, 7, 8], 2 * rows)
    wide = 2 * TILE_W
    for q in range(2):
        top, middle, bottom = (spread(made, b, q) for b in range(3))
        above, below = from_row_above(top), from_row_below(bottom)
        if multi:
            above = above + spread(made_above, 0, q)
            below = below + spread(made_below, 2, q)
        for p, value in enumerate((above + middle + bottom, top + middle + below)):
            value = value + bias_ref[...]
            for j in range(TILE_W):
                grid[pl.ds(p * wide + 2 * j + q, ROWS, stride=2 * wide), :] = value[
                    j * ROWS : (j + 1) * ROWS
                ]
    out_ref[...] = grid[...].astype(BF16)


def place_kernel(returned_ref, slots_ref, out_ref):
    place = row_index((out_ref.shape[0], slots_ref.shape[1]))
    chosen = (place == slots_ref[...]).astype(BF16)
    out_ref[...] = jnp.dot(chosen, returned_ref[...], preferred_element_type=F32).astype(BF16)


def gathered_tokens(tokens):
    members = lax.axis_size("tile")
    if members != 8:
        return [lax.all_gather(tokens, "tile", axis=0, tiled=True)], False

    def swap(block, k):
        return lax.ppermute(block, "tile", [(i, i ^ k) for i in range(members)])

    pair = jnp.concatenate([tokens, swap(tokens, 1)], axis=0)
    return [pair] + [swap(pair, k) for k in (2, 4, 6)], True


def local(tokens, cell_source, gain, shift, weight, bias, cotangent):
    members = lax.axis_size("tile")
    device = lax.axis_index("tile")
    peers = lax.axis_size("chan")
    own, lanes = tokens.shape
    across = across_tiles()
    multi = members > across
    capacity = max(2, own // (members // 2))
    high, wide = 2 * TILE_H, 2 * TILE_W
    shape = jax.ShapeDtypeStruct

    grads = cotangent.reshape(FRAMES, high, wide, lanes)
    from_left = along_row(grads[:, :, -1:], 1)
    from_right = along_row(grads[:, :, :1], -1)
    pieces, swapped = gathered_tokens(tokens)
    args = [
        grads.reshape(-1, lanes),
        from_left.reshape(-1, lanes),
        from_right.reshape(-1, lanes),
    ]
    if multi:
        widened = jnp.concatenate([from_left, grads, from_right], axis=2)
        for edge, step, line in ((widened[:, -1], 1, 0), (widened[:, 0], -1, TILE_H - 1)):
            rim = along_column(edge, step).transpose(1, 0, 2)
            spaced = jnp.zeros((wide + 2, FRAMES, TILE_H, lanes), BF16).at[:, :, line].set(rim)
            args.append(spaced.reshape(wide + 2, ROWS, lanes))
    (partial,) = call(
        functools.partial(dgrad_kernel, multi),
        [shape((CELLS, CHANNELS), F32)],
        args + [weight],
        [pltpu.VMEM((high * wide * FRAMES, lanes), F32), pltpu.VMEM((4 * ROWS, lanes), F32)],
        flops=2 * 27 * CELLS * lanes * CHANNELS,
    )

    by_cell = cell_source.reshape(members, FRAMES, TILE_H, TILE_W).transpose(0, 3, 1, 2)
    by_cell = by_cell.reshape(members, CELLS)
    neighbours = [(0, -1), (0, 0), (0, 1)]
    if multi:
        neighbours = [(r, c) for r in (-1, 0, 1) for c in (-1, 0, 1)]
    size = (CELLS + 2 * ROWS) * (3 if multi else 1)
    cell = shape((CELLS, lanes), F32)
    mine, hat, slope, scale, *sends, packed = call(
        functools.partial(norm_kernel, members, across, swapped, neighbours, peers),
        [cell, cell, cell, shape((1, lanes), F32)]
        + [shape((size + CELLS, lanes), BF16)] * 3
        + [shape((size, lanes), BF16)],
        pieces + [by_cell.T, gain.reshape(1, -1), shift.reshape(1, -1), partial],
        flops=2 * len(neighbours) * CELLS * members * own * lanes,
    )
    received = [
        lax.ppermute(block, "chan", [(i, i ^ (k + 1)) for i in range(peers)])
        for k, block in enumerate(sends)
    ]
    (returning,) = call(
        functools.partial(back_kernel, own, capacity, size),
        [shape((members * capacity, lanes), BF16)],
        [mine, hat, slope, scale, by_cell] + received,
    )
    returned = lax.all_to_all(returning, "tile", split_axis=0, concat_axis=0, tiled=True)
    (decoded,) = call(
        functools.partial(conv_kernel, multi),
        [shape((FRAMES * high * wide, lanes), BF16)],
        [packed] + received + [weight, bias.reshape(1, -1)],
        [pltpu.VMEM((FRAMES * high * wide, lanes), F32)],
        flops=2 * 27 * (CELLS + 2 * ROWS) * lanes * CHANNELS,
    )
    mine_here = cell_source // own == device
    first = jnp.max(jnp.where(mine_here, cell_source % own, -capacity), axis=1) // capacity
    slots = first[:, None] * capacity + jnp.arange(capacity, dtype=jnp.int32)[None, :]
    (token_grad,) = call(
        place_kernel, [shape((own, lanes), BF16)], [returned, slots.reshape(1, -1)]
    )
    return decoded.reshape(1, FRAMES, high, wide, lanes), token_grad


def solution(mesh):
    in_specs = (
        P("tile", "chan"),
        P(),
        P("chan"),
        P("chan"),
        P(None, None, "chan"),
        P("chan"),
        P("tile", None, None, None, "chan"),
    )
    out_specs = (P("tile", None, None, None, "chan"), P("tile", "chan"))
    return jax.shard_map(local, mesh=mesh, in_specs=in_specs, out_specs=out_specs, check_vma=False)
```

time: 190 us -> 52.5 us (0.28)
  local copies, waits for them, and re-layouts: 58.9 us -> 14.7 us
  matrix products: 39.1 us -> 0 us
  waiting for transfers between devices: 27.3 us -> 5.52 us
  other arithmetic: 17.4 us -> 1.4 us
  between operations: 15.3 us -> 0.79 us
  Pallas kernels: 0 us -> 8.28 us
  blocking collectives: 5.26 us -> 0 us
  starting transfers between devices: 25.1 us -> 20.9 us
    dot_general x54 -> x0, matrix products: 39.1 us -> none  [the longest x27 32.7 us: local(): term = jnp.dot(grads, weight[offset].T, preferred_element_type=jnp.float32)]
    unnamed x2 -> x0, waiting for transfers between devices: 19.5 us -> none
    scatter-add x19 -> x0, local copies, waits for them, and re-layouts: 17 us -> none  [local(): accum = accum.at[time_lag:time_lag + FRAMES, row_shift:row_shift + out_h,...]
    concatenate x6 -> x0, other arithmetic: 10.6 us -> none  [the longest x3 10.5 us: local(): jnp.concatenate([upsampled[:1], upsampled[:1], upsampled], axis=0)]
    unnamed x18 -> x36, local copies, waits for them, and re-layouts: 20.7 us -> 11.7 us
    pallas_call x0 -> x5, Pallas kernels: none -> 8.28 us  [call(): pl.pallas_call(kernel, out_shape=outs, in_specs=[VMEM] * len(args), out_s...]
    scatter x1 -> x0, local copies, waits for them, and re-layouts: 7.56 us -> none  [local(): returning = jnp.zeros((members, capacity, my_channels), jnp.bfloat16).at[...]
    all_to_all x1 -> x0, starting transfers between devices: 7.25 us -> none  [local(): lax.all_to_all(outgoing, 'tile', split_axis=0, concat_axis=0, tiled=True)]
  transfers between devices with their start and end apart: 11 -> 10, of which waited for: 4 -> 3; matrix products, arithmetic and copies ran while one was open for 29% -> 13% of each run, Pallas kernels for 0% -> 7%
where the time goes in v1:
time: 52.5 us; the launch traced here: 51.5 us
  starting transfers between devices  20.9 us (40%)
  local copies, waits for them, and re-layouts  14.7 us (28%)
  Pallas kernels  8.28 us (16%)
  waiting for transfers between devices  5.52 us (11%)
  other arithmetic  1.4 us (3%)
  between operations  0.79 us (2%)
    unnamed x36, local copies, waits for them, and re-layouts  11.7 us
    ppermute x4, starting transfers between devices, swap(): return lax.ppermute(block, 'tile', [(i, i ^ k) for i in range(members)])  10.7 us
    pallas_call x5, Pallas kernels, call(): pl.pallas_call(kernel, out_shape=outs, in_specs=[VMEM] * len(args), out_s...  8.28 us
    all_to_all x1, starting transfers between devices, local(): lax.all_to_all(returning, 'tile', split_axis=0, concat_axis=0, tiled=True)  5.1 us
    ppermute x2, starting transfers between devices, along_row(): return lax.ppermute(block, 'tile', route)  3.21 us
    all_to_all x1, waiting for transfers between devices, local(): lax.all_to_all(returning, 'tile', split_axis=0, concat_axis=0, tiled=True)  2.98 us
    ppermute x3, waiting for transfers between devices, local(): lax.ppermute(block, 'chan', [(i, i ^ k + 1) for i in range(peers)])  2.53 us
    ppermute x3, starting transfers between devices, local(): lax.ppermute(block, 'chan', [(i, i ^ k + 1) for i in range(peers)])  1.86 us
  transfers between devices with their start and end apart: 10, of which 3 were waited for; matrix products, arithmetic and copies ran while one was open for 13% of the time, Pallas kernels for 7%

profile of v1, /device:TPU:0, one launch (start us, length us, event | category | flops | bytes accessed | tf_op | source)
XLA Modules:
  0.0 51.5 jit_solution(4200708548896326332)
XLA Ops:
  0.6 3.0 %collective-permute-start = (bf16[64,128]{1,0:T(8,128)(2,1)}, bf16[64,128]{1,0:T(8,128)(2,1)S(1)}, u32[]{:S(2)}, u32[]{:S(2)}) collective-permute-start(bf16[64,128]{1,0:T(8,128)(2,1)} %param.7), channel_id=1, source_target_pairs={{0,4},{4,0},{8,12},{12,8},{16,20},{20,16},{24,28},{28,24},{1,5},{5... | collective-permute-start | bytes 49160 | tf_op jit(solution)/shard_map/ppermute | solution.py:302
  3.7 0.9 %copy.15 = bf16[1,2,8,16,128]{4,2,1,3,0:T(8,128)(2,1)S(1)} copy(bf16[1,2,8,16,128]{4,3,2,1,0:T(8,128)(2,1)} %param.13) | data formatting | bytes 131072 | tf_op args[6]
  4.5 1.9 %collective-permute-start.4 = (bf16[2,8,1,128]{3,1,0,2:T(8,128)(2,1)S(1)}, bf16[2,8,1,128]{3,1,0,2:T(8,128)(2,1)S(1)}, u32[]{:S(2)}, u32[]{:S(2)}) collective-permute-start(bf16[2,8,1,128]{3,1,0,2:T(8,128)(2,1)S(1)} %get-tuple-element.19), channel_id=1, source_target_pairs={{0,4},{4,8},{8,12},{12,16},{16,20},{20,24},{24,28},{1,5},{5,9},{9,... | collective-permute-start | bytes 12296 | tf_op jit(solution)/shard_map/ppermute | solution.py:45
  6.5 1.3 %collective-permute-start.5 = (bf16[2,8,1,128]{3,1,0,2:T(8,128)(2,1)S(1)}, bf16[2,8,1,128]{3,1,0,2:T(8,128)(2,1)S(1)}, u32[]{:S(2)}, u32[]{:S(2)}) collective-permute-start(bf16[2,8,1,128]{3,1,0,2:T(8,128)(2,1)S(1)} %get-tuple-element.18), channel_id=1, source_target_pairs={{4,0},{8,4},{12,8},{16,12},{20,16},{24,20},{28,24},{5,1},{9,5},{13... | collective-permute-start | bytes 12296 | tf_op jit(solution)/shard_map/ppermute | solution.py:45
  7.8 1.3 %constant_dynamic-update-slice_fusion.1 = bf16[128,128]{1,0:T(8,128)(2,1)} fusion(bf16[64,128]{1,0:T(8,128)(2,1)} %param.7), kind=kLoop, calls=%fused_computation.2 | loop fusion | bytes 32768
  9.1 0.0 collective-permute-done
  9.1 0.6 %constant_dynamic-update-slice_fusion.refs_0_ = bf16[128,128]{1,0:T(8,128)(2,1)} fusion(bf16[128,128]{1,0:T(8,128)(2,1)} %constant_dynamic-update-slice_fusion.1, bf16[64,128]{1,0:T(8,128)(2,1)S(1)} %collective-permute-done), kind=kLoop, calls=%fused_computation.1 | loop fusion | bytes 32768 | tf_op jit(solution)/shard_map/concatenate | solution.py:304
  9.7 5.1 %collective-permute-start.1 = (bf16[128,128]{1,0:T(8,128)(2,1)}, bf16[128,128]{1,0:T(8,128)(2,1)}, u32[]{:S(2)}, u32[]{:S(2)}) collective-permute-start(bf16[128,128]{1,0:T(8,128)(2,1)} %constant_dynamic-update-slice_fusion.refs_0_), channel_id=1, source_target_pairs={{0,8},{4,12},{8,0},{12,4},{16,24},{20,28},{24,16},{28,20},{1,9},{5... | collective-permute-start | bytes 98312 | tf_op jit(solution)/shard_map/ppermute | solution.py:302
  14.8 2.6 %collective-permute-start.2 = (bf16[128,128]{1,0:T(8,128)(2,1)}, bf16[128,128]{1,0:T(8,128)(2,1)}, u32[]{:S(2)}, u32[]{:S(2)}) collective-permute-start(bf16[128,128]{1,0:T(8,128)(2,1)} %constant_dynamic-update-slice_fusion.refs_0_), channel_id=1, source_target_pairs={{0,16},{4,20},{8,24},{12,28},{16,0},{20,4},{24,8},{28,12},{1,17},{... | collective-permute-start | bytes 98312 | tf_op jit(solution)/shard_map/ppermute | solution.py:302
  17.4 0.0 collective-permute-start.3
  17.4 1.3 %fusion.2 = s32[8]{0:T(128)} fusion(s32[8,64]{1,0:T(8,128)} %param.8, s32[]{:T(128)S(6)} %axis_index.15), kind=kLoop, calls=%fused_computation.10 | loop fusion | flops 11256 | bytes 2084 | tf_op jit(solution)/shard_map/reduce_max | solution.py:375
  18.7 0.8 %reshape.75 = s32[8,2,4,8]{3,2,1,0:T(4,128)S(1)} reshape(s32[8,64]{1,0:T(8,128)} %param.8) | data formatting | bytes 4096 | tf_op jit(solution)/shard_map/reshape | solution.py:342
  19.5 0.7 %copy.11 = s32[8,2,4,8]{0,2,1,3:T(4,128)} copy(s32[8,2,4,8]{3,2,1,0:T(4,128)S(1)} %reshape.75) | data formatting | bytes 4096 | tf_op jit(solution)/shard_map/reshape | solution.py:342
  20.2 0.0 collective-permute-done.4
  20.2 0.0 collective-permute-done.5
  20.2 0.0 copy-start
  20.2 2.0 %copy-done = bf16[27,512,128]{2,1,0:T(8,128)(2,1)S(1)} copy-done((bf16[27,512,128]{2,1,0:T(8,128)(2,1)S(1)}, bf16[27,512,128]{2,1,0:T(8,128)(2,1)}, u32[]{:S(2)}) %copy-start) | copy-done | bytes 3538968
  22.2 0.8 %copy-done.3 = bf16[1,2,8,16,128]{4,3,2,1,0:T(8,128)(2,1)S(1)} copy-done((bf16[1,2,8,16,128]{4,3,2,1,0:T(8,128)(2,1)S(1)}, bf16[1,2,8,16,128]{4,3,2,1,0:T(8,128)(2,1)}, u32[]{:S(2)}) %copy-start.3) | copy-done | bytes 65560
  23.0 1.2 %shard_map.86.refs_7_ = f32[64,512]{1,0:T(8,128)S(1)} custom-call(bf16[256,128]{1,0:T(8,128)(2,1)S(1)} %bitcast.19, bf16[16,128]{1,0:T(8,128)(2,1)S(1)} %bitcast.21, bf16[16,128]{1,0:T(8,128)(2,1)S(1)} %bitcast.22, bf16[27,512,128]{2,1,0:T(8,128)(2,1)S(1)} %copy-done), custom_call_target="tpu_custom_call" | custom-call | flops 226492416 | bytes 3743744 | tf_op jit(solution)/shard_map/pallas_call | solution.py:27
  24.2 0.0 collective-permute-done.1.refs_1_
  24.2 0.0 collective-permute-done.2.refs_2_
  24.2 0.0 collective-permute-done.3.refs_3_
  24.2 0.0 copy-done.13
  24.3 2.2 %shard_map.87 = (f32[64,128]{1,0:T(8,128)S(1)}, f32[64,128]{1,0:T(8,128)S(1)}, f32[64,128]{1,0:T(8,128)S(1)}, f32[1,128]{1,0:T(1,128)S(1)}, bf16[144,128]{1,0:T(...) custom-call(bf16[128,128]{1,0:T(8,128)(2,1)} %constant_dynamic-update-slice_fusion.refs, ...), custom_call_target="tpu_custom_call" | custom-call | flops 25165824 | bytes 495104 | tf_op jit(solution)/shard_map/pallas_call | solution.py:27
  26.5 0.6 %copy-done.5 = f32[64,128]{1,0:T(8,128)} copy-done((f32[64,128]{1,0:T(8,128)}, f32[64,128]{1,0:T(8,128)S(1)}, u32[]{:S(2)}) %copy-start.5) | copy-done | bytes 32792
  27.1 0.6 %copy-done.7 = f32[64,128]{1,0:T(8,128)} copy-done((f32[64,128]{1,0:T(8,128)}, f32[64,128]{1,0:T(8,128)S(1)}, u32[]{:S(2)}) %copy-start.7) | copy-done | bytes 32792
  27.7 0.6 %copy-done.9 = f32[64,128]{1,0:T(8,128)} copy-done((f32[64,128]{1,0:T(8,128)}, f32[64,128]{1,0:T(8,128)S(1)}, u32[]{:S(2)}) %copy-start.9) | copy-done | bytes 32792
  28.3 0.6 %copy-done.11 = bf16[80,128]{1,0:T(8,128)(2,1)} copy-done((bf16[80,128]{1,0:T(8,128)(2,1)}, bf16[80,128]{1,0:T(8,128)(2,1)S(1)}, u32[]{:S(2)}) %copy-start.11) | copy-done | bytes 20504
  28.9 0.0 collective-permute-start.6
  28.9 1.5 %collective-permute-start.7 = (bf16[144,128]{1,0:T(8,128)(2,1)}, bf16[144,128]{1,0:T(8,128)(2,1)}, u32[]{:S(2)}, u32[]{:S(2)}) collective-permute-start(bf16[144,128]{1,0:T(8,128)(2,1)} %get-tuple-element.12), channel_id=1, source_target_pairs={{0,2},{1,3},{2,0},{3,1},{4,6},{5,7},{6,4},{7,5},{8,10},{9,11},{10,... | collective-permute-start | bytes 110600 | tf_op jit(solution)/shard_map/ppermute | solution.py:358
  30.4 0.3 collective-permute-start.8
  30.8 0.8 %copy.13.refs_4_ = s32[8,64]{1,0:T(8,128)S(1)} copy(s32[8,64]{0,1:T(8,128)} %bitcast.17) | data formatting | bytes 4096 | tf_op jit(solution)/shard_map/reshape | solution.py:343
  31.6 0.0 collective-permute-done.6.refs_1_.refs_5_
  31.6 1.6 %collective-permute-done.7.refs_2_.refs_6_ = bf16[144,128]{1,0:T(8,128)(2,1)} collective-permute-done((bf16[144,128]{1,0:T(8,128)(2,1)}, bf16[144,128]{1,0:T(8,128)(2,1)}, u32[]{:S(2)}, u32[]{:S(2)}) %collective-permute-start.7) | collective-permute-done | bytes 36896 | tf_op jit(solution)/shard_map/ppermute | solution.py:358
  33.2 0.9 %collective-permute-done.8.refs_3_.refs_7_ = bf16[144,128]{1,0:T(8,128)(2,1)} collective-permute-done((bf16[144,128]{1,0:T(8,128)(2,1)}, bf16[144,128]{1,0:T(8,128)(2,1)}, u32[]{:S(2)}, u32[]{:S(2)}) %collective-permute-start.8) | collective-permute-done | bytes 36896 | tf_op jit(solution)/shard_map/ppermute | solution.py:358
  34.1 0.8 %copy-done.6 = f32[64,128]{1,0:T(8,128)S(1)} copy-done((f32[64,128]{1,0:T(8,128)S(1)}, f32[64,128]{1,0:T(8,128)}, u32[]{:S(2)}) %copy-start.6) | copy-done | bytes 32792
  34.9 0.8 %copy-done.8 = f32[64,128]{1,0:T(8,128)S(1)} copy-done((f32[64,128]{1,0:T(8,128)S(1)}, f32[64,128]{1,0:T(8,128)}, u32[]{:S(2)}) %copy-start.8) | copy-done | bytes 32792
  35.6 0.8 %copy-done.10 = f32[64,128]{1,0:T(8,128)S(1)} copy-done((f32[64,128]{1,0:T(8,128)S(1)}, f32[64,128]{1,0:T(8,128)}, u32[]{:S(2)}) %copy-start.10) | copy-done | bytes 32792
  36.4 1.1 %shard_map.89 = bf16[128,128]{1,0:T(8,128)(2,1)S(1)} custom-call(f32[64,128]{1,0:T(8,128)S(1)} %copy-done.6, f32[64,128]{1,0:T(8,128)S(1)} %copy-done.8, f32[64,128]{1,0:T(8,128)S(1)} %copy-done.10, f32[1,128]{1,0:T(1,128)S(1)} %get-tuple-element.17.refs_3_, s32[8,64]{1,0:T(8,128)S(1)} %copy.13.refs_4_, ...), custom_call_target="tpu_custom_call" | custom-call | bytes 244224 | tf_op jit(solution)/shard_map/pallas_call | solution.py:27
  37.6 0.6 %copy-done.4 = bf16[128,128]{1,0:T(8,128)(2,1)} copy-done((bf16[128,128]{1,0:T(8,128)(2,1)}, bf16[128,128]{1,0:T(8,128)(2,1)S(1)}, u32[]{:S(2)}) %copy-start.4) | copy-done | bytes 32792
  38.2 5.1 %all-to-all-start = ((bf16[8,16,128]{2,1,0:T(8,128)(2,1)}), bf16[8,16,128]{2,1,0:T(8,128)(2,1)}, u32[]{:S(2)}, u32[]{:S(2)}) async-start(bf16[8,16,128]{2,1,0:T(8,128)(2,1)} %bitcast.20), calls=%async_computation | async-start | bytes 65536 | tf_op jit(solution)/shard_map/all_to_all | solution.py:366
  43.3 0.1 iota_add_fusion
  43.3 0.1 add.39.slots_ref
  43.4 0.7 %copy-done.12 = bf16[80,128]{1,0:T(8,128)(2,1)S(1)} copy-done((bf16[80,128]{1,0:T(8,128)(2,1)S(1)}, bf16[80,128]{1,0:T(8,128)(2,1)}, u32[]{:S(2)}) %copy-start.12) | copy-done | bytes 20504
  44.1 0.7 %copy-done.15 = f32[128]{0:T(128)S(1)} copy-done((f32[128]{0:T(128)S(1)}, f32[128]{0:T(128)}, u32[]{:S(2)}) %copy-start.15) | copy-done | bytes 536
  44.8 2.3 %shard_map.88 = bf16[256,128]{1,0:T(8,128)(2,1)} custom-call(bf16[80,128]{1,0:T(8,128)(2,1)S(1)} %copy-done.12, bf16[144,128]{1,0:T(8,128)(2,1)} %collective-permute-done.6.refs_1_.refs_5_, bf16[144,128]{1,0:T(8,128)(2,1)} %collective-permute-done.7.refs_2_.refs_6_, bf16[144,128]{1,0:T(8,128)(2,1)} %collective-permute-done.8.refs_3_.refs_7_, ...), custom_call_target="tpu_custom_call" | custom-call | flops 283115520 | bytes 3736064 | tf_op jit(solution)/shard_map/pallas_call | solution.py:27
  47.1 3.0 %all-to-all-done = bf16[8,16,128]{2,1,0:T(8,128)(2,1)} async-done(((bf16[8,16,128]{2,1,0:T(8,128)(2,1)}), bf16[8,16,128]{2,1,0:T(8,128)(2,1)}, u32[]{:S(2)}, u32[]{:S(2)}) %all-to-all-start) | async-done | bytes 32800 | tf_op jit(solution)/shard_map/all_to_all | solution.py:366
  50.1 1.5 %shard_map.90 = bf16[64,128]{1,0:T(8,128)(2,1)} custom-call(bf16[128,128]{1,0:T(8,128)(2,1)} %bitcast.13.returned_ref, s32[1,128]{1,0:T(1,128)S(1)} %add.39.slots_ref), custom_call_target="tpu_custom_call" | custom-call | bytes 49664 | tf_op jit(solution)/shard_map/pallas_call | solution.py:27
  (22 shorter events, 0.0 us)
Async XLA Ops:
  0.6 23.6 %copy-start.13 = (f32[128]{0:T(128)S(1)}, f32[128]{0:T(128)}, u32[]{:S(2)}) copy-start(f32[128]{0:T(128)} %param.9) | copy-start | bytes 1540
  0.6 23.6 %copy-start.14 = (f32[128]{0:T(128)S(1)}, f32[128]{0:T(128)}, u32[]{:S(2)}) copy-start(f32[128]{0:T(128)} %param.10) | copy-start | bytes 1540
  0.6 8.4 %collective-permute-start = (bf16[64,128]{1,0:T(8,128)(2,1)}, bf16[64,128]{1,0:T(8,128)(2,1)S(1)}, u32[]{:S(2)}, u32[]{:S(2)}) collective-permute-start(bf16[64,128]{1,0:T(8,128)(2,1)} %param.7), channel_id=1, source_target_pairs={{0,4},{4,0},{8,12},{12,8},{16,20},{20,16},{24,28},{28,24},{1,5},{5... | collective-permute-start | bytes 49160 | tf_op jit(solution)/shard_map/ppermute | solution.py:302
  4.5 15.6 %collective-permute-start.4 = (bf16[2,8,1,128]{3,1,0,2:T(8,128)(2,1)S(1)}, bf16[2,8,1,128]{3,1,0,2:T(8,128)(2,1)S(1)}, u32[]{:S(2)}, u32[]{:S(2)}) collective-permute-start(bf16[2,8,1,128]{3,1,0,2:T(8,128)(2,1)S(1)} %get-tuple-element.19), channel_id=1, source_target_pairs={{0,4},{4,8},{8,12},{12,16},{16,20},{20,24},{24,28},{1,5},{5,9},{9,... | collective-permute-start | bytes 12296 | tf_op jit(solution)/shard_map/ppermute | solution.py:45
  6.5 13.7 %collective-permute-start.5 = (bf16[2,8,1,128]{3,1,0,2:T(8,128)(2,1)S(1)}, bf16[2,8,1,128]{3,1,0,2:T(8,128)(2,1)S(1)}, u32[]{:S(2)}, u32[]{:S(2)}) collective-permute-start(bf16[2,8,1,128]{3,1,0,2:T(8,128)(2,1)S(1)} %get-tuple-element.18), channel_id=1, source_target_pairs={{4,0},{8,4},{12,8},{16,12},{20,16},{24,20},{28,24},{5,1},{9,5},{13... | collective-permute-start | bytes 12296 | tf_op jit(solution)/shard_map/ppermute | solution.py:45
  9.7 14.5 %collective-permute-start.1 = (bf16[128,128]{1,0:T(8,128)(2,1)}, bf16[128,128]{1,0:T(8,128)(2,1)}, u32[]{:S(2)}, u32[]{:S(2)}) collective-permute-start(bf16[128,128]{1,0:T(8,128)(2,1)} %constant_dynamic-update-slice_fusion.refs_0_), channel_id=1, source_target_pairs={{0,8},{4,12},{8,0},{12,4},{16,24},{20,28},{24,16},{28,20},{1,9},{5... | collective-permute-start | bytes 98312 | tf_op jit(solution)/shard_map/ppermute | solution.py:302
  14.8 9.4 %collective-permute-start.2 = (bf16[128,128]{1,0:T(8,128)(2,1)}, bf16[128,128]{1,0:T(8,128)(2,1)}, u32[]{:S(2)}, u32[]{:S(2)}) collective-permute-start(bf16[128,128]{1,0:T(8,128)(2,1)} %constant_dynamic-update-slice_fusion.refs_0_), channel_id=1, source_target_pairs={{0,16},{4,20},{8,24},{12,28},{16,0},{20,4},{24,8},{28,12},{1,17},{... | collective-permute-start | bytes 98312 | tf_op jit(solution)/shard_map/ppermute | solution.py:302
  17.4 6.9 %collective-permute-start.3 = (bf16[128,128]{1,0:T(8,128)(2,1)}, bf16[128,128]{1,0:T(8,128)(2,1)}, u32[]{:S(2)}, u32[]{:S(2)}) collective-permute-start(bf16[128,128]{1,0:T(8,128)(2,1)} %constant_dynamic-update-slice_fusion.refs_0_), channel_id=1, source_target_pairs={{0,24},{4,28},{8,16},{12,20},{16,8},{20,12},{24,0},{28,4},{1,25},{... | collective-permute-start | bytes 98312 | tf_op jit(solution)/shard_map/ppermute | solution.py:302
  20.2 10.6 %copy-start.16 = (s32[8]{0:T(128)S(1)}, s32[8]{0:T(128)}, u32[]{:S(2)}) copy-start(s32[8]{0:T(128)} %fusion.2) | copy-start | bytes 100
  20.2 2.0 %copy-start = (bf16[27,512,128]{2,1,0:T(8,128)(2,1)S(1)}, bf16[27,512,128]{2,1,0:T(8,128)(2,1)}, u32[]{:S(2)}) copy-start(bf16[27,512,128]{2,1,0:T(8,128)(2,1)} %refs_4_.1) | copy-start | bytes 10616836
  22.2 0.8 %copy-start.3 = (bf16[1,2,8,16,128]{4,3,2,1,0:T(8,128)(2,1)S(1)}, bf16[1,2,8,16,128]{4,3,2,1,0:T(8,128)(2,1)}, u32[]{:S(2)}) copy-start(bf16[1,2,8,16,128]{4,3,2,1,0:T(8,128)(2,1)} %param.13) | copy-start | bytes 196612
  23.0 1.2 %copy-start.2 = (s32[8,2,4,8]{0,2,1,3:T(4,128)S(1)}, s32[8,2,4,8]{0,2,1,3:T(4,128)}, u32[]{:S(2)}) copy-start(s32[8,2,4,8]{0,2,1,3:T(4,128)} %copy.11) | copy-start | bytes 6148
  23.0 20.4 %copy-start.1 = (bf16[27,512,128]{2,1,0:T(8,128)(2,1)S(1)}, bf16[27,512,128]{2,1,0:T(8,128)(2,1)}, u32[]{:S(2)}) copy-start(bf16[27,512,128]{2,1,0:T(8,128)(2,1)} %refs_4_.1) | copy-start | bytes 10616836
  26.5 0.6 %copy-start.5 = (f32[64,128]{1,0:T(8,128)}, f32[64,128]{1,0:T(8,128)S(1)}, u32[]{:S(2)}) copy-start(f32[64,128]{1,0:T(8,128)S(1)} %get-tuple-element.14.refs_0_) | copy-start | bytes 98308
  27.1 0.6 %copy-start.7 = (f32[64,128]{1,0:T(8,128)}, f32[64,128]{1,0:T(8,128)S(1)}, u32[]{:S(2)}) copy-start(f32[64,128]{1,0:T(8,128)S(1)} %get-tuple-element.15.refs_1_) | copy-start | bytes 98308
  27.7 0.6 %copy-start.9 = (f32[64,128]{1,0:T(8,128)}, f32[64,128]{1,0:T(8,128)S(1)}, u32[]{:S(2)}) copy-start(f32[64,128]{1,0:T(8,128)S(1)} %get-tuple-element.16.refs_2_) | copy-start | bytes 98308
  28.3 0.6 %copy-start.11 = (bf16[80,128]{1,0:T(8,128)(2,1)}, bf16[80,128]{1,0:T(8,128)(2,1)S(1)}, u32[]{:S(2)}) copy-start(bf16[80,128]{1,0:T(8,128)(2,1)S(1)} %get-tuple-element.10.refs_0_) | copy-start | bytes 61444
  28.9 2.7 %collective-permute-start.6 = (bf16[144,128]{1,0:T(8,128)(2,1)}, bf16[144,128]{1,0:T(8,128)(2,1)}, u32[]{:S(2)}, u32[]{:S(2)}) collective-permute-start(bf16[144,128]{1,0:T(8,128)(2,1)} %get-tuple-element.11), channel_id=1, source_target_pairs={{0,1},{1,0},{2,3},{3,2},{4,5},{5,4},{6,7},{7,6},{8,9},{9,8},{10,11... | collective-permute-start | bytes 110600 | tf_op jit(solution)/shard_map/ppermute | solution.py:358
  28.9 4.3 %collective-permute-start.7 = (bf16[144,128]{1,0:T(8,128)(2,1)}, bf16[144,128]{1,0:T(8,128)(2,1)}, u32[]{:S(2)}, u32[]{:S(2)}) collective-permute-start(bf16[144,128]{1,0:T(8,128)(2,1)} %get-tuple-element.12), channel_id=1, source_target_pairs={{0,2},{1,3},{2,0},{3,1},{4,6},{5,7},{6,4},{7,5},{8,10},{9,11},{10,... | collective-permute-start | bytes 110600 | tf_op jit(solution)/shard_map/ppermute | solution.py:358
  30.4 3.7 %collective-permute-start.8 = (bf16[144,128]{1,0:T(8,128)(2,1)}, bf16[144,128]{1,0:T(8,128)(2,1)}, u32[]{:S(2)}, u32[]{:S(2)}) collective-permute-start(bf16[144,128]{1,0:T(8,128)(2,1)} %get-tuple-element.13), channel_id=1, source_target_pairs={{0,3},{1,2},{2,1},{3,0},{4,7},{5,6},{6,5},{7,4},{8,11},{9,10},{10,... | collective-permute-start | bytes 110600 | tf_op jit(solution)/shard_map/ppermute | solution.py:358
  34.1 0.8 %copy-start.6 = (f32[64,128]{1,0:T(8,128)S(1)}, f32[64,128]{1,0:T(8,128)}, u32[]{:S(2)}) copy-start(f32[64,128]{1,0:T(8,128)} %copy-done.5) | copy-start | bytes 98308
  34.9 0.8 %copy-start.8 = (f32[64,128]{1,0:T(8,128)S(1)}, f32[64,128]{1,0:T(8,128)}, u32[]{:S(2)}) copy-start(f32[64,128]{1,0:T(8,128)} %copy-done.7) | copy-start | bytes 98308
  35.6 0.8 %copy-start.10 = (f32[64,128]{1,0:T(8,128)S(1)}, f32[64,128]{1,0:T(8,128)}, u32[]{:S(2)}) copy-start(f32[64,128]{1,0:T(8,128)} %copy-done.9) | copy-start | bytes 98308
  37.6 0.6 %copy-start.4 = (bf16[128,128]{1,0:T(8,128)(2,1)}, bf16[128,128]{1,0:T(8,128)(2,1)S(1)}, u32[]{:S(2)}) copy-start(bf16[128,128]{1,0:T(8,128)(2,1)S(1)} %shard_map.89) | copy-start | bytes 98308
  38.2 11.9 %all-to-all-start = ((bf16[8,16,128]{2,1,0:T(8,128)(2,1)}), bf16[8,16,128]{2,1,0:T(8,128)(2,1)}, u32[]{:S(2)}, u32[]{:S(2)}) async-start(bf16[8,16,128]{2,1,0:T(8,128)(2,1)} %bitcast.20), calls=%async_computation | async-start | bytes 65536 | tf_op jit(solution)/shard_map/all_to_all | solution.py:366
  43.4 0.7 %copy-start.12 = (bf16[80,128]{1,0:T(8,128)(2,1)S(1)}, bf16[80,128]{1,0:T(8,128)(2,1)}, u32[]{:S(2)}) copy-start(bf16[80,128]{1,0:T(8,128)(2,1)} %copy-done.11) | copy-start | bytes 61444
  44.1 0.7 %copy-start.15 = (f32[128]{0:T(128)S(1)}, f32[128]{0:T(128)}, u32[]{:S(2)}) copy-start(f32[128]{0:T(128)} %param.12) | copy-start | bytes 1540

commit v2 on v1

--- a/solution.py
+++ b/solution.py
@@ -15,22 +15,24 @@
 CELLS = FRAMES * TILE_H * TILE_W
 ROWS = FRAMES * TILE_H
 EPS = 1e-06
+VMEM_LIMIT = 12 * 2**20
 F32 = jnp.float32
 BF16 = jnp.bfloat16
 VMEM = pl.BlockSpec(memory_space=pltpu.VMEM)
+ANY = pl.BlockSpec(memory_space=pl.ANY)
 HIGHEST = lax.Precision.HIGHEST
 
 
-def call(kernel, outs, args, scratch=(), flops=0):
+def call(kernel, outs, args, scratch=(), flops=0, loose=()):
     moved = sum(a.size * a.dtype.itemsize for a in args)
     moved += sum(o.size * o.dtype.itemsize for o in outs)
     return pl.pallas_call(
         kernel,
         out_shape=outs,
-        in_specs=[VMEM] * len(args),
+        in_specs=[ANY if i in loose else VMEM for i in range(len(args))],
         out_specs=[VMEM] * len(outs),
         scratch_shapes=list(scratch),
-        compiler_params=pltpu.CompilerParams(vmem_limit_bytes=48 * 2**20),
+        compiler_params=pltpu.CompilerParams(vmem_limit_bytes=VMEM_LIMIT),
         cost_estimate=pl.CostEstimate(flops=flops, bytes_accessed=moved, transcendentals=0),
     )(*args)
 
@@ -65,15 +67,12 @@
     return jnp.where(keep, pltpu.roll(x, x.shape[0] - 1, 0), 0.0)
 
 
-def dgrad_kernel(multi, *refs):
-    if multi:
-        e_ref, l_ref, r_ref, a_ref, b_ref, w_ref, out_ref, grid, sides = refs
-    else:
-        e_ref, l_ref, r_ref, w_ref, out_ref, grid, sides = refs
+def dgrad(lines, left, right, rims, w_ref, grid, sides):
+    multi = len(rims) > 0
     wide = 2 * TILE_W
-    grid[...] = e_ref[...].astype(F32)
-    sides[: 2 * ROWS] = l_ref[...].astype(F32)
-    sides[2 * ROWS :] = r_ref[...].astype(F32)
+    grid[...] = lines.astype(F32)
+    sides[: 2 * ROWS] = left.astype(F32)
+    sides[2 * ROWS :] = right.astype(F32)
 
     def column(p, x):
         if x < 0:
@@ -94,8 +93,8 @@
         even, odd = fold(columns[0], e), fold(columns[1], e)
         below, above = from_row_below(even), from_row_above(odd)
         if multi:
-            low = [b_ref[x].astype(F32) for x in range(wide + 2)]
-            high = [a_ref[x].astype(F32) for x in range(wide + 2)]
+            high = [rims[0][x].astype(F32) for x in range(wide + 2)]
+            low = [rims[1][x].astype(F32) for x in range(wide + 2)]
             below, above = below + fold(low, e), above + fold(high, e)
         for b, folded in enumerate((odd + below, even + odd, above + even)):
             tap = 3 * b + e
@@ -112,7 +111,7 @@
         total = total + lax.dot_general(
             x, w_ref[i], (((1,), (1,)), ((), ())), preferred_element_type=F32
         )
-    out_ref[...] = total
+    return total
 
 
 def contract(x, i, y, j, w_ref):
@@ -134,32 +133,38 @@
     return jnp.sum(x, axis=0, keepdims=True)
 
 
-def norm_kernel(members, across, swapped, neighbours, peers, *refs):
-    pieces = refs[:-12]
-    source_ref, gain_ref, shift_ref, partial_ref = refs[-12:-8]
-    mine_ref, hat_ref, slope_ref, scale_ref = refs[-8:-4]
-    sends, own_ref = refs[-4:-1], refs[-1]
+def main_kernel(members, across, woven, neighbours, count, *refs):
+    pieces, refs = refs[:count], refs[count:]
+    lines_ref, w_ref, take_ref, gain_ref, shift_ref = refs[:5]
+    others, refs = refs[5:-11], refs[-11:]
+    mine_ref, hat_ref, slope_ref, scale_ref = refs[:4]
+    sends, own_ref = refs[4:7], refs[7]
+    partial_ref, grid, sides = refs[8:11]
     tile = lax.axis_index("tile")
     chan = lax.axis_index("chan")
-    tokens = jnp.concatenate([p[...] for p in pieces], axis=0) if len(pieces) > 1 else pieces[0][...]
-    total = tokens.shape[0]
-    own = total // members
+    if woven:
+        near = others[0][: 2 * ROWS]
+        far = jnp.zeros_like(near)
+        column = tile % 2
+        wanted = tile // 2 + 2 * column - 1
+        for k in range(1, count):
+            far = jnp.where(wanted == tile // 2 ^ k, pieces[k][-2 * ROWS :], far)
+        left = jnp.where(column == 1, near, far)
+        right = jnp.where(column == 1, far, near)
+        tokens = jnp.concatenate([p[: -2 * ROWS] for p in pieces], axis=0)
+        rims = ()
+    else:
+        left, right = others[0][...], others[1][...]
+        tokens = pieces[0][...]
+        rims = others[2:]
+    partial_ref[...] = dgrad(lines_ref[...], left, right, rims, w_ref, grid, sides)
     lanes = tokens.shape[1]
-    source = source_ref[...]
-    lane = lax.broadcasted_iota(jnp.int32, source.shape, 1)
     gain, shift = gain_ref[...], shift_ref[...]
-    place = lax.broadcasted_iota(jnp.int32, (CELLS, total), 1)
-    columns, there = [], []
+    there = []
     for dr, dc in neighbours:
         col, row = tile % across + dc, tile // across + dr
         there.append((col >= 0) & (col < across) & (row >= 0) & (row < members // across))
-        wanted = jnp.sum(
-            jnp.where(lane == tile + dr * across + dc, source, 0), axis=1, keepdims=True
-        )
-        if swapped:
-            wanted = wanted ^ (tile * own)
-        columns.append((place == wanted).astype(BF16))
-    chosen = jnp.concatenate(columns, axis=0)
+    chosen = take_ref[...]
     features = jnp.dot(chosen, tokens, preferred_element_type=F32)
     features = [features[i * CELLS : (i + 1) * CELLS] for i in range(len(neighbours))]
     means = group_mean(stacked([column_sums(f) for f in features]))
@@ -209,33 +214,74 @@
     return jnp.concatenate(rows, axis=0)
 
 
-def back_kernel(own, capacity, size, *refs):
-    mine_ref, hat_ref, slope_ref, scale_ref, source_ref = refs[:5]
-    received, out_ref = refs[5:-1], refs[-1]
-    tile = lax.axis_index("tile")
+def fetch(copies):
+    for copy in copies:
+        copy.start()
+    for copy in copies:
+        copy.wait()
+
+
+def back_kernel(size, *refs):
+    mine_ref, hat_ref, slope_ref, scale_ref, pack_ref = refs[:5]
+    received, outs = refs[5:8], refs[8:-2]
+    space, sems = refs[-2:]
+    copies = [
+        pltpu.make_async_copy(r.at[pl.ds(size, CELLS)], space.at[k], sems.at[k])
+        for k, r in enumerate(received)
+    ]
+    fetch(copies)
     grad = mine_ref[...]
-    for r in received:
-        grad = grad + r[size:].astype(F32)
+    for k in range(3):
+        grad = grad + space[k].astype(F32)
     grad = grad * slope_ref[...]
     hat = hat_ref[...]
     means = group_mean(stacked([column_sums(grad), column_sums(grad * hat)]))
     result = scale_ref[...] * (grad - means[0:1] - hat * means[1:2])
-    source = source_ref[pl.ds(tile, 1), :]
-    slot = source // own * capacity + source % capacity
-    place = row_index((out_ref.shape[0], CELLS))
-    chosen = (place == slot).astype(BF16)
-    packed = jnp.dot(chosen, result.astype(BF16), preferred_element_type=F32)
-    out_ref[...] = packed.astype(BF16)
+    packed = jnp.dot(pack_ref[...], result.astype(BF16), preferred_element_type=F32).astype(BF16)
+    begin = 0
+    for out in outs:
+        out[...] = packed[begin : begin + out.shape[0]]
+        begin += out.shape[0]
+
+
+def route_kernel(kept_ref, came_ref, *outs):
+    some = outs[0].shape[0] // 2
+    for k, out in enumerate(outs):
+        out[:some] = kept_ref[k * some : (k + 1) * some]
+        out[some:] = came_ref[k * some : (k + 1) * some]
+
+
+def join_kernel(tokens_ref, peer_ref, edges_ref, out_ref):
+    own = tokens_ref.shape[0]
+    out_ref[:own] = tokens_ref[...]
+    out_ref[own : 2 * own] = peer_ref[...]
+    out_ref[2 * own :] = edges_ref[2 * ROWS :]
+
+
+def edge_kernel(lines_ref, out_ref, grid):
+    wide = 2 * TILE_W
+    grid[...] = lines_ref[...].astype(F32)
+    first = grid[pl.ds(0, 2 * ROWS, stride=wide), :]
+    last = grid[pl.ds(wide - 1, 2 * ROWS, stride=wide), :]
+    odd = lax.axis_index("tile") % 2 == 1
+    out_ref[: 2 * ROWS] = jnp.where(odd, first, last).astype(BF16)
+    out_ref[2 * ROWS :] = jnp.where(odd, last, first).astype(BF16)
 
 
 def conv_kernel(multi, *refs):
-    own_ref, r1_ref, r2_ref, r3_ref, w_ref, bias_ref, out_ref, grid = refs
+    own_ref, *received, hbm_ref, bias_ref, out_ref, grid, space, w_ref, sems = refs
     chan = lax.axis_index("chan")
     rows = CELLS + 2 * ROWS
     lanes = own_ref.shape[1]
     size = own_ref.shape[0]
+    copies = [
+        pltpu.make_async_copy(r.at[pl.ds(0, size)], space.at[k], sems.at[k])
+        for k, r in enumerate(received)
+    ]
+    copies.append(pltpu.make_async_copy(hbm_ref, w_ref, sems.at[3]))
+    fetch(copies)
     grid_in = []
-    received = [own_ref[...], r1_ref[:size], r2_ref[:size], r3_ref[:size]]
+    received = [own_ref[...], space[0], space[1], space[2]]
     for c in range(4):
         piece = received[3]
         for k in range(3):
@@ -287,96 +333,144 @@
     out_ref[...] = grid[...].astype(BF16)
 
 
-def place_kernel(returned_ref, slots_ref, out_ref):
-    place = row_index((out_ref.shape[0], slots_ref.shape[1]))
-    chosen = (place == slots_ref[...]).astype(BF16)
-    out_ref[...] = jnp.dot(chosen, returned_ref[...], preferred_element_type=F32).astype(BF16)
-
-
-def gathered_tokens(tokens):
-    members = lax.axis_size("tile")
-    if members != 8:
-        return [lax.all_gather(tokens, "tile", axis=0, tiled=True)], False
-
-    def swap(block, k):
-        return lax.ppermute(block, "tile", [(i, i ^ k) for i in range(members)])
-
-    pair = jnp.concatenate([tokens, swap(tokens, 1)], axis=0)
-    return [pair] + [swap(pair, k) for k in (2, 4, 6)], True
+def place_kernel(put_ref, *refs):
+    returned, out_ref = refs[:-1], refs[-1]
+    values = [r[...] for r in returned]
+    values = jnp.concatenate(values, axis=0) if len(values) > 1 else values[0]
+    placed = jnp.dot(put_ref[...], values, preferred_element_type=F32)
+    out_ref[...] = placed.astype(BF16)
+
+
+def cell_of(place):
+    return place % ROWS // TILE_H * (TILE_H * TILE_W) + place % TILE_H * TILE_W + place // ROWS
+
+
+def index_kernel(across, woven, neighbours, own, capacity, source_ref, take_ref, pack_ref, put_ref):
+    tile = lax.axis_index("tile")
+    source = source_ref[...]
+    members = source.shape[0]
+    square = (CELLS, CELLS)
+    left = lax.broadcasted_iota(jnp.int32, square, 0)
+    right = lax.broadcasted_iota(jnp.int32, square, 1)
+    place = lax.broadcasted_iota(jnp.int32, (CELLS, members * own), 1)
+    for i, (dr, dc) in enumerate(neighbours):
+        other = jnp.clip(tile + dr * across + dc, 0, members - 1)
+        line = source_ref[pl.ds(other, 1), :]
+        wanted = jnp.sum(jnp.where(cell_of(left) == right, line, 0), axis=1, keepdims=True)
+        if (dr, dc) == (0, 0):
+            owner = wanted // own
+            if woven:
+                owner = owner ^ tile
+                owner = owner // 2 + owner % 2 * (members // 2)
+            slot = owner * capacity + wanted % capacity
+            slot = jnp.sum(jnp.where(left == right, slot, 0), axis=0, keepdims=True)
+        if woven:
+            wanted = wanted ^ (tile * own)
+        take_ref[i * CELLS : (i + 1) * CELLS] = (place == wanted).astype(F32).astype(BF16)
+    pack_ref[...] = (row_index(pack_ref.shape) == slot).astype(F32).astype(BF16)
+    mine = source // own == tile
+    first = jnp.where(mine, source % own, -capacity)
+    first = jnp.max(first, axis=1, keepdims=True) // capacity * capacity
+    wide = (members, members * capacity)
+    spot = lax.broadcasted_iota(jnp.int32, wide, 1)
+    sender = spot // capacity
+    if woven:
+        sender = sender ^ tile
+    meant = jnp.where(sender == row_index(wide), first + spot % capacity, 0)
+    meant = jnp.sum(meant, axis=0, keepdims=True)
+    put_ref[...] = (row_index(put_ref.shape) == meant).astype(F32).astype(BF16)
+
+
+def swapped(block, axis, k):
+    return lax.ppermute(block, axis, [(i, i ^ k) for i in range(lax.axis_size(axis))])
 
 
 def local(tokens, cell_source, gain, shift, weight, bias, cotangent):
     members = lax.axis_size("tile")
-    device = lax.axis_index("tile")
-    peers = lax.axis_size("chan")
     own, lanes = tokens.shape
     across = across_tiles()
     multi = members > across
+    woven = members == 8
     capacity = max(2, own // (members // 2))
+    slots = members * capacity
     high, wide = 2 * TILE_H, 2 * TILE_W
+    area = FRAMES * high * wide
     shape = jax.ShapeDtypeStruct
 
-    grads = cotangent.reshape(FRAMES, high, wide, lanes)
-    from_left = along_row(grads[:, :, -1:], 1)
-    from_right = along_row(grads[:, :, :1], -1)
-    pieces, swapped = gathered_tokens(tokens)
-    args = [
-        grads.reshape(-1, lanes),
-        from_left.reshape(-1, lanes),
-        from_right.reshape(-1, lanes),
-    ]
+    def block(rows):
+        return shape((rows, lanes), BF16)
+
+    neighbours = [(0, -1), (0, 0), (0, 1)]
     if multi:
-        widened = jnp.concatenate([from_left, grads, from_right], axis=2)
+        neighbours = [(r, c) for r in (-1, 0, 1) for c in (-1, 0, 1)]
+    take, pack, put = call(
+        functools.partial(index_kernel, across, woven, neighbours, own, capacity),
+        [
+            shape((len(neighbours) * CELLS, members * own), BF16),
+            shape((slots, CELLS), BF16),
+            shape((own, slots), BF16),
+        ],
+        [cell_source],
+    )
+    lines = cotangent.reshape(area, lanes)
+    spread = pltpu.VMEM((area, lanes), F32)
+    if woven:
+        peer = swapped(tokens, "tile", 1)
+        (edges,) = call(edge_kernel, [block(4 * ROWS)], [lines], [spread])
+        edges = swapped(edges, "tile", 1)
+        (pair,) = call(join_kernel, [block(2 * own + 2 * ROWS)], [tokens, peer, edges])
+        pieces = [pair] + [swapped(pair, "tile", k) for k in (2, 4, 6)]
+        others = [edges]
+    else:
+        pieces = [lax.all_gather(tokens, "tile", axis=0, tiled=True)]
+        others = [along_row(lines[wide - 1 :: wide], 1), along_row(lines[::wide], -1)]
+    if multi:
+        side = (FRAMES, high, 1, lanes)
+        widened = [others[0].reshape(side), lines.reshape(FRAMES, high, wide, lanes)]
+        widened = jnp.concatenate(widened + [others[1].reshape(side)], axis=2)
         for edge, step, line in ((widened[:, -1], 1, 0), (widened[:, 0], -1, TILE_H - 1)):
             rim = along_column(edge, step).transpose(1, 0, 2)
             spaced = jnp.zeros((wide + 2, FRAMES, TILE_H, lanes), BF16).at[:, :, line].set(rim)
-            args.append(spaced.reshape(wide + 2, ROWS, lanes))
-    (partial,) = call(
-        functools.partial(dgrad_kernel, multi),
-        [shape((CELLS, CHANNELS), F32)],
-        args + [weight],
-        [pltpu.VMEM((high * wide * FRAMES, lanes), F32), pltpu.VMEM((4 * ROWS, lanes), F32)],
-        flops=2 * 27 * CELLS * lanes * CHANNELS,
-    )
-
-    by_cell = cell_source.reshape(members, FRAMES, TILE_H, TILE_W).transpose(0, 3, 1, 2)
-    by_cell = by_cell.reshape(members, CELLS)
-    neighbours = [(0, -1), (0, 0), (0, 1)]
-    if multi:
-        neighbours = [(r, c) for r in (-1, 0, 1) for c in (-1, 0, 1)]
+            others.append(spaced.reshape(wide + 2, ROWS, lanes))
+
     size = (CELLS + 2 * ROWS) * (3 if multi else 1)
     cell = shape((CELLS, lanes), F32)
     mine, hat, slope, scale, *sends, packed = call(
-        functools.partial(norm_kernel, members, across, swapped, neighbours, peers),
-        [cell, cell, cell, shape((1, lanes), F32)]
-        + [shape((size + CELLS, lanes), BF16)] * 3
-        + [shape((size, lanes), BF16)],
-        pieces + [by_cell.T, gain.reshape(1, -1), shift.reshape(1, -1), partial],
-        flops=2 * len(neighbours) * CELLS * members * own * lanes,
+        functools.partial(main_kernel, members, across, woven, neighbours, len(pieces)),
+        [cell, cell, cell, shape((1, lanes), F32)] + [block(size + CELLS)] * 3 + [block(size)],
+        pieces + [lines, weight, take, gain.reshape(1, -1), shift.reshape(1, -1)] + others,
+        [pltpu.VMEM((CELLS, CHANNELS), F32), spread, pltpu.VMEM((4 * ROWS, lanes), F32)],
+        flops=2 * 27 * CELLS * lanes * CHANNELS,
     )
-    received = [
-        lax.ppermute(block, "chan", [(i, i ^ (k + 1)) for i in range(peers)])
-        for k, block in enumerate(sends)
-    ]
-    (returning,) = call(
-        functools.partial(back_kernel, own, capacity, size),
-        [shape((members * capacity, lanes), BF16)],
-        [mine, hat, slope, scale, by_cell] + received,
+    received = [swapped(send, "chan", k + 1) for k, send in enumerate(sends)]
+    halves = [block(slots // 2)] * 2 if woven else [block(slots)]
+    returning = call(
+        functools.partial(back_kernel, size),
+        halves,
+        [mine, hat, slope, scale, pack] + received,
+        [pltpu.VMEM((3, CELLS, lanes), BF16), pltpu.SemaphoreType.DMA((3,))],
+        loose=(5, 6, 7),
     )
-    returned = lax.all_to_all(returning, "tile", split_axis=0, concat_axis=0, tiled=True)
+    if woven:
+        came = swapped(returning[1], "tile", 1)
+        routed = call(route_kernel, [block(2 * capacity)] * 4, [returning[0], came])
+        returned = [routed[0]] + [swapped(r, "tile", 2 * k + 2) for k, r in enumerate(routed[1:])]
+    else:
+        returned = [lax.all_to_all(returning[0], "tile", split_axis=0, concat_axis=0, tiled=True)]
     (decoded,) = call(
         functools.partial(conv_kernel, multi),
-        [shape((FRAMES * high * wide, lanes), BF16)],
+        [block(area)],
         [packed] + received + [weight, bias.reshape(1, -1)],
-        [pltpu.VMEM((FRAMES * high * wide, lanes), F32)],
+        [
+            spread,
+            pltpu.VMEM((3, size, lanes), BF16),
+            pltpu.VMEM(weight.shape, BF16),
+            pltpu.SemaphoreType.DMA((4,)),
+        ],
         flops=2 * 27 * (CELLS + 2 * ROWS) * lanes * CHANNELS,
+        loose=(1, 2, 3, 4),
     )
-    mine_here = cell_source // own == device
-    first = jnp.max(jnp.where(mine_here, cell_source % own, -capacity), axis=1) // capacity
-    slots = first[:, None] * capacity + jnp.arange(capacity, dtype=jnp.int32)[None, :]
-    (token_grad,) = call(
-        place_kernel, [shape((own, lanes), BF16)], [returned, slots.reshape(1, -1)]
-    )
+    (token_grad,) = call(place_kernel, [block(own)], [put] + returned)
     return decoded.reshape(1, FRAMES, high, wide, lanes), token_grad
 
 

time: 52.5 us -> 41.2 us (0.78); the launches traced: 51.5 us -> 40.9 us
  waiting for transfers between devices: 5.52 us -> 14.2 us
  local copies, waits for them, and re-layouts: 14.7 us -> 6.4 us
  starting transfers between devices: 20.9 us -> 14.4 us
  Pallas kernels: 8.28 us -> 5.15 us
  other arithmetic: 1.4 us -> 0 us
    ppermute x9 -> x12, waiting for transfers between devices: 2.54 us -> 14.2 us  [swapped(): lax.ppermute(block, axis, [(i, i ^ k) for i in range(lax.axis_size(axis))])]
    unnamed x36 -> x18, local copies, waits for them, and re-layouts: 11.7 us -> 6.4 us
    all_to_all x1 -> x0, starting transfers between devices: 5.1 us -> none  [local(): lax.all_to_all(returning, 'tile', split_axis=0, concat_axis=0, tiled=True)]
    pallas_call x5 -> x8, Pallas kernels: 8.28 us -> 5.15 us  [call(): pl.pallas_call(kernel, out_shape=outs, in_specs=[ANY if i in loose else V...]
    all_to_all x1 -> x0, waiting for transfers between devices: 2.98 us -> none  [local(): lax.all_to_all(returning, 'tile', split_axis=0, concat_axis=0, tiled=True)]
    reshape x3 -> x0, local copies, waits for them, and re-layouts: 2.28 us -> none  [the longest x2 1.46 us: local(): cell_source.reshape(members, FRAMES, TILE_H, TILE_W).transpose(0, 3, 1, 2)]
    ppermute x9 -> x12, starting transfers between devices: 15.8 us -> 14.4 us  [swapped(): lax.ppermute(block, axis, [(i, i ^ k) for i in range(lax.axis_size(axis))])]
    reduce_max x1 -> x0, other arithmetic: 1.32 us -> none  [local(): jnp.max(jnp.where(mine_here, cell_source % own, -capacity), axis=1)]
  transfers between devices with their start and end apart: 10 -> 12, of which waited for: 3 -> 7; matrix products, arithmetic and copies ran while one was open for 13% -> 0% of each run, Pallas kernels for 7% -> 5%
where the time goes in v2:
time: 41.2 us; the launch traced here: 40.9 us
  starting transfers between devices  14.4 us (35%)
  waiting for transfers between devices  14.2 us (34%)
  local copies, waits for them, and re-layouts  6.4 us (16%)
  Pallas kernels  5.15 us (12%)
  between operations  0.71 us (2%)
    ppermute x12, starting transfers between devices, swapped(): lax.ppermute(block, axis, [(i, i ^ k) for i in range(lax.axis_size(axis))])  14.4 us
    ppermute x12, waiting for transfers between devices, swapped(): lax.ppermute(block, axis, [(i, i ^ k) for i in range(lax.axis_size(axis))])  14.2 us
    unnamed x18, local copies, waits for them, and re-layouts  6.4 us
    pallas_call x8, Pallas kernels, call(): pl.pallas_call(kernel, out_shape=outs, in_specs=[ANY if i in loose else V...  5.15 us
  transfers between devices with their start and end apart: 12, of which 7 were waited for; matrix products, arithmetic and copies ran while one was open for 0% of the time, Pallas kernels for 5%

profile of v2, /device:TPU:0, one launch (start us, length us, event | category | flops | bytes accessed | tf_op | source)
XLA Modules:
  0.0 40.9 jit_solution(11510544897786834306)
XLA Ops:
  0.6 0.0 copy-start.8
  0.6 3.0 %collective-permute-start = (bf16[64,128]{1,0:T(8,128)(2,1)}, bf16[64,128]{1,0:T(8,128)(2,1)S(1)}, u32[]{:S(2)}, u32[]{:S(2)}) collective-permute-start(bf16[64,128]{1,0:T(8,128)(2,1)} %tokens_ref.1), channel_id=1, source_target_pairs={{0,4},{4,0},{8,12},{12,8},{16,20},{20,16},{24,28},{28,24},{1,5},{5... | collective-permute-start | bytes 49160 | tf_op jit(solution)/shard_map/ppermute | solution.py:385
  3.6 0.0 copy-start.2
  3.6 0.8 %copy-done.2 = bf16[1,2,8,16,128]{4,3,2,1,0:T(8,128)(2,1)S(1)} copy-done((bf16[1,2,8,16,128]{4,3,2,1,0:T(8,128)(2,1)S(1)}, bf16[1,2,8,16,128]{4,3,2,1,0:T(8,128)(2,1)}, u32[]{:S(2)}) %copy-start.2) | copy-done | bytes 65560
  4.5 0.1 collective-permute-start.1
  4.6 3.6 %collective-permute-done.1.edges_ref.refs_9_ = bf16[32,128]{1,0:T(8,128)(2,1)S(1)} collective-permute-done((bf16[32,128]{1,0:T(8,128)(2,1)S(1)}, bf16[32,128]{1,0:T(8,128)(2,1)S(1)}, u32[]{:S(2)}, u32[]{:S(2)}) %collective-permute-start.1) | collective-permute-done | bytes 8224 | tf_op jit(solution)/shard_map/ppermute | solution.py:385
  8.2 0.0 collective-permute-done.peer_ref
  8.2 0.0 copy-start.4
  8.2 0.7 %copy-done.4 = bf16[64,128]{1,0:T(8,128)(2,1)S(1)} copy-done((bf16[64,128]{1,0:T(8,128)(2,1)S(1)}, bf16[64,128]{1,0:T(8,128)(2,1)}, u32[]{:S(2)}) %copy-start.4) | copy-done | bytes 16408
  8.9 3.6 %collective-permute-start.4 = (bf16[144,128]{1,0:T(8,128)(2,1)S(1)}, bf16[144,128]{1,0:T(8,128)(2,1)S(1)}, u32[]{:S(2)}, u32[]{:S(2)}) collective-permute-start(bf16[144,128]{1,0:T(8,128)(2,1)S(1)} %shard_map.87.refs_0_), channel_id=1, source_target_pairs={{0,24},{4,28},{8,16},{12,20},{16,8},{20,12},{24,0},{28,4},{1,25},{... | collective-permute-start | bytes 110600 | tf_op jit(solution)/shard_map/ppermute | solution.py:385
  12.6 0.0 collective-permute-start.3
  12.6 0.8 %collective-permute-start.2 = (bf16[144,128]{1,0:T(8,128)(2,1)S(1)}, bf16[144,128]{1,0:T(8,128)(2,1)S(1)}, u32[]{:S(2)}, u32[]{:S(2)}) collective-permute-start(bf16[144,128]{1,0:T(8,128)(2,1)S(1)} %shard_map.87.refs_0_), channel_id=1, source_target_pairs={{0,8},{4,12},{8,0},{12,4},{16,24},{20,28},{24,16},{28,20},{1,9},{5... | collective-permute-start | bytes 110600 | tf_op jit(solution)/shard_map/ppermute | solution.py:385
  13.3 0.0 copy-start.5
  13.3 0.7 %copy-done.5 = s32[8,64]{1,0:T(8,128)S(1)} copy-done((s32[8,64]{1,0:T(8,128)S(1)}, s32[8,64]{1,0:T(8,128)}, u32[]{:S(2)}) %copy-start.5) | copy-done | bytes 2072
  14.0 0.2 shard_map.88
  14.3 0.5 %collective-permute-done.4.refs_3_ = bf16[144,128]{1,0:T(8,128)(2,1)S(1)} collective-permute-done((bf16[144,128]{1,0:T(8,128)(2,1)S(1)}, bf16[144,128]{1,0:T(8,128)(2,1)S(1)}, u32[]{:S(2)}, u32[]{:S(2)}) %collective-permute-start.4) | collective-permute-done | bytes 36896 | tf_op jit(solution)/shard_map/ppermute | solution.py:385
  14.8 2.6 %collective-permute-done.3.refs_2_ = bf16[144,128]{1,0:T(8,128)(2,1)S(1)} collective-permute-done((bf16[144,128]{1,0:T(8,128)(2,1)S(1)}, bf16[144,128]{1,0:T(8,128)(2,1)S(1)}, u32[]{:S(2)}, u32[]{:S(2)}) %collective-permute-start.3) | collective-permute-done | bytes 36896 | tf_op jit(solution)/shard_map/ppermute | solution.py:385
  17.4 0.0 collective-permute-done.2.refs_1_
  17.4 0.0 copy-start
  17.4 2.0 %copy-done = bf16[27,512,128]{2,1,0:T(8,128)(2,1)S(1)} copy-done((bf16[27,512,128]{2,1,0:T(8,128)(2,1)S(1)}, bf16[27,512,128]{2,1,0:T(8,128)(2,1)}, u32[]{:S(2)}) %copy-start) | copy-done | bytes 3538968
  19.4 0.0 copy-start.3
  19.4 0.8 %copy-done.3 = bf16[1,2,8,16,128]{4,3,2,1,0:T(8,128)(2,1)S(1)} copy-done((bf16[1,2,8,16,128]{4,3,2,1,0:T(8,128)(2,1)S(1)}, bf16[1,2,8,16,128]{4,3,2,1,0:T(8,128)(2,1)}, u32[]{:S(2)}) %copy-start.3) | copy-done | bytes 65560
  20.3 0.0 copy-start.6
  20.3 0.7 %copy-done.6 = f32[128]{0:T(128)S(1)} copy-done((f32[128]{0:T(128)S(1)}, f32[128]{0:T(128)}, u32[]{:S(2)}) %copy-start.6) | copy-done | bytes 536
  20.9 0.0 copy-start.7
  20.9 0.7 %copy-done.7 = f32[128]{0:T(128)S(1)} copy-done((f32[128]{0:T(128)S(1)}, f32[128]{0:T(128)}, u32[]{:S(2)}) %copy-start.7) | copy-done | bytes 536
  21.6 0.0 copy-start.1
  21.6 1.8 %shard_map.89 = (f32[64,128]{1,0:T(8,128)S(1)}, f32[64,128]{1,0:T(8,128)S(1)}, f32[64,128]{1,0:T(8,128)S(1)}, f32[1,128]{1,0:T(1,128)S(1)}, bf16[144,128]{1,0:T(...) custom-call(bf16[144,128]{1,0:T(8,128)(2,1)S(1)} %shard_map.87.refs_0_, ...), custom_call_target="tpu_custom_call" | custom-call | flops 226492416 | bytes 4187648 | tf_op jit(solution)/shard_map/pallas_call | solution.py:29
  23.3 0.1 collective-permute-start.5
  23.4 1.6 %collective-permute-start.6 = (bf16[144,128]{1,0:T(8,128)(2,1)S(1)}, bf16[144,128]{1,0:T(8,128)(2,1)S(1)}, u32[]{:S(2)}, u32[]{:S(2)}) collective-permute-start(bf16[144,128]{1,0:T(8,128)(2,1)S(1)} %get-tuple-element.22), channel_id=1, source_target_pairs={{0,2},{1,3},{2,0},{3,1},{4,6},{5,7},{6,4},{7,5},{8,10},{9,11},{10,... | collective-permute-start | bytes 110600 | tf_op jit(solution)/shard_map/ppermute | solution.py:385
  25.0 0.3 collective-permute-start.7
  25.3 0.0 collective-permute-done.5.refs_1_.refs_5_
  25.3 2.2 %collective-permute-done.6.refs_2_.refs_6_ = bf16[144,128]{1,0:T(8,128)(2,1)S(1)} collective-permute-done((bf16[144,128]{1,0:T(8,128)(2,1)S(1)}, bf16[144,128]{1,0:T(8,128)(2,1)S(1)}, u32[]{:S(2)}, u32[]{:S(2)}) %collective-permute-start.6) | collective-permute-done | bytes 36896 | tf_op jit(solution)/shard_map/ppermute | solution.py:385
  27.4 1.0 %collective-permute-done.7.refs_3_.refs_7_ = bf16[144,128]{1,0:T(8,128)(2,1)S(1)} collective-permute-done((bf16[144,128]{1,0:T(8,128)(2,1)S(1)}, bf16[144,128]{1,0:T(8,128)(2,1)S(1)}, u32[]{:S(2)}, u32[]{:S(2)}) %collective-permute-start.7) | collective-permute-done | bytes 36896 | tf_op jit(solution)/shard_map/ppermute | solution.py:385
  28.4 0.4 %shard_map.91 = (bf16[64,128]{1,0:T(8,128)(2,1)S(1)}, bf16[64,128]{1,0:T(8,128)(2,1)S(1)}) custom-call(f32[64,128]{1,0:T(8,128)S(1)} %get-tuple-element.25.refs_0_, f32[64,128]{1,0:T(8,128)S(1)} %get-tuple-element.26.refs_1_, f32[64,128]{1,0:T(8,128)S(1)} %get-tuple-element.27.refs_2_, f32[1,128]{1,0:T(1,128)S(1)} %get-tuple-element.28.refs_3_, ...), custom_call_target="tpu_custom_call" | custom-call | bytes 258560 | tf_op jit(solution)/shard_map/pallas_call | solution.py:29
  28.9 0.6 %collective-permute-start.8 = (bf16[64,128]{1,0:T(8,128)(2,1)S(1)}, bf16[64,128]{1,0:T(8,128)(2,1)S(1)}, u32[]{:S(2)}, u32[]{:S(2)}) collective-permute-start(bf16[64,128]{1,0:T(8,128)(2,1)S(1)} %get-tuple-element.31), channel_id=1, source_target_pairs={{0,4},{4,0},{8,12},{12,8},{16,20},{20,16},{24,28},{28,24},{1,5},{5... | collective-permute-start | bytes 49160 | tf_op jit(solution)/shard_map/ppermute | solution.py:385
  29.5 3.2 %collective-permute-done.8.came_ref = bf16[64,128]{1,0:T(8,128)(2,1)S(1)} collective-permute-done((bf16[64,128]{1,0:T(8,128)(2,1)S(1)}, bf16[64,128]{1,0:T(8,128)(2,1)S(1)}, u32[]{:S(2)}, u32[]{:S(2)}) %collective-permute-start.8) | collective-permute-done | bytes 16416 | tf_op jit(solution)/shard_map/ppermute | solution.py:385
  32.7 0.0 collective-permute-start.9
  32.7 2.0 %collective-permute-start.10 = (bf16[32,128]{1,0:T(8,128)(2,1)S(1)}, bf16[32,128]{1,0:T(8,128)(2,1)S(1)}, u32[]{:S(2)}, u32[]{:S(2)}) collective-permute-start(bf16[32,128]{1,0:T(8,128)(2,1)S(1)} %get-tuple-element.34), channel_id=1, source_target_pairs={{0,16},{4,20},{8,24},{12,28},{16,0},{20,4},{24,8},{28,12},{1,17},{... | collective-permute-start | bytes 24584 | tf_op jit(solution)/shard_map/ppermute | solution.py:385
  34.7 2.4 %collective-permute-start.11 = (bf16[32,128]{1,0:T(8,128)(2,1)S(1)}, bf16[32,128]{1,0:T(8,128)(2,1)S(1)}, u32[]{:S(2)}, u32[]{:S(2)}) collective-permute-start(bf16[32,128]{1,0:T(8,128)(2,1)S(1)} %get-tuple-element.35), channel_id=1, source_target_pairs={{0,24},{4,28},{8,16},{12,20},{16,8},{20,12},{24,0},{28,4},{1,25},{... | collective-permute-start | bytes 24584 | tf_op jit(solution)/shard_map/ppermute | solution.py:385
  37.0 0.0 copy-done.8
  37.1 0.0 copy-done.1
  37.1 2.0 %shard_map.90 = bf16[256,128]{1,0:T(8,128)(2,1)} custom-call(bf16[80,128]{1,0:T(8,128)(2,1)S(1)} %get-tuple-element.20.refs_0_, bf16[144,128]{1,0:T(8,128)(2,1)S(1)} %collective-permute-done.5.refs_1_.refs_5_, bf16[144,128]{1,0:T(8,128)(2,1)S(1)} %collective-permute-done.6.refs_2_.refs_6_, bf16[144,128]{1,0:T(8,128)(2,1)S(1)} %collective-permute-done.7.refs_3_.refs_7_, ...), custom_call_target="tpu_custom_call" | custom-call | flops 283115520 | bytes 3736064 | tf_op jit(solution)/shard_map/pallas_call | solution.py:29
  39.0 0.0 collective-permute-done.9.refs_1_
  39.1 0.0 collective-permute-done.10.refs_2_
  39.1 1.1 %collective-permute-done.11.refs_3_ = bf16[32,128]{1,0:T(8,128)(2,1)S(1)} collective-permute-done((bf16[32,128]{1,0:T(8,128)(2,1)S(1)}, bf16[32,128]{1,0:T(8,128)(2,1)S(1)}, u32[]{:S(2)}, u32[]{:S(2)}) %collective-permute-start.11) | collective-permute-done | bytes 8224 | tf_op jit(solution)/shard_map/ppermute | solution.py:385
  40.1 0.7 %shard_map.93 = bf16[64,128]{1,0:T(8,128)(2,1)} custom-call(bf16[64,128]{1,0:T(8,128)(2,1)S(1)} %get-tuple-element.24.put_ref, bf16[32,128]{1,0:T(8,128)(2,1)S(1)} %get-tuple-element.32.refs_0_, bf16[32,128]{1,0:T(8,128)(2,1)S(1)} %collective-permute-done.9.refs_1_, bf16[32,128]{1,0:T(8,128)(2,1)S(1)} %collective-permute-done.10.refs_2_, ...), custom_call_target="tpu_custom_call" | custom-call | bytes 65536 | tf_op jit(solution)/shard_map/pallas_call | solution.py:29
  (3 shorter events, 0.0 us)
Async XLA Ops:
  0.6 36.4 %copy-start.8 = (f32[128]{0:T(128)S(1)}, f32[128]{0:T(128)}, u32[]{:S(2)}) copy-start(f32[128]{0:T(128)} %param.12) | copy-start | bytes 1540
  0.6 7.6 %collective-permute-start = (bf16[64,128]{1,0:T(8,128)(2,1)}, bf16[64,128]{1,0:T(8,128)(2,1)S(1)}, u32[]{:S(2)}, u32[]{:S(2)}) collective-permute-start(bf16[64,128]{1,0:T(8,128)(2,1)} %tokens_ref.1), channel_id=1, source_target_pairs={{0,4},{4,0},{8,12},{12,8},{16,20},{20,16},{24,28},{28,24},{1,5},{5... | collective-permute-start | bytes 49160 | tf_op jit(solution)/shard_map/ppermute | solution.py:385
  3.6 0.8 %copy-start.2 = (bf16[1,2,8,16,128]{4,3,2,1,0:T(8,128)(2,1)S(1)}, bf16[1,2,8,16,128]{4,3,2,1,0:T(8,128)(2,1)}, u32[]{:S(2)}) copy-start(bf16[1,2,8,16,128]{4,3,2,1,0:T(8,128)(2,1)} %param.13) | copy-start | bytes 196612
  4.5 3.7 %collective-permute-start.1 = (bf16[32,128]{1,0:T(8,128)(2,1)S(1)}, bf16[32,128]{1,0:T(8,128)(2,1)S(1)}, u32[]{:S(2)}, u32[]{:S(2)}) collective-permute-start(bf16[32,128]{1,0:T(8,128)(2,1)S(1)} %shard_map.86), channel_id=1, source_target_pairs={{0,4},{4,0},{8,12},{12,8},{16,20},{20,16},{24,28},{28,24},{1,5},{5... | collective-permute-start | bytes 24584 | tf_op jit(solution)/shard_map/ppermute | solution.py:385
  8.2 0.7 %copy-start.4 = (bf16[64,128]{1,0:T(8,128)(2,1)S(1)}, bf16[64,128]{1,0:T(8,128)(2,1)}, u32[]{:S(2)}) copy-start(bf16[64,128]{1,0:T(8,128)(2,1)} %tokens_ref.1) | copy-start | bytes 49156
  8.9 5.9 %collective-permute-start.4 = (bf16[144,128]{1,0:T(8,128)(2,1)S(1)}, bf16[144,128]{1,0:T(8,128)(2,1)S(1)}, u32[]{:S(2)}, u32[]{:S(2)}) collective-permute-start(bf16[144,128]{1,0:T(8,128)(2,1)S(1)} %shard_map.87.refs_0_), channel_id=1, source_target_pairs={{0,24},{4,28},{8,16},{12,20},{16,8},{20,12},{24,0},{28,4},{1,25},{... | collective-permute-start | bytes 110600 | tf_op jit(solution)/shard_map/ppermute | solution.py:385
  12.6 4.9 %collective-permute-start.3 = (bf16[144,128]{1,0:T(8,128)(2,1)S(1)}, bf16[144,128]{1,0:T(8,128)(2,1)S(1)}, u32[]{:S(2)}, u32[]{:S(2)}) collective-permute-start(bf16[144,128]{1,0:T(8,128)(2,1)S(1)} %shard_map.87.refs_0_), channel_id=1, source_target_pairs={{0,16},{4,20},{8,24},{12,28},{16,0},{20,4},{24,8},{28,12},{1,17},{... | collective-permute-start | bytes 110600 | tf_op jit(solution)/shard_map/ppermute | solution.py:385
  12.6 4.9 %collective-permute-start.2 = (bf16[144,128]{1,0:T(8,128)(2,1)S(1)}, bf16[144,128]{1,0:T(8,128)(2,1)S(1)}, u32[]{:S(2)}, u32[]{:S(2)}) collective-permute-start(bf16[144,128]{1,0:T(8,128)(2,1)S(1)} %shard_map.87.refs_0_), channel_id=1, source_target_pairs={{0,8},{4,12},{8,0},{12,4},{16,24},{20,28},{24,16},{28,20},{1,9},{5... | collective-permute-start | bytes 110600 | tf_op jit(solution)/shard_map/ppermute | solution.py:385
  13.3 0.7 %copy-start.5 = (s32[8,64]{1,0:T(8,128)S(1)}, s32[8,64]{1,0:T(8,128)}, u32[]{:S(2)}) copy-start(s32[8,64]{1,0:T(8,128)} %source_ref.1) | copy-start | bytes 6148
  17.4 2.0 %copy-start = (bf16[27,512,128]{2,1,0:T(8,128)(2,1)S(1)}, bf16[27,512,128]{2,1,0:T(8,128)(2,1)}, u32[]{:S(2)}) copy-start(bf16[27,512,128]{2,1,0:T(8,128)(2,1)} %refs_4_.1) | copy-start | bytes 10616836
  19.4 0.8 %copy-start.3 = (bf16[1,2,8,16,128]{4,3,2,1,0:T(8,128)(2,1)S(1)}, bf16[1,2,8,16,128]{4,3,2,1,0:T(8,128)(2,1)}, u32[]{:S(2)}) copy-start(bf16[1,2,8,16,128]{4,3,2,1,0:T(8,128)(2,1)} %param.13) | copy-start | bytes 196612
  20.3 0.7 %copy-start.6 = (f32[128]{0:T(128)S(1)}, f32[128]{0:T(128)}, u32[]{:S(2)}) copy-start(f32[128]{0:T(128)} %param.9) | copy-start | bytes 1540
  20.9 0.7 %copy-start.7 = (f32[128]{0:T(128)S(1)}, f32[128]{0:T(128)}, u32[]{:S(2)}) copy-start(f32[128]{0:T(128)} %param.10) | copy-start | bytes 1540
  21.6 15.5 %copy-start.1 = (bf16[27,512,128]{2,1,0:T(8,128)(2,1)S(1)}, bf16[27,512,128]{2,1,0:T(8,128)(2,1)}, u32[]{:S(2)}) copy-start(bf16[27,512,128]{2,1,0:T(8,128)(2,1)} %refs_4_.1) | copy-start | bytes 10616836
  23.3 1.9 %collective-permute-start.5 = (bf16[144,128]{1,0:T(8,128)(2,1)S(1)}, bf16[144,128]{1,0:T(8,128)(2,1)S(1)}, u32[]{:S(2)}, u32[]{:S(2)}) collective-permute-start(bf16[144,128]{1,0:T(8,128)(2,1)S(1)} %get-tuple-element.21), channel_id=1, source_target_pairs={{0,1},{1,0},{2,3},{3,2},{4,5},{5,4},{6,7},{7,6},{8,9},{9,8},{10,11... | collective-permute-start | bytes 110600 | tf_op jit(solution)/shard_map/ppermute | solution.py:385
  23.4 4.0 %collective-permute-start.6 = (bf16[144,128]{1,0:T(8,128)(2,1)S(1)}, bf16[144,128]{1,0:T(8,128)(2,1)S(1)}, u32[]{:S(2)}, u32[]{:S(2)}) collective-permute-start(bf16[144,128]{1,0:T(8,128)(2,1)S(1)} %get-tuple-element.22), channel_id=1, source_target_pairs={{0,2},{1,3},{2,0},{3,1},{4,6},{5,7},{6,4},{7,5},{8,10},{9,11},{10,... | collective-permute-start | bytes 110600 | tf_op jit(solution)/shard_map/ppermute | solution.py:385
  25.0 3.4 %collective-permute-start.7 = (bf16[144,128]{1,0:T(8,128)(2,1)S(1)}, bf16[144,128]{1,0:T(8,128)(2,1)S(1)}, u32[]{:S(2)}, u32[]{:S(2)}) collective-permute-start(bf16[144,128]{1,0:T(8,128)(2,1)S(1)} %get-tuple-element.23), channel_id=1, source_target_pairs={{0,3},{1,2},{2,1},{3,0},{4,7},{5,6},{6,5},{7,4},{8,11},{9,10},{10,... | collective-permute-start | bytes 110600 | tf_op jit(solution)/shard_map/ppermute | solution.py:385
  28.9 3.8 %collective-permute-start.8 = (bf16[64,128]{1,0:T(8,128)(2,1)S(1)}, bf16[64,128]{1,0:T(8,128)(2,1)S(1)}, u32[]{:S(2)}, u32[]{:S(2)}) collective-permute-start(bf16[64,128]{1,0:T(8,128)(2,1)S(1)} %get-tuple-element.31), channel_id=1, source_target_pairs={{0,4},{4,0},{8,12},{12,8},{16,20},{20,16},{24,28},{28,24},{1,5},{5... | collective-permute-start | bytes 49160 | tf_op jit(solution)/shard_map/ppermute | solution.py:385
  32.7 6.4 %collective-permute-start.9 = (bf16[32,128]{1,0:T(8,128)(2,1)S(1)}, bf16[32,128]{1,0:T(8,128)(2,1)S(1)}, u32[]{:S(2)}, u32[]{:S(2)}) collective-permute-start(bf16[32,128]{1,0:T(8,128)(2,1)S(1)} %get-tuple-element.33), channel_id=1, source_target_pairs={{0,8},{4,12},{8,0},{12,4},{16,24},{20,28},{24,16},{28,20},{1,9},{5... | collective-permute-start | bytes 24584 | tf_op jit(solution)/shard_map/ppermute | solution.py:385
  32.7 6.4 %collective-permute-start.10 = (bf16[32,128]{1,0:T(8,128)(2,1)S(1)}, bf16[32,128]{1,0:T(8,128)(2,1)S(1)}, u32[]{:S(2)}, u32[]{:S(2)}) collective-permute-start(bf16[32,128]{1,0:T(8,128)(2,1)S(1)} %get-tuple-element.34), channel_id=1, source_target_pairs={{0,16},{4,20},{8,24},{12,28},{16,0},{20,4},{24,8},{28,12},{1,17},{... | collective-permute-start | bytes 24584 | tf_op jit(solution)/shard_map/ppermute | solution.py:385
  34.7 5.4 %collective-permute-start.11 = (bf16[32,128]{1,0:T(8,128)(2,1)S(1)}, bf16[32,128]{1,0:T(8,128)(2,1)S(1)}, u32[]{:S(2)}, u32[]{:S(2)}) collective-permute-start(bf16[32,128]{1,0:T(8,128)(2,1)S(1)} %get-tuple-element.35), channel_id=1, source_target_pairs={{0,24},{4,28},{8,16},{12,20},{16,8},{20,12},{24,0},{28,4},{1,25},{... | collective-permute-start | bytes 24584 | tf_op jit(solution)/shard_map/ppermute | solution.py:385

commit v3 on v2

--- a/solution.py
+++ b/solution.py
@@ -19,17 +19,21 @@
 F32 = jnp.float32
 BF16 = jnp.bfloat16
 VMEM = pl.BlockSpec(memory_space=pltpu.VMEM)
-ANY = pl.BlockSpec(memory_space=pl.ANY)
+FAR = pl.BlockSpec(memory_space=pltpu.HBM)
 HIGHEST = lax.Precision.HIGHEST
 
 
 def call(kernel, outs, args, scratch=(), flops=0, loose=()):
+    args = [
+        pltpu.with_memory_space_constraint(a, pltpu.HBM) if i in loose else a
+        for i, a in enumerate(args)
+    ]
     moved = sum(a.size * a.dtype.itemsize for a in args)
     moved += sum(o.size * o.dtype.itemsize for o in outs)
     return pl.pallas_call(
         kernel,
         out_shape=outs,
-        in_specs=[ANY if i in loose else VMEM for i in range(len(args))],
+        in_specs=[FAR if i in loose else VMEM for i in range(len(args))],
         out_specs=[VMEM] * len(outs),
         scratch_shapes=list(scratch),
         compiler_params=pltpu.CompilerParams(vmem_limit_bytes=VMEM_LIMIT),
@@ -67,10 +71,9 @@
     return jnp.where(keep, pltpu.roll(x, x.shape[0] - 1, 0), 0.0)
 
 
-def dgrad(lines, left, right, rims, w_ref, grid, sides):
+def dgrad(grid, left, right, rims, w_ref, sides):
     multi = len(rims) > 0
     wide = 2 * TILE_W
-    grid[...] = lines.astype(F32)
     sides[: 2 * ROWS] = left.astype(F32)
     sides[2 * ROWS :] = right.astype(F32)
 
@@ -136,14 +139,14 @@
 def main_kernel(members, across, woven, neighbours, count, *refs):
     pieces, refs = refs[:count], refs[count:]
     lines_ref, w_ref, take_ref, gain_ref, shift_ref = refs[:5]
-    others, refs = refs[5:-11], refs[-11:]
+    others, refs = refs[5:-10], refs[-10:]
     mine_ref, hat_ref, slope_ref, scale_ref = refs[:4]
     sends, own_ref = refs[4:7], refs[7]
-    partial_ref, grid, sides = refs[8:11]
+    partial_ref, sides = refs[8:10]
     tile = lax.axis_index("tile")
     chan = lax.axis_index("chan")
     if woven:
-        near = others[0][: 2 * ROWS]
+        near = others[0][-4 * ROWS : -2 * ROWS]
         far = jnp.zeros_like(near)
         column = tile % 2
         wanted = tile // 2 + 2 * column - 1
@@ -157,7 +160,7 @@
         left, right = others[0][...], others[1][...]
         tokens = pieces[0][...]
         rims = others[2:]
-    partial_ref[...] = dgrad(lines_ref[...], left, right, rims, w_ref, grid, sides)
+    partial_ref[...] = dgrad(lines_ref, left, right, rims, w_ref, sides)
     lanes = tokens.shape[1]
     gain, shift = gain_ref[...], shift_ref[...]
     there = []
@@ -223,16 +226,10 @@
 
 def back_kernel(size, *refs):
     mine_ref, hat_ref, slope_ref, scale_ref, pack_ref = refs[:5]
-    received, outs = refs[5:8], refs[8:-2]
-    space, sems = refs[-2:]
-    copies = [
-        pltpu.make_async_copy(r.at[pl.ds(size, CELLS)], space.at[k], sems.at[k])
-        for k, r in enumerate(received)
-    ]
-    fetch(copies)
+    received, outs = refs[5:8], refs[8:]
     grad = mine_ref[...]
-    for k in range(3):
-        grad = grad + space[k].astype(F32)
+    for r in received:
+        grad = grad + r[size:].astype(F32)
     grad = grad * slope_ref[...]
     hat = hat_ref[...]
     means = group_mean(stacked([column_sums(grad), column_sums(grad * hat)]))
@@ -251,37 +248,35 @@
         out[some:] = came_ref[k * some : (k + 1) * some]
 
 
-def join_kernel(tokens_ref, peer_ref, edges_ref, out_ref):
+def early_kernel(tokens_ref, lines_ref, out_ref, grid, space, sems):
     own = tokens_ref.shape[0]
-    out_ref[:own] = tokens_ref[...]
-    out_ref[own : 2 * own] = peer_ref[...]
-    out_ref[2 * own :] = edges_ref[2 * ROWS :]
-
-
-def edge_kernel(lines_ref, out_ref, grid):
+    first_copy = pltpu.make_async_copy(lines_ref, space, sems.at[0])
+    other_copy = pltpu.make_async_copy(tokens_ref, out_ref.at[pl.ds(0, own)], sems.at[1])
+    fetch([first_copy, other_copy])
     wide = 2 * TILE_W
-    grid[...] = lines_ref[...].astype(F32)
+    grid[...] = space[...].astype(F32)
     first = grid[pl.ds(0, 2 * ROWS, stride=wide), :]
     last = grid[pl.ds(wide - 1, 2 * ROWS, stride=wide), :]
     odd = lax.axis_index("tile") % 2 == 1
-    out_ref[: 2 * ROWS] = jnp.where(odd, first, last).astype(BF16)
-    out_ref[2 * ROWS :] = jnp.where(odd, last, first).astype(BF16)
+    out_ref[own : own + 2 * ROWS] = jnp.where(odd, first, last).astype(BF16)
+    out_ref[own + 2 * ROWS :] = jnp.where(odd, last, first).astype(BF16)
+
+
+def join_kernel(mine_ref, peer_ref, out_ref):
+    own = mine_ref.shape[0] - 4 * ROWS
+    out_ref[:own] = mine_ref[:own]
+    out_ref[own : 2 * own] = peer_ref[:own]
+    out_ref[2 * own :] = peer_ref[own + 2 * ROWS :]
 
 
 def conv_kernel(multi, *refs):
-    own_ref, *received, hbm_ref, bias_ref, out_ref, grid, space, w_ref, sems = refs
+    own_ref, *received, w_ref, bias_ref, out_ref, grid = refs
     chan = lax.axis_index("chan")
     rows = CELLS + 2 * ROWS
     lanes = own_ref.shape[1]
     size = own_ref.shape[0]
-    copies = [
-        pltpu.make_async_copy(r.at[pl.ds(0, size)], space.at[k], sems.at[k])
-        for k, r in enumerate(received)
-    ]
-    copies.append(pltpu.make_async_copy(hbm_ref, w_ref, sems.at[3]))
-    fetch(copies)
     grid_in = []
-    received = [own_ref[...], space[0], space[1], space[2]]
+    received = [own_ref[...]] + [r[:size] for r in received]
     for c in range(4):
         piece = received[3]
         for k in range(3):
@@ -345,7 +340,15 @@
     return place % ROWS // TILE_H * (TILE_H * TILE_W) + place % TILE_H * TILE_W + place // ROWS
 
 
-def index_kernel(across, woven, neighbours, own, capacity, source_ref, take_ref, pack_ref, put_ref):
+def prep_kernel(across, woven, neighbours, own, capacity, *refs):
+    ins, (take_ref, pack_ref, put_ref, *outs), (source_ref, space, sems) = refs[:6], refs[6:-3], refs[-3:]
+    copies = [
+        pltpu.make_async_copy(hbm, vmem, sems.at[k])
+        for k, (hbm, vmem) in enumerate(zip(ins, [source_ref, space] + outs[1:]))
+    ]
+    for copy in copies:
+        copy.start()
+    copies[0].wait()
     tile = lax.axis_index("tile")
     source = source_ref[...]
     members = source.shape[0]
@@ -379,6 +382,10 @@
     meant = jnp.where(sender == row_index(wide), first + spot % capacity, 0)
     meant = jnp.sum(meant, axis=0, keepdims=True)
     put_ref[...] = (row_index(put_ref.shape) == meant).astype(F32).astype(BF16)
+    copies[1].wait()
+    outs[0][...] = space[...].astype(F32)
+    for copy in copies[2:]:
+        copy.wait()
 
 
 def swapped(block, axis, k):
@@ -403,24 +410,39 @@
     neighbours = [(0, -1), (0, 0), (0, 1)]
     if multi:
         neighbours = [(r, c) for r in (-1, 0, 1) for c in (-1, 0, 1)]
-    take, pack, put = call(
-        functools.partial(index_kernel, across, woven, neighbours, own, capacity),
+    lines = cotangent.reshape(area, lanes)
+    spread = pltpu.VMEM((area, lanes), F32)
+    flat = [v.reshape(1, lanes) for v in (gain, shift, bias)]
+    ins = [cell_source, lines, weight] + flat
+    take, pack, put, grid, weight, gain, shift, bias = call(
+        functools.partial(prep_kernel, across, woven, neighbours, own, capacity),
         [
             shape((len(neighbours) * CELLS, members * own), BF16),
             shape((slots, CELLS), BF16),
             shape((own, slots), BF16),
+            shape((area, lanes), F32),
+        ]
+        + [shape(v.shape, v.dtype) for v in ins[2:]],
+        ins,
+        [
+            pltpu.VMEM(cell_source.shape, jnp.int32),
+            pltpu.VMEM(lines.shape, BF16),
+            pltpu.SemaphoreType.DMA((len(ins),)),
         ],
-        [cell_source],
+        loose=range(len(ins)),
     )
-    lines = cotangent.reshape(area, lanes)
-    spread = pltpu.VMEM((area, lanes), F32)
     if woven:
-        peer = swapped(tokens, "tile", 1)
-        (edges,) = call(edge_kernel, [block(4 * ROWS)], [lines], [spread])
-        edges = swapped(edges, "tile", 1)
-        (pair,) = call(join_kernel, [block(2 * own + 2 * ROWS)], [tokens, peer, edges])
+        (early,) = call(
+            early_kernel,
+            [block(own + 4 * ROWS)],
+            [tokens, lines],
+            [spread, pltpu.VMEM((area, lanes), BF16), pltpu.SemaphoreType.DMA((2,))],
+            loose=(0, 1),
+        )
+        peer = swapped(early, "tile", 1)
+        (pair,) = call(join_kernel, [block(2 * own + 2 * ROWS)], [early, peer])
         pieces = [pair] + [swapped(pair, "tile", k) for k in (2, 4, 6)]
-        others = [edges]
+        others = [peer]
     else:
         pieces = [lax.all_gather(tokens, "tile", axis=0, tiled=True)]
         others = [along_row(lines[wide - 1 :: wide], 1), along_row(lines[::wide], -1)]
@@ -438,8 +460,8 @@
     mine, hat, slope, scale, *sends, packed = call(
         functools.partial(main_kernel, members, across, woven, neighbours, len(pieces)),
         [cell, cell, cell, shape((1, lanes), F32)] + [block(size + CELLS)] * 3 + [block(size)],
-        pieces + [lines, weight, take, gain.reshape(1, -1), shift.reshape(1, -1)] + others,
-        [pltpu.VMEM((CELLS, CHANNELS), F32), spread, pltpu.VMEM((4 * ROWS, lanes), F32)],
+        pieces + [grid, weight, take, gain, shift] + others,
+        [pltpu.VMEM((CELLS, CHANNELS), F32), pltpu.VMEM((4 * ROWS, lanes), F32)],
         flops=2 * 27 * CELLS * lanes * CHANNELS,
     )
     received = [swapped(send, "chan", k + 1) for k, send in enumerate(sends)]
@@ -448,8 +470,6 @@
         functools.partial(back_kernel, size),
         halves,
         [mine, hat, slope, scale, pack] + received,
-        [pltpu.VMEM((3, CELLS, lanes), BF16), pltpu.SemaphoreType.DMA((3,))],
-        loose=(5, 6, 7),
     )
     if woven:
         came = swapped(returning[1], "tile", 1)
@@ -460,15 +480,9 @@
     (decoded,) = call(
         functools.partial(conv_kernel, multi),
         [block(area)],
-        [packed] + received + [weight, bias.reshape(1, -1)],
-        [
-            spread,
-            pltpu.VMEM((3, size, lanes), BF16),
-            pltpu.VMEM(weight.shape, BF16),
-            pltpu.SemaphoreType.DMA((4,)),
-        ],
+        [packed] + received + [weight, bias],
+        [spread],
         flops=2 * 27 * (CELLS + 2 * ROWS) * lanes * CHANNELS,
-        loose=(1, 2, 3, 4),
     )
     (token_grad,) = call(place_kernel, [block(own)], [put] + returned)
     return decoded.reshape(1, FRAMES, high, wide, lanes), token_grad

time: 41.2 us -> 35 us (0.85)
  local copies, waits for them, and re-layouts: 6.4 us -> 0 us
  waiting for transfers between devices: 14.2 us -> 11.1 us
  Pallas kernels: 5.15 us -> 7.3 us
  starting transfers between devices: 14.4 us -> 15.6 us
    unnamed x18 -> x0, local copies, waits for them, and re-layouts: 6.4 us -> none
    ppermute x12 -> x11, waiting for transfers between devices: 14.2 us -> 11.1 us  [swapped(): lax.ppermute(block, axis, [(i, i ^ k) for i in range(lax.axis_size(axis))])]
    pallas_call x8, Pallas kernels: 5.15 us -> 7.3 us  [call(): pl.pallas_call(kernel, out_shape=outs, in_specs=[FAR if i in loose else V...]
    ppermute x12 -> x11, starting transfers between devices: 14.4 us -> 15.6 us  [swapped(): lax.ppermute(block, axis, [(i, i ^ k) for i in range(lax.axis_size(axis))])]
  transfers between devices with their start and end apart: 12 -> 11, of which waited for: 7 -> 6; matrix products, arithmetic and copies ran while one was open for 0% -> 0% of each run, Pallas kernels for 5% -> 10%
where the time goes in v3:
time: 35 us; the launch traced here: 34.8 us
  starting transfers between devices  15.6 us (45%)
  waiting for transfers between devices  11.1 us (32%)
  Pallas kernels  7.3 us (21%)
  between operations  0.69 us (2%)
    ppermute x11, starting transfers between devices, swapped(): lax.ppermute(block, axis, [(i, i ^ k) for i in range(lax.axis_size(axis))])  15.6 us
    ppermute x11, waiting for transfers between devices, swapped(): lax.ppermute(block, axis, [(i, i ^ k) for i in range(lax.axis_size(axis))])  11.1 us
    pallas_call x8, Pallas kernels, call(): pl.pallas_call(kernel, out_shape=outs, in_specs=[FAR if i in loose else V...  7.3 us
  transfers between devices with their start and end apart: 11, of which 6 were waited for; matrix products, arithmetic and copies ran while one was open for 0% of the time, Pallas kernels for 10%

profile of v3, /device:TPU:0, one launch (start us, length us, event | category | flops | bytes accessed | tf_op | source)
XLA Modules:
  0.0 34.8 jit_solution(7701617558362326093)
XLA Ops:
  0.6 0.9 %shard_map.86.mine_ref = bf16[96,128]{1,0:T(8,128)(2,1)S(1)} custom-call(bf16[64,128]{1,0:T(8,128)(2,1)} %tokens_ref.1, bf16[256,128]{1,0:T(8,128)(2,1)} %bitcast.5), custom_call_target="tpu_custom_call" | custom-call | bytes 106496 | tf_op jit(solution)/shard_map/pallas_call | solution.py:33
  1.5 3.0 %collective-permute-start = (bf16[96,128]{1,0:T(8,128)(2,1)S(1)}, bf16[96,128]{1,0:T(8,128)(2,1)S(1)}, u32[]{:S(2)}, u32[]{:S(2)}) collective-permute-start(bf16[96,128]{1,0:T(8,128)(2,1)S(1)} %shard_map.86.mine_ref), channel_id=1, source_target_pairs={{0,4},{4,0},{8,12},{12,8},{16,20},{20,16},{24,28},{28,24},{1,5},{5... | collective-permute-start | bytes 73736 | tf_op jit(solution)/shard_map/ppermute | solution.py:392
  4.5 1.8 %collective-permute-done.peer_ref.refs_9_ = bf16[96,128]{1,0:T(8,128)(2,1)S(1)} collective-permute-done((bf16[96,128]{1,0:T(8,128)(2,1)S(1)}, bf16[96,128]{1,0:T(8,128)(2,1)S(1)}, u32[]{:S(2)}, u32[]{:S(2)}) %collective-permute-start) | collective-permute-done | bytes 24608 | tf_op jit(solution)/shard_map/ppermute | solution.py:392
  6.3 4.1 %collective-permute-start.3 = (bf16[144,128]{1,0:T(8,128)(2,1)S(1)}, bf16[144,128]{1,0:T(8,128)(2,1)S(1)}, u32[]{:S(2)}, u32[]{:S(2)}) collective-permute-start(bf16[144,128]{1,0:T(8,128)(2,1)S(1)} %shard_map.87.refs_0_), channel_id=1, source_target_pairs={{0,24},{4,28},{8,16},{12,20},{16,8},{20,12},{24,0},{28,4},{1,25},{... | collective-permute-start | bytes 110600 | tf_op jit(solution)/shard_map/ppermute | solution.py:392
  10.5 0.0 collective-permute-start.2
  10.5 0.6 %collective-permute-start.1 = (bf16[144,128]{1,0:T(8,128)(2,1)S(1)}, bf16[144,128]{1,0:T(8,128)(2,1)S(1)}, u32[]{:S(2)}, u32[]{:S(2)}) collective-permute-start(bf16[144,128]{1,0:T(8,128)(2,1)S(1)} %shard_map.87.refs_0_), channel_id=1, source_target_pairs={{0,8},{4,12},{8,0},{12,4},{16,24},{20,28},{24,16},{28,20},{1,9},{5... | collective-permute-start | bytes 110600 | tf_op jit(solution)/shard_map/ppermute | solution.py:392
  11.1 2.1 %shard_map.88 = (bf16[192,512]{1,0:T(8,128)(2,1)S(1)}, bf16[128,64]{1,0:T(8,128)(2,1)S(1)}, bf16[64,128]{1,0:T(8,128)(2,1)S(1)}, f32[256,128]{1,0:T(8,128)S(1)},...) custom-call(s32[8,64]{1,0:T(8,128)} %refs_0_.1, ...), custom_call_target="tpu_custom_call" | custom-call | bytes 7508992 | tf_op jit(solution)/shard_map/pallas_call | solution.py:33
  13.2 0.0 collective-permute-done.3.refs_3_
  13.2 2.1 %collective-permute-done.2.refs_2_ = bf16[144,128]{1,0:T(8,128)(2,1)S(1)} collective-permute-done((bf16[144,128]{1,0:T(8,128)(2,1)S(1)}, bf16[144,128]{1,0:T(8,128)(2,1)S(1)}, u32[]{:S(2)}, u32[]{:S(2)}) %collective-permute-start.2) | collective-permute-done | bytes 36896 | tf_op jit(solution)/shard_map/ppermute | solution.py:392
  15.3 0.0 collective-permute-done.1.refs_1_
  15.3 1.7 %shard_map.89 = (f32[64,128]{1,0:T(8,128)S(1)}, f32[64,128]{1,0:T(8,128)S(1)}, f32[64,128]{1,0:T(8,128)S(1)}, f32[1,128]{1,0:T(1,128)S(1)}, bf16[144,128]{1,0:T(...) custom-call(bf16[144,128]{1,0:T(8,128)(2,1)S(1)} %shard_map.87.refs_0_, ...), custom_call_target="tpu_custom_call" | custom-call | flops 226492416 | bytes 4269568 | tf_op jit(solution)/shard_map/pallas_call | solution.py:33
  17.1 0.1 collective-permute-start.4
  17.2 1.6 %collective-permute-start.5 = (bf16[144,128]{1,0:T(8,128)(2,1)S(1)}, bf16[144,128]{1,0:T(8,128)(2,1)S(1)}, u32[]{:S(2)}, u32[]{:S(2)}) collective-permute-start(bf16[144,128]{1,0:T(8,128)(2,1)S(1)} %get-tuple-element.31), channel_id=1, source_target_pairs={{0,2},{1,3},{2,0},{3,1},{4,6},{5,7},{6,4},{7,5},{8,10},{9,11},{10,... | collective-permute-start | bytes 110600 | tf_op jit(solution)/shard_map/ppermute | solution.py:392
  18.7 0.3 collective-permute-start.6
  19.0 0.0 collective-permute-done.4.refs_1_.refs_5_
  19.0 2.2 %collective-permute-done.5.refs_2_.refs_6_ = bf16[144,128]{1,0:T(8,128)(2,1)S(1)} collective-permute-done((bf16[144,128]{1,0:T(8,128)(2,1)S(1)}, bf16[144,128]{1,0:T(8,128)(2,1)S(1)}, u32[]{:S(2)}, u32[]{:S(2)}) %collective-permute-start.5) | collective-permute-done | bytes 36896 | tf_op jit(solution)/shard_map/ppermute | solution.py:392
  21.2 1.0 %collective-permute-done.6.refs_3_.refs_7_ = bf16[144,128]{1,0:T(8,128)(2,1)S(1)} collective-permute-done((bf16[144,128]{1,0:T(8,128)(2,1)S(1)}, bf16[144,128]{1,0:T(8,128)(2,1)S(1)}, u32[]{:S(2)}, u32[]{:S(2)}) %collective-permute-start.6) | collective-permute-done | bytes 36896 | tf_op jit(solution)/shard_map/ppermute | solution.py:392
  22.2 0.3 shard_map.91
  22.5 1.6 %collective-permute-start.7 = (bf16[64,128]{1,0:T(8,128)(2,1)S(1)}, bf16[64,128]{1,0:T(8,128)(2,1)S(1)}, u32[]{:S(2)}, u32[]{:S(2)}) collective-permute-start(bf16[64,128]{1,0:T(8,128)(2,1)S(1)} %get-tuple-element.41), channel_id=1, source_target_pairs={{0,4},{4,0},{8,12},{12,8},{16,20},{20,16},{24,28},{28,24},{1,5},{5... | collective-permute-start | bytes 49160 | tf_op jit(solution)/shard_map/ppermute | solution.py:392
  24.1 2.2 %collective-permute-done.7.came_ref = bf16[64,128]{1,0:T(8,128)(2,1)S(1)} collective-permute-done((bf16[64,128]{1,0:T(8,128)(2,1)S(1)}, bf16[64,128]{1,0:T(8,128)(2,1)S(1)}, u32[]{:S(2)}, u32[]{:S(2)}) %collective-permute-start.7) | collective-permute-done | bytes 16416 | tf_op jit(solution)/shard_map/ppermute | solution.py:392
  26.3 0.0 collective-permute-start.8
  26.3 2.3 %collective-permute-start.9 = (bf16[32,128]{1,0:T(8,128)(2,1)S(1)}, bf16[32,128]{1,0:T(8,128)(2,1)S(1)}, u32[]{:S(2)}, u32[]{:S(2)}) collective-permute-start(bf16[32,128]{1,0:T(8,128)(2,1)S(1)} %get-tuple-element.44), channel_id=1, source_target_pairs={{0,16},{4,20},{8,24},{12,28},{16,0},{20,4},{24,8},{28,12},{1,17},{... | collective-permute-start | bytes 24584 | tf_op jit(solution)/shard_map/ppermute | solution.py:392
  28.6 2.1 %collective-permute-start.10 = (bf16[32,128]{1,0:T(8,128)(2,1)S(1)}, bf16[32,128]{1,0:T(8,128)(2,1)S(1)}, u32[]{:S(2)}, u32[]{:S(2)}) collective-permute-start(bf16[32,128]{1,0:T(8,128)(2,1)S(1)} %get-tuple-element.45), channel_id=1, source_target_pairs={{0,24},{4,28},{8,16},{12,20},{16,8},{20,12},{24,0},{28,4},{1,25},{... | collective-permute-start | bytes 24584 | tf_op jit(solution)/shard_map/ppermute | solution.py:392
  30.7 1.5 %shard_map.90 = bf16[256,128]{1,0:T(8,128)(2,1)} custom-call(bf16[80,128]{1,0:T(8,128)(2,1)S(1)} %get-tuple-element.29.refs_0_, bf16[144,128]{1,0:T(8,128)(2,1)S(1)} %collective-permute-done.4.refs_1_.refs_5_, bf16[144,128]{1,0:T(8,128)(2,1)S(1)} %collective-permute-done.5.refs_2_.refs_6_, bf16[144,128]{1,0:T(8,128)(2,1)S(1)} %collective-permute-done.6.refs_3_.refs_7_, ...), custom_call_target="tpu_custom_call" | custom-call | flops 283115520 | bytes 3736064 | tf_op jit(solution)/shard_map/pallas_call | solution.py:33
  32.2 0.0 collective-permute-done.8.refs_1_
  32.2 0.0 collective-permute-done.9.refs_2_
  32.2 1.8 %collective-permute-done.10.refs_3_ = bf16[32,128]{1,0:T(8,128)(2,1)S(1)} collective-permute-done((bf16[32,128]{1,0:T(8,128)(2,1)S(1)}, bf16[32,128]{1,0:T(8,128)(2,1)S(1)}, u32[]{:S(2)}, u32[]{:S(2)}) %collective-permute-start.10) | collective-permute-done | bytes 8224 | tf_op jit(solution)/shard_map/ppermute | solution.py:392
  34.0 0.7 %shard_map.93 = bf16[64,128]{1,0:T(8,128)(2,1)} custom-call(bf16[64,128]{1,0:T(8,128)(2,1)S(1)} %get-tuple-element.34.put_ref, bf16[32,128]{1,0:T(8,128)(2,1)S(1)} %get-tuple-element.42.refs_0_, bf16[32,128]{1,0:T(8,128)(2,1)S(1)} %collective-permute-done.8.refs_1_, bf16[32,128]{1,0:T(8,128)(2,1)S(1)} %collective-permute-done.9.refs_2_, ...), custom_call_target="tpu_custom_call" | custom-call | bytes 65536 | tf_op jit(solution)/shard_map/pallas_call | solution.py:33
  (2 shorter events, 0.0 us)
Async XLA Ops:
  1.5 4.8 %collective-permute-start = (bf16[96,128]{1,0:T(8,128)(2,1)S(1)}, bf16[96,128]{1,0:T(8,128)(2,1)S(1)}, u32[]{:S(2)}, u32[]{:S(2)}) collective-permute-start(bf16[96,128]{1,0:T(8,128)(2,1)S(1)} %shard_map.86.mine_ref), channel_id=1, source_target_pairs={{0,4},{4,0},{8,12},{12,8},{16,20},{20,16},{24,28},{28,24},{1,5},{5... | collective-permute-start | bytes 73736 | tf_op jit(solution)/shard_map/ppermute | solution.py:392
  6.3 6.9 %collective-permute-start.3 = (bf16[144,128]{1,0:T(8,128)(2,1)S(1)}, bf16[144,128]{1,0:T(8,128)(2,1)S(1)}, u32[]{:S(2)}, u32[]{:S(2)}) collective-permute-start(bf16[144,128]{1,0:T(8,128)(2,1)S(1)} %shard_map.87.refs_0_), channel_id=1, source_target_pairs={{0,24},{4,28},{8,16},{12,20},{16,8},{20,12},{24,0},{28,4},{1,25},{... | collective-permute-start | bytes 110600 | tf_op jit(solution)/shard_map/ppermute | solution.py:392
  10.5 4.9 %collective-permute-start.2 = (bf16[144,128]{1,0:T(8,128)(2,1)S(1)}, bf16[144,128]{1,0:T(8,128)(2,1)S(1)}, u32[]{:S(2)}, u32[]{:S(2)}) collective-permute-start(bf16[144,128]{1,0:T(8,128)(2,1)S(1)} %shard_map.87.refs_0_), channel_id=1, source_target_pairs={{0,16},{4,20},{8,24},{12,28},{16,0},{20,4},{24,8},{28,12},{1,17},{... | collective-permute-start | bytes 110600 | tf_op jit(solution)/shard_map/ppermute | solution.py:392
  10.5 4.9 %collective-permute-start.1 = (bf16[144,128]{1,0:T(8,128)(2,1)S(1)}, bf16[144,128]{1,0:T(8,128)(2,1)S(1)}, u32[]{:S(2)}, u32[]{:S(2)}) collective-permute-start(bf16[144,128]{1,0:T(8,128)(2,1)S(1)} %shard_map.87.refs_0_), channel_id=1, source_target_pairs={{0,8},{4,12},{8,0},{12,4},{16,24},{20,28},{24,16},{28,20},{1,9},{5... | collective-permute-start | bytes 110600 | tf_op jit(solution)/shard_map/ppermute | solution.py:392
  17.1 1.9 %collective-permute-start.4 = (bf16[144,128]{1,0:T(8,128)(2,1)S(1)}, bf16[144,128]{1,0:T(8,128)(2,1)S(1)}, u32[]{:S(2)}, u32[]{:S(2)}) collective-permute-start(bf16[144,128]{1,0:T(8,128)(2,1)S(1)} %get-tuple-element.30), channel_id=1, source_target_pairs={{0,1},{1,0},{2,3},{3,2},{4,5},{5,4},{6,7},{7,6},{8,9},{9,8},{10,11... | collective-permute-start | bytes 110600 | tf_op jit(solution)/shard_map/ppermute | solution.py:392
  17.2 4.0 %collective-permute-start.5 = (bf16[144,128]{1,0:T(8,128)(2,1)S(1)}, bf16[144,128]{1,0:T(8,128)(2,1)S(1)}, u32[]{:S(2)}, u32[]{:S(2)}) collective-permute-start(bf16[144,128]{1,0:T(8,128)(2,1)S(1)} %get-tuple-element.31), channel_id=1, source_target_pairs={{0,2},{1,3},{2,0},{3,1},{4,6},{5,7},{6,4},{7,5},{8,10},{9,11},{10,... | collective-permute-start | bytes 110600 | tf_op jit(solution)/shard_map/ppermute | solution.py:392
  18.7 3.4 %collective-permute-start.6 = (bf16[144,128]{1,0:T(8,128)(2,1)S(1)}, bf16[144,128]{1,0:T(8,128)(2,1)S(1)}, u32[]{:S(2)}, u32[]{:S(2)}) collective-permute-start(bf16[144,128]{1,0:T(8,128)(2,1)S(1)} %get-tuple-element.32), channel_id=1, source_target_pairs={{0,3},{1,2},{2,1},{3,0},{4,7},{5,6},{6,5},{7,4},{8,11},{9,10},{10,... | collective-permute-start | bytes 110600 | tf_op jit(solution)/shard_map/ppermute | solution.py:392
  22.5 3.8 %collective-permute-start.7 = (bf16[64,128]{1,0:T(8,128)(2,1)S(1)}, bf16[64,128]{1,0:T(8,128)(2,1)S(1)}, u32[]{:S(2)}, u32[]{:S(2)}) collective-permute-start(bf16[64,128]{1,0:T(8,128)(2,1)S(1)} %get-tuple-element.41), channel_id=1, source_target_pairs={{0,4},{4,0},{8,12},{12,8},{16,20},{20,16},{24,28},{28,24},{1,5},{5... | collective-permute-start | bytes 49160 | tf_op jit(solution)/shard_map/ppermute | solution.py:392
  26.3 5.9 %collective-permute-start.8 = (bf16[32,128]{1,0:T(8,128)(2,1)S(1)}, bf16[32,128]{1,0:T(8,128)(2,1)S(1)}, u32[]{:S(2)}, u32[]{:S(2)}) collective-permute-start(bf16[32,128]{1,0:T(8,128)(2,1)S(1)} %get-tuple-element.43), channel_id=1, source_target_pairs={{0,8},{4,12},{8,0},{12,4},{16,24},{20,28},{24,16},{28,20},{1,9},{5... | collective-permute-start | bytes 24584 | tf_op jit(solution)/shard_map/ppermute | solution.py:392
  26.3 5.9 %collective-permute-start.9 = (bf16[32,128]{1,0:T(8,128)(2,1)S(1)}, bf16[32,128]{1,0:T(8,128)(2,1)S(1)}, u32[]{:S(2)}, u32[]{:S(2)}) collective-permute-start(bf16[32,128]{1,0:T(8,128)(2,1)S(1)} %get-tuple-element.44), channel_id=1, source_target_pairs={{0,16},{4,20},{8,24},{12,28},{16,0},{20,4},{24,8},{28,12},{1,17},{... | collective-permute-start | bytes 24584 | tf_op jit(solution)/shard_map/ppermute | solution.py:392
  28.6 5.4 %collective-permute-start.10 = (bf16[32,128]{1,0:T(8,128)(2,1)S(1)}, bf16[32,128]{1,0:T(8,128)(2,1)S(1)}, u32[]{:S(2)}, u32[]{:S(2)}) collective-permute-start(bf16[32,128]{1,0:T(8,128)(2,1)S(1)} %get-tuple-element.45), channel_id=1, source_target_pairs={{0,24},{4,28},{8,16},{12,20},{16,8},{20,12},{24,0},{28,4},{1,25},{... | collective-permute-start | bytes 24584 | tf_op jit(solution)/shard_map/ppermute | solution.py:392

commit v4 on v3

v4 whole, which is shorter than its diff:
```python
import functools

import jax
import jax.numpy as jnp
from jax import lax
from jax.experimental import pallas as pl
from jax.experimental.pallas import tpu as pltpu
from jax.sharding import PartitionSpec as P

CHANNELS = 512
GROUP = 16
FRAMES = 2
TILE_H = 4
TILE_W = 8
CELLS = FRAMES * TILE_H * TILE_W
ROWS = FRAMES * TILE_H
EPS = 1e-06
VMEM_LIMIT = 12 * 2**20
F32 = jnp.float32
BF16 = jnp.bfloat16
VMEM = pl.BlockSpec(memory_space=pltpu.VMEM)
FAR = pl.BlockSpec(memory_space=pltpu.HBM)
HIGHEST = lax.Precision.HIGHEST


def call(kernel, outs, args, scratch=(), flops=0, loose=()):
    args = [
        pltpu.with_memory_space_constraint(a, pltpu.HBM) if i in loose else a
        for i, a in enumerate(args)
    ]
    moved = sum(a.size * a.dtype.itemsize for a in args)
    moved += sum(o.size * o.dtype.itemsize for o in outs)
    return pl.pallas_call(
        kernel,
        out_shape=outs,
        in_specs=[FAR if i in loose else VMEM for i in range(len(args))],
        out_specs=[VMEM] * len(outs),
        scratch_shapes=list(scratch),
        compiler_params=pltpu.CompilerParams(vmem_limit_bytes=VMEM_LIMIT),
        cost_estimate=pl.CostEstimate(flops=flops, bytes_accessed=moved, transcendentals=0),
    )(*args)


def across_tiles():
    return min(lax.axis_size("tile"), 16)


def along_row(block, step):
    count, across = lax.axis_size("tile"), across_tiles()
    route = [(i, i + step) for i in range(count) if 0 <= i % across + step < across]
    return lax.ppermute(block, "tile", route)


def along_column(block, step):
    count, across = lax.axis_size("tile"), across_tiles()
    route = [(i, i + step * across) for i in range(count) if 0 <= i + step * across < count]
    return lax.ppermute(block, "tile", route)


def row_index(shape):
    return lax.broadcasted_iota(jnp.int32, shape, 0)


def from_row_above(x):
    keep = row_index(x.shape) % TILE_H != 0
    return jnp.where(keep, pltpu.roll(x, 1, 0), 0.0)


def from_row_below(x):
    keep = row_index(x.shape) % TILE_H != TILE_H - 1
    return jnp.where(keep, pltpu.roll(x, x.shape[0] - 1, 0), 0.0)


def folded_columns(grid, cut, wide, left=None, right=None):
    def column(p, x):
        if x < 0:
            return left(p)
        if x >= wide:
            return right(p)
        return grid[pl.ds(x // cut * (FRAMES * 2 * TILE_H * cut) + p * cut + x % cut, ROWS, stride=2 * cut), :]

    return [[column(p, x) for x in range(-1, wide + 1)] for p in range(2)]


def fold(parts, e):
    pairs = [parts[2 * s + 2 - e] + parts[2 * s + 3 - e] for s in range(len(parts) // 2 - 1)]
    return jnp.concatenate(pairs, axis=0)


def fold_taps(columns, rims=()):
    taps = [None] * 9
    for e in range(3):
        even, odd = fold(columns[0], e), fold(columns[1], e)
        below, above = from_row_below(even), from_row_above(odd)
        if rims:
            high = [rims[0][x].astype(F32) for x in range(len(columns[0]))]
            low = [rims[1][x].astype(F32) for x in range(len(columns[0]))]
            below, above = below + fold(low, e), above + fold(high, e)
        taps[e], taps[3 + e], taps[6 + e] = odd + below, even + odd, above + even
    return taps


def adjoint(taps, w_ref):
    rows = taps[0].shape[0]
    total = jnp.zeros((rows, CHANNELS), F32)
    first = row_index(taps[0].shape) % ROWS < TILE_H
    latest = []
    for tap, value in enumerate(taps):
        both = value + pltpu.roll(value, rows - TILE_H, 0)
        both = jnp.where(first, both, 0.0).astype(BF16)
        latest.append((value.astype(BF16), tap + 18))
        total = total + contract(both, tap, both, tap + 9, w_ref)
        if len(latest) == 2:
            (x, i), (y, j) = latest
            total = total + contract(x, i, y, j, w_ref)
            latest = []
    for x, i in latest:
        total = total + lax.dot_general(
            x, w_ref[i], (((1,), (1,)), ((), ())), preferred_element_type=F32
        )
    return total


def share(partial_ref, outs):
    lanes = outs[0].shape[1]
    chan = lax.axis_index("chan")
    for k, out in enumerate(outs):
        begin = pl.multiple_of((chan ^ k) * lanes, 128)
        out[...] = partial_ref[:, pl.ds(begin, lanes)].astype(out.dtype)


def contract(x, i, y, j, w_ref):
    left = jnp.concatenate([x, y], axis=1)
    right = jnp.concatenate([w_ref[i], w_ref[j]], axis=1)
    return lax.dot_general(left, right, (((1,), (1,)), ((), ())), preferred_element_type=F32)


def group_mean(sums):
    lanes = sums.shape[1]
    left = lax.broadcasted_iota(jnp.int32, (lanes, lanes), 0) // GROUP
    right = lax.broadcasted_iota(jnp.int32, (lanes, lanes), 1) // GROUP
    same = (left == right).astype(F32)
    whole = jnp.dot(sums, same, preferred_element_type=F32, precision=HIGHEST)
    return whole * (1.0 / (CELLS * GROUP))


def column_sums(x):
    return jnp.sum(x, axis=0, keepdims=True)


def silu_parts(hat, gain, shift):
    value = hat * gain + shift
    gate = 1.0 / (1.0 + jnp.exp(-value))
    return value * gate, gate * (1.0 + value * (1.0 - gate)) * gain


def standardized(features):
    means = group_mean(stacked([column_sums(f) for f in features]))
    centred = [f - means[i : i + 1] for i, f in enumerate(features)]
    spreads = group_mean(stacked([column_sums(c * c) for c in centred]))
    scales = lax.rsqrt(spreads + EPS)
    return [c * scales[i : i + 1] for i, c in enumerate(centred)], scales


def tile_adjoint_kernel(grid_ref, w_ref, left_ref, right_ref, *refs):
    rims, outs, (partial_ref, sides) = refs[:-6], refs[-6:-2], refs[-2:]
    wide = 2 * TILE_W
    sides[: 2 * ROWS] = left_ref[...].astype(F32)
    sides[2 * ROWS :] = right_ref[...].astype(F32)
    columns = folded_columns(
        grid_ref,
        wide,
        wide,
        lambda p: sides[pl.ds(p, ROWS, stride=2), :],
        lambda p: sides[pl.ds(2 * ROWS + p, ROWS, stride=2), :],
    )
    partial_ref[...] = adjoint(fold_taps(columns, rims), w_ref)
    share(partial_ref, outs)


def tile_norm_kernel(members, across, neighbours, *refs):
    tokens_ref, take_ref, gain_ref, shift_ref = refs[:4]
    hat_ref, slope_ref, scale_ref, own_ref = refs[4:]
    tile = lax.axis_index("tile")
    tokens = tokens_ref[...]
    lanes = tokens.shape[1]
    gain, shift = gain_ref[...], shift_ref[...]
    there = []
    for dr, dc in neighbours:
        col, row = tile % across + dc, tile // across + dr
        there.append((col >= 0) & (col < across) & (row >= 0) & (row < members // across))
    chosen = take_ref[...]
    features = jnp.dot(chosen, tokens, preferred_element_type=F32)
    features = [features[i * CELLS : (i + 1) * CELLS] for i in range(len(neighbours))]
    hats, scales = standardized(features)
    blocks = {}
    for i, (dr, dc) in enumerate(neighbours):
        hat = hats[i][-ROWS:] if dc == -1 else hats[i][:ROWS] if dc == 1 else hats[i]
        active, slope = silu_parts(hat, gain, shift)
        if (dr, dc) == (0, 0):
            hat_ref[...] = hat
            slope_ref[...] = slope
            scale_ref[...] = scales[i : i + 1]
        else:
            active = jnp.where(there[i], active, 0.0)
        blocks[dr, dc] = active
    parts = [blocks[0, dc] for dc in (-1, 0, 1)]
    if len(neighbours) == 9:
        rows = CELLS + 2 * ROWS
        line = row_index((rows, lanes)) % TILE_H
        for dr, take, keep in ((-1, rows - TILE_H + 1, 0), (1, TILE_H - 1, TILE_H - 1)):
            block = jnp.concatenate([blocks[dr, dc] for dc in (-1, 0, 1)], axis=0)
            parts.append(jnp.where(line == keep, pltpu.roll(block, take, 0), 0.0))
    own_ref[...] = jnp.concatenate(parts, axis=0).astype(BF16)


def pair_adjoint_kernel(taps_ref, w_ref, *refs):
    pieces, outs, (partial_ref, sides) = refs[:4], refs[4:8], refs[8:]
    place = lax.axis_index("tile") // 2
    zero = jnp.zeros((2 * ROWS, taps_ref.shape[2]), BF16)
    left, right = zero, zero
    for k in range(1, 4):
        edges = pieces[k][-4 * ROWS :]
        left = jnp.where(place ^ k == place - 1, edges[2 * ROWS :], left)
        right = jnp.where(place ^ k == place + 1, edges[: 2 * ROWS], right)
    sides[: 2 * ROWS] = left.astype(F32)
    sides[2 * ROWS :] = right.astype(F32)
    rims = []
    for begin in (0, 2 * ROWS):
        even, odd = (sides[pl.ds(begin + p, ROWS, stride=2), :] for p in range(2))
        below, above = from_row_below(even), from_row_above(odd)
        rims.append((odd + below, even + odd, above + even))
    taps = []
    for tap in range(9):
        value, b, e = taps_ref[tap], tap // 3, tap % 3
        if e == 0:
            value = jnp.concatenate([value[:-ROWS], value[-ROWS:] + rims[1][b]], axis=0)
        if e == 2:
            value = jnp.concatenate([value[:ROWS] + rims[0][b], value[ROWS:]], axis=0)
        taps.append(value)
    partial_ref[...] = adjoint(taps, w_ref)
    share(partial_ref, outs)


def pair_norm_kernel(*refs):
    pieces, (take_ref, gain_ref, shift_ref) = refs[:4], refs[4:7]
    hat_ref, slope_ref, scale_ref, own_ref = refs[7:]
    tile = lax.axis_index("tile")
    odd = tile % 2 == 1
    tokens = jnp.concatenate([p[: -4 * ROWS] for p in pieces], axis=0)
    features = jnp.dot(take_ref[...], tokens, preferred_element_type=F32)
    hats, scales = standardized([features[i * CELLS : (i + 1) * CELLS] for i in range(3)])
    hat = jnp.concatenate(hats[:2], axis=0)
    active, slope = silu_parts(hat, gain_ref[...], shift_ref[...])
    hat_ref[...] = hat
    slope_ref[...] = slope
    scale_ref[...] = scales[:2]
    outer = jnp.where(odd, hats[2][:ROWS], hats[2][-ROWS:])
    outer, _ = silu_parts(outer, gain_ref[...], shift_ref[...])
    outer = jnp.where((tile == 0) | (tile == 7), 0.0, outer)
    own_ref[:ROWS] = jnp.where(odd, active[CELLS - ROWS : CELLS], outer).astype(BF16)
    own_ref[ROWS:-ROWS] = jnp.where(odd, active[CELLS:], active[:CELLS]).astype(BF16)
    own_ref[-ROWS:] = jnp.where(odd, outer, active[CELLS : CELLS + ROWS]).astype(BF16)


def stacked(rows):
    lanes = rows[0].shape[1]
    pad = -len(rows) % 8
    if pad:
        rows = rows + [jnp.zeros((pad, lanes), F32)]
    return jnp.concatenate(rows, axis=0)


def fetch(copies):
    for copy in copies:
        copy.start()
    for copy in copies:
        copy.wait()


def back_kernel(*refs):
    mine_ref, hat_ref, slope_ref, scale_ref, pack_ref = refs[:5]
    received, outs = refs[5:8], refs[8:]
    grad = mine_ref[...]
    for r in received:
        grad = grad + r[...].astype(F32)
    grad = grad * slope_ref[...]
    hat = hat_ref[...]
    tiles = grad.shape[0] // CELLS
    spans = [slice(i * CELLS, (i + 1) * CELLS) for i in range(tiles)]
    sums = [column_sums(grad[c]) for c in spans] + [column_sums(grad[c] * hat[c]) for c in spans]
    means = group_mean(stacked(sums))
    result = []
    for i, c in enumerate(spans):
        value = grad[c] - means[i : i + 1] - hat[c] * means[tiles + i : tiles + i + 1]
        result.append(scale_ref[i : i + 1] * value)
    result = (jnp.concatenate(result, axis=0) if tiles > 1 else result[0]).astype(BF16)
    packed = jnp.dot(pack_ref[...], result, preferred_element_type=F32).astype(BF16)
    begin = 0
    for out in outs:
        out[...] = packed[begin : begin + out.shape[0]]
        begin += out.shape[0]


def fetch(copies):
    for copy in copies:
        copy.start()
    for copy in copies:
        copy.wait()


def early_kernel(tokens_ref, lines_ref, own_ref, grid_ref, space, sems):
    fetch(
        [
            pltpu.make_async_copy(tokens_ref, own_ref, sems.at[0]),
            pltpu.make_async_copy(lines_ref, space, sems.at[1]),
        ]
    )
    grid_ref[...] = space[...].astype(F32)


def join_kernel(own_ref, peer_ref, grid_ref, lines_ref, out_ref, pair_ref):
    own, area = own_ref.shape[0], grid_ref.shape[0]
    odd = lax.axis_index("tile") % 2
    wide = 2 * TILE_W
    out_ref[pl.ds(pl.multiple_of(odd * own, own), own), :] = own_ref[...]
    out_ref[pl.ds(pl.multiple_of((1 - odd) * own, own), own), :] = peer_ref[...]
    pair_ref[pl.ds(pl.multiple_of(odd * area, area), area), :] = grid_ref[...]
    pair_ref[pl.ds(pl.multiple_of((1 - odd) * area, area), area), :] = lines_ref[...].astype(F32)
    left = pair_ref[pl.ds(0, 2 * ROWS, stride=wide), :]
    right = pair_ref[pl.ds(area + wide - 1, 2 * ROWS, stride=wide), :]
    out_ref[2 * own : 2 * own + 2 * ROWS] = left.astype(BF16)
    out_ref[2 * own + 2 * ROWS :] = right.astype(BF16)


def conv_kernel(multi, *refs):
    own_ref, *received, w_ref, bias_ref, out_ref, grid = refs
    chan = lax.axis_index("chan")
    rows = CELLS + 2 * ROWS
    lanes = own_ref.shape[1]
    grid_in = []
    received = [own_ref[...]] + [r[...] for r in received]
    for c in range(4):
        piece = received[3]
        for k in range(3):
            piece = jnp.where(chan ^ k == c, received[k], piece)
        grid_in.append(piece)
    cells = jnp.concatenate(grid_in, axis=1).astype(F32)
    line = row_index(cells.shape) % ROWS < TILE_H
    early = jnp.where(line, cells, pltpu.roll(cells, TILE_H, 0)).astype(BF16)
    cells = cells.astype(BF16)

    def products(taps, begin):
        x = cells[begin : begin + rows]
        y = early[begin : begin + rows]
        made = {}
        for at in range(0, len(taps), 2):
            pair = taps[at : at + 2]
            acc = None
            for a, left in ((0, y), (9, y), (18, x)):
                right = jnp.concatenate([w_ref[a + t] for t in pair], axis=1)
                term = jnp.dot(left, right, preferred_element_type=F32)
                acc = term if acc is None else acc + term
            for n, t in enumerate(pair):
                made[t] = acc[:, n * lanes : (n + 1) * lanes]
        return made

    def spread(made, b, q):
        first, middle, last = (made[3 * b + e] for e in range(3))
        if q == 0:
            return first[:CELLS] + middle[ROWS:-ROWS] + last[ROWS:-ROWS]
        return first[ROWS:-ROWS] + middle[ROWS:-ROWS] + last[2 * ROWS :]

    made = products(list(range(9)), 0)
    if multi:
        made_above = products([0, 1, 2], rows)
        made_below = products([6, 7, 8], 2 * rows)
    wide = 2 * TILE_W
    for q in range(2):
        top, middle, bottom = (spread(made, b, q) for b in range(3))
        above, below = from_row_above(top), from_row_below(bottom)
        if multi:
            above = above + spread(made_above, 0, q)
            below = below + spread(made_below, 2, q)
        for p, value in enumerate((above + middle + bottom, top + middle + below)):
            value = value + bias_ref[...]
            for j in range(TILE_W):
                grid[pl.ds(p * wide + 2 * j + q, ROWS, stride=2 * wide), :] = value[
                    j * ROWS : (j + 1) * ROWS
                ]
    out_ref[...] = grid[...].astype(BF16)


def place_kernel(put_ref, *refs):
    returned, out_ref = refs[:-1], refs[-1]
    values = [r[...] for r in returned]
    values = jnp.concatenate(values, axis=0) if len(values) > 1 else values[0]
    placed = jnp.dot(put_ref[...], values, preferred_element_type=F32)
    out_ref[...] = placed.astype(BF16)


def cell_of(place):
    return place % ROWS // TILE_H * (TILE_H * TILE_W) + place % TILE_H * TILE_W + place // ROWS


def sources_of(source_ref, tile):
    square = (CELLS, CELLS)
    left = lax.broadcasted_iota(jnp.int32, square, 0)
    right = lax.broadcasted_iota(jnp.int32, square, 1)
    line = source_ref[pl.ds(tile, 1), :]
    column = jnp.sum(jnp.where(cell_of(left) == right, line, 0), axis=1, keepdims=True)
    return column, jnp.sum(jnp.where(left == right, column, 0), axis=0, keepdims=True)


def one_hot(match):
    return match.astype(F32).astype(BF16)


def first_places(source, own, capacity, sender):
    members = source.shape[0]
    first = jnp.where(source // own == lax.axis_index("tile"), source % own, -capacity)
    first = jnp.max(first, axis=1, keepdims=True) // capacity * capacity
    wide = (members, members * capacity)
    spot = lax.broadcasted_iota(jnp.int32, wide, 1)
    match = sender(spot // capacity) == row_index(wide)
    return jnp.sum(jnp.where(match, first + spot % capacity, 0), axis=0, keepdims=True)


def load_all(ins, outs, sems):
    copies = [
        pltpu.make_async_copy(hbm, vmem, sems.at[k]) for k, (hbm, vmem) in enumerate(zip(ins, outs))
    ]
    for copy in copies:
        copy.start()
    return copies


def tile_prep_kernel(across, neighbours, own, capacity, *refs):
    ins, (take_ref, pack_ref, put_ref, grid_ref, *outs) = refs[:6], refs[6:-3]
    source_ref, space, sems = refs[-3:]
    copies = load_all(ins, [source_ref, space] + outs, sems)
    for copy in copies:
        copy.wait()
    tile = lax.axis_index("tile")
    members = source_ref.shape[0]
    place = lax.broadcasted_iota(jnp.int32, (CELLS, members * own), 1)
    for i, (dr, dc) in enumerate(neighbours):
        other = jnp.clip(tile + dr * across + dc, 0, members - 1)
        column, row = sources_of(source_ref, other)
        if (dr, dc) == (0, 0):
            slot = row // own * capacity + row % capacity
            pack_ref[...] = one_hot(row_index(pack_ref.shape) == slot)
        take_ref[i * CELLS : (i + 1) * CELLS] = one_hot(place == column)
    spots = first_places(source_ref[...], own, capacity, lambda sender: sender)
    put_ref[...] = one_hot(row_index(put_ref.shape) == spots)
    grid_ref[...] = space[...].astype(F32)


def pair_prep_kernel(own, capacity, pair_ref, *refs):
    ins, (take_ref, pack_ref, put_ref, taps_ref, *outs), (source_ref, sems) = refs[:5], refs[5:-2], refs[-2:]
    copies = load_all(ins, [source_ref] + outs, sems)
    wide = 2 * TILE_W
    zero = jnp.zeros((ROWS, pair_ref.shape[1]), F32)
    columns = folded_columns(pair_ref, wide, 2 * wide, lambda p: zero, lambda p: zero)
    for tap, value in enumerate(fold_taps(columns)):
        taps_ref[tap] = value
    copies[0].wait()
    tile = lax.axis_index("tile")
    z, x = tile // 2, tile % 2
    members = source_ref.shape[0]
    place = lax.broadcasted_iota(jnp.int32, (CELLS, members * own), 1)
    outer = jnp.clip(tile + 2 * x - 1, 0, members - 1)
    for i, other in enumerate((2 * z, 2 * z + 1, outer)):
        column, row = sources_of(source_ref, other)
        take_ref[i * CELLS : (i + 1) * CELLS] = one_hot(place == column ^ (2 * z * own))
        if i < 2:
            owner = row // own
            slot = (owner // 2 ^ z) * (2 * capacity) + i * capacity + row % capacity
            slot = jnp.where(owner % 2 == x, slot, -1)
            shape = (pack_ref.shape[0], CELLS)
            pack_ref[:, i * CELLS : (i + 1) * CELLS] = one_hot(row_index(shape) == slot)
    spots = first_places(source_ref[...], own, capacity, lambda k: (k // 2 ^ z) * 2 + k % 2)
    put_ref[...] = one_hot(row_index(put_ref.shape) == spots)
    for copy in copies[1:]:
        copy.wait()


def swapped(block, axis, k):
    return lax.ppermute(block, axis, [(i, i ^ k) for i in range(lax.axis_size(axis))])


def shape(rows, lanes, kind=BF16):
    return jax.ShapeDtypeStruct((rows, lanes), kind)


def chan_swaps(blocks):
    return [swapped(block, "chan", k + 1) for k, block in enumerate(blocks)]


def pair_plan(tokens, cell_source, gain, shift, weight, bias, lines):
    own, lanes = tokens.shape
    members = lax.axis_size("tile")
    capacity = max(2, own // (members // 2))
    slots = members * capacity
    area = lines.shape[0]
    peer = swapped(tokens, "tile", 1)
    other = swapped(lines, "tile", 1)
    kept, grid = call(
        early_kernel,
        [shape(own, lanes), shape(area, lanes, F32)],
        [tokens, lines],
        [pltpu.VMEM((area, lanes), BF16), pltpu.SemaphoreType.DMA((2,))],
        loose=(0, 1),
    )
    block, pair = call(
        join_kernel,
        [shape(2 * own + 4 * ROWS, lanes), shape(2 * area, lanes, F32)],
        [kept, peer, grid, other],
    )
    pieces = [block] + [swapped(block, "tile", k) for k in (2, 4, 6)]
    ins = [cell_source, weight] + [v.reshape(1, lanes) for v in (gain, shift, bias)]
    take, pack, put, taps, weight, gain, shift, bias = call(
        functools.partial(pair_prep_kernel, own, capacity),
        [
            shape(3 * CELLS, members * own),
            shape(slots, 2 * CELLS),
            shape(own, slots),
            jax.ShapeDtypeStruct((9, 2 * CELLS, lanes), F32),
        ]
        + [jax.ShapeDtypeStruct(v.shape, v.dtype) for v in ins[1:]],
        [pair] + ins,
        [pltpu.VMEM(cell_source.shape, jnp.int32), pltpu.SemaphoreType.DMA((len(ins),))],
        loose=range(1, 6),
    )
    cell = shape(2 * CELLS, lanes, F32)
    mine, *sends = call(
        pair_adjoint_kernel,
        [cell] + [shape(2 * CELLS, lanes)] * 3,
        [taps, weight] + pieces,
        [pltpu.VMEM((2 * CELLS, CHANNELS), F32), pltpu.VMEM((4 * ROWS, lanes), F32)],
        flops=4 * 27 * CELLS * lanes * CHANNELS,
    )
    sends = chan_swaps(sends)
    hat, slope, scale, cells = call(
        pair_norm_kernel,
        [cell, cell, shape(2, lanes, F32), shape(CELLS + 2 * ROWS, lanes)],
        pieces + [take, gain, shift],
        flops=6 * CELLS * members * own * lanes,
    )
    received = chan_swaps([cells] * 3)
    routed = call(
        back_kernel,
        [shape(2 * capacity, lanes)] * 4,
        [mine, hat, slope, scale, pack] + sends,
    )
    returned = [routed[0]] + [swapped(r, "tile", 2 * k + 2) for k, r in enumerate(routed[1:])]
    return cells, received, weight, bias, put, returned


def tile_plan(tokens, cell_source, gain, shift, weight, bias, lines):
    own, lanes = tokens.shape
    members = lax.axis_size("tile")
    across = across_tiles()
    multi = members > across
    capacity = max(2, own // (members // 2))
    slots = members * capacity
    high, wide = 2 * TILE_H, 2 * TILE_W
    area = lines.shape[0]
    neighbours = [(0, -1), (0, 0), (0, 1)]
    if multi:
        neighbours = [(r, c) for r in (-1, 0, 1) for c in (-1, 0, 1)]
    gathered = lax.all_gather(tokens, "tile", axis=0, tiled=True)
    others = [along_row(lines[wide - 1 :: wide], 1), along_row(lines[::wide], -1)]
    if multi:
        side = (FRAMES, high, 1, lanes)
        widened = [others[0].reshape(side), lines.reshape(FRAMES, high, wide, lanes)]
        widened = jnp.concatenate(widened + [others[1].reshape(side)], axis=2)
        for edge, step, line in ((widened[:, -1], 1, 0), (widened[:, 0], -1, TILE_H - 1)):
            rim = along_column(edge, step).transpose(1, 0, 2)
            spaced = jnp.zeros((wide + 2, FRAMES, TILE_H, lanes), BF16).at[:, :, line].set(rim)
            others.append(spaced.reshape(wide + 2, ROWS, lanes))
    ins = [cell_source, lines, weight] + [v.reshape(1, lanes) for v in (gain, shift, bias)]
    take, pack, put, grid, weight, gain, shift, bias = call(
        functools.partial(tile_prep_kernel, across, neighbours, own, capacity),
        [
            shape(len(neighbours) * CELLS, members * own),
            shape(slots, CELLS),
            shape(own, slots),
            shape(area, lanes, F32),
        ]
        + [jax.ShapeDtypeStruct(v.shape, v.dtype) for v in ins[2:]],
        ins,
        [
            pltpu.VMEM(cell_source.shape, jnp.int32),
            pltpu.VMEM(lines.shape, BF16),
            pltpu.SemaphoreType.DMA((len(ins),)),
        ],
        loose=range(len(ins)),
    )
    cell = shape(CELLS, lanes, F32)
    mine, *sends = call(
        tile_adjoint_kernel,
        [cell] + [shape(CELLS, lanes)] * 3,
        [grid, weight] + others,
        [pltpu.VMEM((CELLS, CHANNELS), F32), pltpu.VMEM((4 * ROWS, lanes), F32)],
        flops=2 * 27 * CELLS * lanes * CHANNELS,
    )
    sends = chan_swaps(sends)
    size = (CELLS + 2 * ROWS) * (3 if multi else 1)
    hat, slope, scale, cells = call(
        functools.partial(tile_norm_kernel, members, across, neighbours),
        [cell, cell, shape(1, lanes, F32), shape(size, lanes)],
        [gathered, take, gain, shift],
        flops=2 * len(neighbours) * CELLS * members * own * lanes,
    )
    received = chan_swaps([cells] * 3)
    (packed,) = call(back_kernel, [shape(slots, lanes)], [mine, hat, slope, scale, pack] + sends)
    returned = lax.all_to_all(packed, "tile", split_axis=0, concat_axis=0, tiled=True)
    return cells, received, weight, bias, put, [returned]


def local(tokens, cell_source, gain, shift, weight, bias, cotangent):
    own, lanes = tokens.shape
    lines = cotangent.reshape(-1, lanes)
    members = lax.axis_size("tile")
    plan = pair_plan if members == 8 else tile_plan
    cells, received, weight, bias, put, returned = plan(
        tokens, cell_source, gain, shift, weight, bias, lines
    )
    (decoded,) = call(
        functools.partial(conv_kernel, members > across_tiles()),
        [shape(lines.shape[0], lanes)],
        [cells] + received + [weight, bias],
        [pltpu.VMEM(lines.shape, F32)],
        flops=2 * 27 * (CELLS + 2 * ROWS) * lanes * CHANNELS,
    )
    (token_grad,) = call(place_kernel, [shape(own, lanes)], [put] + returned)
    return decoded.reshape(cotangent.shape), token_grad


def solution(mesh):
    in_specs = (
        P("tile", "chan"),
        P(),
        P("chan"),
        P("chan"),
        P(None, None, "chan"),
        P("chan"),
        P("tile", None, None, None, "chan"),
    )
    out_specs = (P("tile", None, None, None, "chan"), P("tile", "chan"))
    return jax.shard_map(local, mesh=mesh, in_specs=in_specs, out_specs=out_specs, check_vma=False)
```

time: 35 us -> 32.5 us (0.929)
  waiting for transfers between devices: 11.1 us -> 7.84 us
  starting transfers between devices: 15.6 us -> 16.1 us
    ppermute x11 -> x14, waiting for transfers between devices: 11.1 us -> 7.84 us  [swapped(): lax.ppermute(block, axis, [(i, i ^ k) for i in range(lax.axis_size(axis))])]
    ppermute x11 -> x14, starting transfers between devices: 15.6 us -> 16.1 us  [swapped(): lax.ppermute(block, axis, [(i, i ^ k) for i in range(lax.axis_size(axis))])]
  transfers between devices with their start and end apart: 11 -> 14, of which waited for: 6 -> 5; matrix products, arithmetic and copies ran while one was open for 0% -> 0% of each run, Pallas kernels for 10% -> 17%
where the time goes in v4:
time: 32.5 us; the launch traced here: 32.2 us
  starting transfers between devices  16.1 us (50%)
  waiting for transfers between devices  7.84 us (24%)
  Pallas kernels  7.58 us (23%)
  between operations  0.72 us (2%)
    ppermute x14, starting transfers between devices, swapped(): lax.ppermute(block, axis, [(i, i ^ k) for i in range(lax.axis_size(axis))])  16.1 us
    ppermute x14, waiting for transfers between devices, swapped(): lax.ppermute(block, axis, [(i, i ^ k) for i in range(lax.axis_size(axis))])  7.84 us
    pallas_call x8, Pallas kernels, call(): pl.pallas_call(kernel, out_shape=outs, in_specs=[FAR if i in loose else V...  7.58 us
  transfers between devices with their start and end apart: 14, of which 5 were waited for; matrix products, arithmetic and copies ran while one was open for 0% of the time, Pallas kernels for 17%

profile of v4, /device:TPU:0, one launch (start us, length us, event | category | flops | bytes accessed | tf_op | source)
XLA Modules:
  0.0 32.2 jit_solution(10166448183195539181)
XLA Ops:
  0.6 3.0 %collective-permute-start.1 = (bf16[256,128]{1,0:T(8,128)(2,1)}, bf16[256,128]{1,0:T(8,128)(2,1)S(1)}, u32[]{:S(2)}, u32[]{:S(2)}) collective-permute-start(bf16[256,128]{1,0:T(8,128)(2,1)} %bitcast.6), channel_id=1, source_target_pairs={{0,4},{4,0},{8,12},{12,8},{16,20},{20,16},{24,28},{28,24},{1,5},{5... | collective-permute-start | bytes 196616 | tf_op jit(solution)/shard_map/ppermute | solution.py:489
  3.6 0.1 collective-permute-start
  3.7 0.9 %shard_map.86 = (bf16[64,128]{1,0:T(8,128)(2,1)S(1)}, f32[256,128]{1,0:T(8,128)S(1)}) custom-call(bf16[64,128]{1,0:T(8,128)(2,1)} %tokens_ref.1, bf16[256,128]{1,0:T(8,128)(2,1)} %bitcast.7), custom_call_target="tpu_custom_call" | custom-call | bytes 229376 | tf_op jit(solution)/shard_map/pallas_call | solution.py:33
  4.6 3.0 %collective-permute-done.peer_ref = bf16[64,128]{1,0:T(8,128)(2,1)S(1)} collective-permute-done((bf16[64,128]{1,0:T(8,128)(2,1)}, bf16[64,128]{1,0:T(8,128)(2,1)S(1)}, u32[]{:S(2)}, u32[]{:S(2)}) %collective-permute-start) | collective-permute-done | bytes 16416 | tf_op jit(solution)/shard_map/ppermute | solution.py:489
  7.6 0.0 collective-permute-done.1.lines_ref
  7.6 1.6 %collective-permute-start.2 = (bf16[160,128]{1,0:T(8,128)(2,1)S(1)}, bf16[160,128]{1,0:T(8,128)(2,1)S(1)}, u32[]{:S(2)}, u32[]{:S(2)}) collective-permute-start(bf16[160,128]{1,0:T(8,128)(2,1)S(1)} %get-tuple-element.28.refs_0_), channel_id=1, source_target_pairs={{0,8},{4,12},{8,0},{12,4},{16,24},{20,28},{24,16},{28,20},{1,9},{5... | collective-permute-start | bytes 122888 | tf_op jit(solution)/shard_map/ppermute | solution.py:489
  9.3 2.6 %collective-permute-start.3 = (bf16[160,128]{1,0:T(8,128)(2,1)S(1)}, bf16[160,128]{1,0:T(8,128)(2,1)S(1)}, u32[]{:S(2)}, u32[]{:S(2)}) collective-permute-start(bf16[160,128]{1,0:T(8,128)(2,1)S(1)} %get-tuple-element.28.refs_0_), channel_id=1, source_target_pairs={{0,16},{4,20},{8,24},{12,28},{16,0},{20,4},{24,8},{28,12},{1,17},{... | collective-permute-start | bytes 122888 | tf_op jit(solution)/shard_map/ppermute | solution.py:489
  11.9 0.2 collective-permute-start.4
  12.1 2.1 %shard_map.88 = (bf16[192,512]{1,0:T(8,128)(2,1)S(1)}, bf16[128,128]{1,0:T(8,128)(2,1)S(1)}, bf16[64,128]{1,0:T(8,128)(2,1)S(1)}, f32[9,128,128]{2,1,0:T(8,128)S...) custom-call(f32[512,128]{1,0:T(8,128)S(1)} %get-tuple-element.29.pai, ...), custom_call_target="tpu_custom_call" | custom-call | bytes 8180736 | tf_op jit(solution)/shard_map/pallas_call | solution.py:33
  14.2 0.0 collective-permute-done.2.refs_1_
  14.2 0.9 %collective-permute-done.3.refs_2_ = bf16[160,128]{1,0:T(8,128)(2,1)S(1)} collective-permute-done((bf16[160,128]{1,0:T(8,128)(2,1)S(1)}, bf16[160,128]{1,0:T(8,128)(2,1)S(1)}, u32[]{:S(2)}, u32[]{:S(2)}) %collective-permute-start.3) | collective-permute-done | bytes 40992 | tf_op jit(solution)/shard_map/ppermute | solution.py:489
  15.0 2.6 %collective-permute-done.4.refs_3_ = bf16[160,128]{1,0:T(8,128)(2,1)S(1)} collective-permute-done((bf16[160,128]{1,0:T(8,128)(2,1)S(1)}, bf16[160,128]{1,0:T(8,128)(2,1)S(1)}, u32[]{:S(2)}, u32[]{:S(2)}) %collective-permute-start.4) | collective-permute-done | bytes 40992 | tf_op jit(solution)/shard_map/ppermute | solution.py:489
  17.7 1.3 %shard_map.91 = (f32[128,128]{1,0:T(8,128)S(1)}, bf16[128,128]{1,0:T(8,128)(2,1)S(1)}, bf16[128,128]{1,0:T(8,128)(2,1)S(1)}, bf16[128,128]{1,0:T(8,128)(2,1)S(1)}) custom-call(f32[9,128,128]{2,1,0:T(8,128)S(1)} %get-tuple-element.37.taps_ref, bf16[27,512,128]{2,1,0:T(8,128)(2,1)S(1)} %get-tuple-element.34.refs_4_.w_ref, ...), custom_call_target="tpu_custom_call" | custom-call | flops 452984832 | bytes 4456448 | tf_op jit(solution)/shard_map/pallas_call | solution.py:33
  19.0 0.1 collective-permute-start.10
  19.1 1.6 %collective-permute-start.8 = (bf16[128,128]{1,0:T(8,128)(2,1)S(1)}, bf16[128,128]{1,0:T(8,128)(2,1)S(1)}, u32[]{:S(2)}, u32[]{:S(2)}) collective-permute-start(bf16[128,128]{1,0:T(8,128)(2,1)S(1)} %get-tuple-element.43), channel_id=1, source_target_pairs={{0,1},{1,0},{2,3},{3,2},{4,5},{5,4},{6,7},{7,6},{8,9},{9,8},{10,11... | collective-permute-start | bytes 98312 | tf_op jit(solution)/shard_map/ppermute | solution.py:489
  20.7 0.5 %collective-permute-start.9 = (bf16[128,128]{1,0:T(8,128)(2,1)S(1)}, bf16[128,128]{1,0:T(8,128)(2,1)S(1)}, u32[]{:S(2)}, u32[]{:S(2)}) collective-permute-start(bf16[128,128]{1,0:T(8,128)(2,1)S(1)} %get-tuple-element.44), channel_id=1, source_target_pairs={{0,2},{1,3},{2,0},{3,1},{4,6},{5,7},{6,4},{7,5},{8,10},{9,11},{10,... | collective-permute-start | bytes 98312 | tf_op jit(solution)/shard_map/ppermute | solution.py:489
  21.2 0.7 %shard_map.89 = (f32[128,128]{1,0:T(8,128)S(1)}, f32[128,128]{1,0:T(8,128)S(1)}, f32[2,128]{1,0:T(2,128)S(1)}, bf16[80,128]{1,0:T(8,128)(2,1)S(1)}) custom-call(bf16[160,128]{1,0:T(8,128)(2,1)S(1)} %get-tuple-element.28.refs_0_, bf16[160,128]{1,0:T(8,128)(2,1)S(1)} %collective-permute-done.2.refs_1_, bf16[160,128]{1,0:T(8,128)(2,1)S(1)} %collective-permute-done.3.refs_2_, ...), custom_call_target="tpu_custom_call" | custom-call | flops 25165824 | bytes 514048 | tf_op jit(solution)/shard_map/pallas_call | solution.py:33
  21.9 0.1 collective-permute-start.5
  22.0 1.6 %collective-permute-start.6 = (bf16[80,128]{1,0:T(8,128)(2,1)S(1)}, bf16[80,128]{1,0:T(8,128)(2,1)S(1)}, u32[]{:S(2)}, u32[]{:S(2)}) collective-permute-start(bf16[80,128]{1,0:T(8,128)(2,1)S(1)} %get-tuple-element.33.refs_0_), channel_id=1, source_target_pairs={{0,2},{1,3},{2,0},{3,1},{4,6},{5,7},{6,4},{7,5},{8,10},{9,11},{10,... | collective-permute-start | bytes 61448 | tf_op jit(solution)/shard_map/ppermute | solution.py:489
  23.6 0.0 collective-permute-done.10.refs_7_
  23.6 0.3 collective-permute-start.7
  23.8 0.0 collective-permute-done.8.refs_5_
  23.8 0.8 %collective-permute-done.9.refs_6_ = bf16[128,128]{1,0:T(8,128)(2,1)S(1)} collective-permute-done((bf16[128,128]{1,0:T(8,128)(2,1)S(1)}, bf16[128,128]{1,0:T(8,128)(2,1)S(1)}, u32[]{:S(2)}, u32[]{:S(2)}) %collective-permute-start.9) | collective-permute-done | bytes 32800 | tf_op jit(solution)/shard_map/ppermute | solution.py:489
  24.6 0.4 %shard_map.92 = (bf16[32,128]{1,0:T(8,128)(2,1)S(1)}, bf16[32,128]{1,0:T(8,128)(2,1)S(1)}, bf16[32,128]{1,0:T(8,128)(2,1)S(1)}, bf16[32,128]{1,0:T(8,128)(2,1)S(1)}) custom-call(f32[128,128]{1,0:T(8,128)S(1)} %get-tuple-element.38.refs_0_, f32[128,128]{1,0:T(8,128)S(1)} %get-tuple-element.39.refs_1_, f32[128,128]{1,0:T(8,128)S(1)} %get-tuple-element.40.refs_2_, ...), custom_call_target="tpu_custom_call" | custom-call | bytes 361472 | tf_op jit(solution)/shard_map/pallas_call | solution.py:33
  25.0 0.1 collective-permute-start.11
  25.1 1.0 %collective-permute-start.12 = (bf16[32,128]{1,0:T(8,128)(2,1)S(1)}, bf16[32,128]{1,0:T(8,128)(2,1)S(1)}, u32[]{:S(2)}, u32[]{:S(2)}) collective-permute-start(bf16[32,128]{1,0:T(8,128)(2,1)S(1)} %get-tuple-element.48), channel_id=1, source_target_pairs={{0,16},{4,20},{8,24},{12,28},{16,0},{20,4},{24,8},{28,12},{1,17},{... | collective-permute-start | bytes 24584 | tf_op jit(solution)/shard_map/ppermute | solution.py:489
  26.1 0.0 collective-permute-done.5.refs_1_
  26.1 3.4 %collective-permute-start.13 = (bf16[32,128]{1,0:T(8,128)(2,1)S(1)}, bf16[32,128]{1,0:T(8,128)(2,1)S(1)}, u32[]{:S(2)}, u32[]{:S(2)}) collective-permute-start(bf16[32,128]{1,0:T(8,128)(2,1)S(1)} %get-tuple-element.49), channel_id=1, source_target_pairs={{0,24},{4,28},{8,16},{12,20},{16,8},{20,12},{24,0},{28,4},{1,25},{... | collective-permute-start | bytes 24584 | tf_op jit(solution)/shard_map/ppermute | solution.py:489
  29.4 0.0 collective-permute-done.6.refs_2_
  29.4 0.0 collective-permute-done.7.refs_3_
  29.5 1.5 %shard_map.90 = bf16[256,128]{1,0:T(8,128)(2,1)} custom-call(bf16[80,128]{1,0:T(8,128)(2,1)S(1)} %get-tuple-element.33.refs_0_, bf16[80,128]{1,0:T(8,128)(2,1)S(1)} %collective-permute-done.5.refs_1_, bf16[80,128]{1,0:T(8,128)(2,1)S(1)} %collective-permute-done.6.refs_2_, bf16[80,128]{1,0:T(8,128)(2,1)S(1)} %collective-permute-done.7.refs_3_, ...), custom_call_target="tpu_custom_call" | custom-call | flops 283115520 | bytes 3686912 | tf_op jit(solution)/shard_map/pallas_call | solution.py:33
  30.9 0.0 collective-permute-done.11.refs_1_
  30.9 0.0 collective-permute-done.12.refs_2_
  30.9 0.6 %collective-permute-done.13.refs_3_ = bf16[32,128]{1,0:T(8,128)(2,1)S(1)} collective-permute-done((bf16[32,128]{1,0:T(8,128)(2,1)S(1)}, bf16[32,128]{1,0:T(8,128)(2,1)S(1)}, u32[]{:S(2)}, u32[]{:S(2)}) %collective-permute-start.13) | collective-permute-done | bytes 8224 | tf_op jit(solution)/shard_map/ppermute | solution.py:489
  31.5 0.7 %shard_map.93 = bf16[64,128]{1,0:T(8,128)(2,1)} custom-call(bf16[64,128]{1,0:T(8,128)(2,1)S(1)} %get-tuple-element.36.put_ref, bf16[32,128]{1,0:T(8,128)(2,1)S(1)} %get-tuple-element.46.refs_0_, bf16[32,128]{1,0:T(8,128)(2,1)S(1)} %collective-permute-done.11.refs_1_, bf16[32,128]{1,0:T(8,128)(2,1)S(1)} %collective-permute-done.12.refs_2_, ...), custom_call_target="tpu_custom_call" | custom-call | bytes 65536 | tf_op jit(solution)/shard_map/pallas_call | solution.py:33
  (1 shorter events, 0.0 us)
Async XLA Ops:
  0.6 7.0 %collective-permute-start.1 = (bf16[256,128]{1,0:T(8,128)(2,1)}, bf16[256,128]{1,0:T(8,128)(2,1)S(1)}, u32[]{:S(2)}, u32[]{:S(2)}) collective-permute-start(bf16[256,128]{1,0:T(8,128)(2,1)} %bitcast.6), channel_id=1, source_target_pairs={{0,4},{4,0},{8,12},{12,8},{16,20},{20,16},{24,28},{28,24},{1,5},{5... | collective-permute-start | bytes 196616 | tf_op jit(solution)/shard_map/ppermute | solution.py:489
  3.6 3.9 %collective-permute-start = (bf16[64,128]{1,0:T(8,128)(2,1)}, bf16[64,128]{1,0:T(8,128)(2,1)S(1)}, u32[]{:S(2)}, u32[]{:S(2)}) collective-permute-start(bf16[64,128]{1,0:T(8,128)(2,1)} %tokens_ref.1), channel_id=1, source_target_pairs={{0,4},{4,0},{8,12},{12,8},{16,20},{20,16},{24,28},{28,24},{1,5},{5... | collective-permute-start | bytes 49160 | tf_op jit(solution)/shard_map/ppermute | solution.py:489
  7.6 6.5 %collective-permute-start.2 = (bf16[160,128]{1,0:T(8,128)(2,1)S(1)}, bf16[160,128]{1,0:T(8,128)(2,1)S(1)}, u32[]{:S(2)}, u32[]{:S(2)}) collective-permute-start(bf16[160,128]{1,0:T(8,128)(2,1)S(1)} %get-tuple-element.28.refs_0_), channel_id=1, source_target_pairs={{0,8},{4,12},{8,0},{12,4},{16,24},{20,28},{24,16},{28,20},{1,9},{5... | collective-permute-start | bytes 122888 | tf_op jit(solution)/shard_map/ppermute | solution.py:489
  9.3 5.8 %collective-permute-start.3 = (bf16[160,128]{1,0:T(8,128)(2,1)S(1)}, bf16[160,128]{1,0:T(8,128)(2,1)S(1)}, u32[]{:S(2)}, u32[]{:S(2)}) collective-permute-start(bf16[160,128]{1,0:T(8,128)(2,1)S(1)} %get-tuple-element.28.refs_0_), channel_id=1, source_target_pairs={{0,16},{4,20},{8,24},{12,28},{16,0},{20,4},{24,8},{28,12},{1,17},{... | collective-permute-start | bytes 122888 | tf_op jit(solution)/shard_map/ppermute | solution.py:489
  11.9 5.8 %collective-permute-start.4 = (bf16[160,128]{1,0:T(8,128)(2,1)S(1)}, bf16[160,128]{1,0:T(8,128)(2,1)S(1)}, u32[]{:S(2)}, u32[]{:S(2)}) collective-permute-start(bf16[160,128]{1,0:T(8,128)(2,1)S(1)} %get-tuple-element.28.refs_0_), channel_id=1, source_target_pairs={{0,24},{4,28},{8,16},{12,20},{16,8},{20,12},{24,0},{28,4},{1,25},{... | collective-permute-start | bytes 122888 | tf_op jit(solution)/shard_map/ppermute | solution.py:489
  19.0 4.6 %collective-permute-start.10 = (bf16[128,128]{1,0:T(8,128)(2,1)S(1)}, bf16[128,128]{1,0:T(8,128)(2,1)S(1)}, u32[]{:S(2)}, u32[]{:S(2)}) collective-permute-start(bf16[128,128]{1,0:T(8,128)(2,1)S(1)} %get-tuple-element.45), channel_id=1, source_target_pairs={{0,3},{1,2},{2,1},{3,0},{4,7},{5,6},{6,5},{7,4},{8,11},{9,10},{10,... | collective-permute-start | bytes 98312 | tf_op jit(solution)/shard_map/ppermute | solution.py:489
  19.1 4.8 %collective-permute-start.8 = (bf16[128,128]{1,0:T(8,128)(2,1)S(1)}, bf16[128,128]{1,0:T(8,128)(2,1)S(1)}, u32[]{:S(2)}, u32[]{:S(2)}) collective-permute-start(bf16[128,128]{1,0:T(8,128)(2,1)S(1)} %get-tuple-element.43), channel_id=1, source_target_pairs={{0,1},{1,0},{2,3},{3,2},{4,5},{5,4},{6,7},{7,6},{8,9},{9,8},{10,11... | collective-permute-start | bytes 98312 | tf_op jit(solution)/shard_map/ppermute | solution.py:489
  20.7 3.9 %collective-permute-start.9 = (bf16[128,128]{1,0:T(8,128)(2,1)S(1)}, bf16[128,128]{1,0:T(8,128)(2,1)S(1)}, u32[]{:S(2)}, u32[]{:S(2)}) collective-permute-start(bf16[128,128]{1,0:T(8,128)(2,1)S(1)} %get-tuple-element.44), channel_id=1, source_target_pairs={{0,2},{1,3},{2,0},{3,1},{4,6},{5,7},{6,4},{7,5},{8,10},{9,11},{10,... | collective-permute-start | bytes 98312 | tf_op jit(solution)/shard_map/ppermute | solution.py:489
  21.9 4.2 %collective-permute-start.5 = (bf16[80,128]{1,0:T(8,128)(2,1)S(1)}, bf16[80,128]{1,0:T(8,128)(2,1)S(1)}, u32[]{:S(2)}, u32[]{:S(2)}) collective-permute-start(bf16[80,128]{1,0:T(8,128)(2,1)S(1)} %get-tuple-element.33.refs_0_), channel_id=1, source_target_pairs={{0,1},{1,0},{2,3},{3,2},{4,5},{5,4},{6,7},{7,6},{8,9},{9,8},{10,11... | collective-permute-start | bytes 61448 | tf_op jit(solution)/shard_map/ppermute | solution.py:489
  22.0 7.5 %collective-permute-start.6 = (bf16[80,128]{1,0:T(8,128)(2,1)S(1)}, bf16[80,128]{1,0:T(8,128)(2,1)S(1)}, u32[]{:S(2)}, u32[]{:S(2)}) collective-permute-start(bf16[80,128]{1,0:T(8,128)(2,1)S(1)} %get-tuple-element.33.refs_0_), channel_id=1, source_target_pairs={{0,2},{1,3},{2,0},{3,1},{4,6},{5,7},{6,4},{7,5},{8,10},{9,11},{10,... | collective-permute-start | bytes 61448 | tf_op jit(solution)/shard_map/ppermute | solution.py:489
  23.6 5.9 %collective-permute-start.7 = (bf16[80,128]{1,0:T(8,128)(2,1)S(1)}, bf16[80,128]{1,0:T(8,128)(2,1)S(1)}, u32[]{:S(2)}, u32[]{:S(2)}) collective-permute-start(bf16[80,128]{1,0:T(8,128)(2,1)S(1)} %get-tuple-element.33.refs_0_), channel_id=1, source_target_pairs={{0,3},{1,2},{2,1},{3,0},{4,7},{5,6},{6,5},{7,4},{8,11},{9,10},{10,... | collective-permute-start | bytes 61448 | tf_op jit(solution)/shard_map/ppermute | solution.py:489
  25.0 5.9 %collective-permute-start.11 = (bf16[32,128]{1,0:T(8,128)(2,1)S(1)}, bf16[32,128]{1,0:T(8,128)(2,1)S(1)}, u32[]{:S(2)}, u32[]{:S(2)}) collective-permute-start(bf16[32,128]{1,0:T(8,128)(2,1)S(1)} %get-tuple-element.47), channel_id=1, source_target_pairs={{0,8},{4,12},{8,0},{12,4},{16,24},{20,28},{24,16},{28,20},{1,9},{5... | collective-permute-start | bytes 24584 | tf_op jit(solution)/shard_map/ppermute | solution.py:489
  25.1 5.9 %collective-permute-start.12 = (bf16[32,128]{1,0:T(8,128)(2,1)S(1)}, bf16[32,128]{1,0:T(8,128)(2,1)S(1)}, u32[]{:S(2)}, u32[]{:S(2)}) collective-permute-start(bf16[32,128]{1,0:T(8,128)(2,1)S(1)} %get-tuple-element.48), channel_id=1, source_target_pairs={{0,16},{4,20},{8,24},{12,28},{16,0},{20,4},{24,8},{28,12},{1,17},{... | collective-permute-start | bytes 24584 | tf_op jit(solution)/shard_map/ppermute | solution.py:489
  26.1 5.4 %collective-permute-start.13 = (bf16[32,128]{1,0:T(8,128)(2,1)S(1)}, bf16[32,128]{1,0:T(8,128)(2,1)S(1)}, u32[]{:S(2)}, u32[]{:S(2)}) collective-permute-start(bf16[32,128]{1,0:T(8,128)(2,1)S(1)} %get-tuple-element.49), channel_id=1, source_target_pairs={{0,24},{4,28},{8,16},{12,20},{16,8},{20,12},{24,0},{28,4},{1,25},{... | collective-permute-start | bytes 24584 | tf_op jit(solution)/shard_map/ppermute | solution.py:489

commit v5 on v4

--- a/solution.py
+++ b/solution.py
@@ -319,7 +319,7 @@
     grid_ref[...] = space[...].astype(F32)
 
 
-def join_kernel(own_ref, peer_ref, grid_ref, lines_ref, out_ref, pair_ref):
+def join_kernel(own_ref, peer_ref, grid_ref, lines_ref, after_ref, out_ref, pair_ref):
     own, area = own_ref.shape[0], grid_ref.shape[0]
     odd = lax.axis_index("tile") % 2
     wide = 2 * TILE_W
@@ -456,14 +456,10 @@
     grid_ref[...] = space[...].astype(F32)
 
 
-def pair_prep_kernel(own, capacity, pair_ref, *refs):
-    ins, (take_ref, pack_ref, put_ref, taps_ref, *outs), (source_ref, sems) = refs[:5], refs[5:-2], refs[-2:]
+def pair_prep_kernel(own, capacity, *refs):
+    ins, (take_ref, pack_ref, put_ref, *outs) = refs[:5], refs[5:-2]
+    source_ref, sems = refs[-2:]
     copies = load_all(ins, [source_ref] + outs, sems)
-    wide = 2 * TILE_W
-    zero = jnp.zeros((ROWS, pair_ref.shape[1]), F32)
-    columns = folded_columns(pair_ref, wide, 2 * wide, lambda p: zero, lambda p: zero)
-    for tap, value in enumerate(fold_taps(columns)):
-        taps_ref[tap] = value
     copies[0].wait()
     tile = lax.axis_index("tile")
     z, x = tile // 2, tile % 2
@@ -485,6 +481,14 @@
         copy.wait()
 
 
+def pair_fold_kernel(pair_ref, taps_ref):
+    wide = 2 * TILE_W
+    zero = jnp.zeros((ROWS, pair_ref.shape[1]), F32)
+    columns = folded_columns(pair_ref, wide, 2 * wide, lambda p: zero, lambda p: zero)
+    for tap, value in enumerate(fold_taps(columns)):
+        taps_ref[tap] = value
+
+
 def swapped(block, axis, k):
     return lax.ppermute(block, axis, [(i, i ^ k) for i in range(lax.axis_size(axis))])
 
@@ -512,26 +516,26 @@
         [pltpu.VMEM((area, lanes), BF16), pltpu.SemaphoreType.DMA((2,))],
         loose=(0, 1),
     )
-    block, pair = call(
-        join_kernel,
-        [shape(2 * own + 4 * ROWS, lanes), shape(2 * area, lanes, F32)],
-        [kept, peer, grid, other],
-    )
-    pieces = [block] + [swapped(block, "tile", k) for k in (2, 4, 6)]
     ins = [cell_source, weight] + [v.reshape(1, lanes) for v in (gain, shift, bias)]
-    take, pack, put, taps, weight, gain, shift, bias = call(
+    take, pack, put, weight, gain, shift, bias = call(
         functools.partial(pair_prep_kernel, own, capacity),
         [
             shape(3 * CELLS, members * own),
             shape(slots, 2 * CELLS),
             shape(own, slots),
-            jax.ShapeDtypeStruct((9, 2 * CELLS, lanes), F32),
         ]
         + [jax.ShapeDtypeStruct(v.shape, v.dtype) for v in ins[1:]],
-        [pair] + ins,
+        ins,
         [pltpu.VMEM(cell_source.shape, jnp.int32), pltpu.SemaphoreType.DMA((len(ins),))],
-        loose=range(1, 6),
-    )
+        loose=range(5),
+    )
+    block, pair = call(
+        join_kernel,
+        [shape(2 * own + 4 * ROWS, lanes), shape(2 * area, lanes, F32)],
+        [kept, peer, grid, other, put],
+    )
+    pieces = [block] + [swapped(block, "tile", k) for k in (2, 4, 6)]
+    (taps,) = call(pair_fold_kernel, [jax.ShapeDtypeStruct((9, 2 * CELLS, lanes), F32)], [pair])
     cell = shape(2 * CELLS, lanes, F32)
     mine, *sends = call(
         pair_adjoint_kernel,

time: 32.5 us -> 31.5 us (0.969)
  waiting for transfers between devices: 7.84 us -> 6.83 us
    ppermute x14, waiting for transfers between devices: 7.84 us -> 6.83 us  [swapped(): lax.ppermute(block, axis, [(i, i ^ k) for i in range(lax.axis_size(axis))])]
    pallas_call x8 -> x9, Pallas kernels: 7.58 us -> 7.79 us  [call(): pl.pallas_call(kernel, out_shape=outs, in_specs=[FAR if i in loose else V...]
  transfers between devices with their start and end apart: 14 -> 14, of which waited for: 5 -> 5; matrix products, arithmetic and copies ran while one was open for 0% -> 0% of each run, Pallas kernels for 17% -> 18%
where the time goes in v5:
time: 31.5 us; the launch traced here: 31.3 us
  starting transfers between devices  16 us (51%)
  Pallas kernels  7.79 us (25%)
  waiting for transfers between devices  6.83 us (22%)
  between operations  0.71 us (2%)
    ppermute x14, starting transfers between devices, swapped(): lax.ppermute(block, axis, [(i, i ^ k) for i in range(lax.axis_size(axis))])  16 us
    pallas_call x9, Pallas kernels, call(): pl.pallas_call(kernel, out_shape=outs, in_specs=[FAR if i in loose else V...  7.79 us
    ppermute x14, waiting for transfers between devices, swapped(): lax.ppermute(block, axis, [(i, i ^ k) for i in range(lax.axis_size(axis))])  6.83 us
  transfers between devices with their start and end apart: 14, of which 5 were waited for; matrix products, arithmetic and copies ran while one was open for 0% of the time, Pallas kernels for 18%

profile of v5, /device:TPU:0, one launch (start us, length us, event | category | flops | bytes accessed | tf_op | source)
XLA Modules:
  0.0 31.3 jit_solution(1875323458301991093)
XLA Ops:
  0.6 3.0 %collective-permute-start.1 = (bf16[256,128]{1,0:T(8,128)(2,1)}, bf16[256,128]{1,0:T(8,128)(2,1)S(1)}, u32[]{:S(2)}, u32[]{:S(2)}) collective-permute-start(bf16[256,128]{1,0:T(8,128)(2,1)} %bitcast.6), channel_id=1, source_target_pairs={{0,4},{4,0},{8,12},{12,8},{16,20},{20,16},{24,28},{28,24},{1,5},{5... | collective-permute-start | bytes 196616 | tf_op jit(solution)/shard_map/ppermute | solution.py:493
  3.6 0.1 collective-permute-start
  3.7 0.9 %shard_map.86 = (bf16[64,128]{1,0:T(8,128)(2,1)S(1)}, f32[256,128]{1,0:T(8,128)S(1)}) custom-call(bf16[64,128]{1,0:T(8,128)(2,1)} %tokens_ref.1, bf16[256,128]{1,0:T(8,128)(2,1)} %bitcast.7), custom_call_target="tpu_custom_call" | custom-call | bytes 229376 | tf_op jit(solution)/shard_map/pallas_call | solution.py:33
  4.6 2.1 %shard_map.87 = (bf16[192,512]{1,0:T(8,128)(2,1)S(1)}, bf16[128,128]{1,0:T(8,128)(2,1)S(1)}, bf16[64,128]{1,0:T(8,128)(2,1)S(1)}, bf16[27,512,128]{2,1,0:T(8,128...) custom-call(s32[8,64]{1,0:T(8,128)} %refs_0_.1, bf16[27,512,128]{2,1,0:T(8,128)(2,1)} %refs_1_.1, ...), custom_call_target="tpu_custom_call" | custom-call | bytes 7328768 | tf_op jit(solution)/shard_map/pallas_call | solution.py:33
  6.7 0.9 %collective-permute-done.peer_ref = bf16[64,128]{1,0:T(8,128)(2,1)S(1)} collective-permute-done((bf16[64,128]{1,0:T(8,128)(2,1)}, bf16[64,128]{1,0:T(8,128)(2,1)S(1)}, u32[]{:S(2)}, u32[]{:S(2)}) %collective-permute-start) | collective-permute-done | bytes 16416 | tf_op jit(solution)/shard_map/ppermute | solution.py:493
  7.6 0.0 collective-permute-done.1.lines_ref
  7.6 3.7 %collective-permute-start.4 = (bf16[160,128]{1,0:T(8,128)(2,1)S(1)}, bf16[160,128]{1,0:T(8,128)(2,1)S(1)}, u32[]{:S(2)}, u32[]{:S(2)}) collective-permute-start(bf16[160,128]{1,0:T(8,128)(2,1)S(1)} %get-tuple-element.28.refs_0_), channel_id=1, source_target_pairs={{0,24},{4,28},{8,16},{12,20},{16,8},{20,12},{24,0},{28,4},{1,25},{... | collective-permute-start | bytes 122888 | tf_op jit(solution)/shard_map/ppermute | solution.py:493
  11.3 0.0 collective-permute-start.3
  11.3 0.8 %collective-permute-start.2 = (bf16[160,128]{1,0:T(8,128)(2,1)S(1)}, bf16[160,128]{1,0:T(8,128)(2,1)S(1)}, u32[]{:S(2)}, u32[]{:S(2)}) collective-permute-start(bf16[160,128]{1,0:T(8,128)(2,1)S(1)} %get-tuple-element.28.refs_0_), channel_id=1, source_target_pairs={{0,8},{4,12},{8,0},{12,4},{16,24},{20,28},{24,16},{28,20},{1,9},{5... | collective-permute-start | bytes 122888 | tf_op jit(solution)/shard_map/ppermute | solution.py:493
  12.1 0.2 shard_map.91.taps_ref
  12.3 1.2 %collective-permute-done.4.refs_3_ = bf16[160,128]{1,0:T(8,128)(2,1)S(1)} collective-permute-done((bf16[160,128]{1,0:T(8,128)(2,1)S(1)}, bf16[160,128]{1,0:T(8,128)(2,1)S(1)}, u32[]{:S(2)}, u32[]{:S(2)}) %collective-permute-start.4) | collective-permute-done | bytes 40992 | tf_op jit(solution)/shard_map/ppermute | solution.py:493
  13.5 2.7 %collective-permute-done.3.refs_2_ = bf16[160,128]{1,0:T(8,128)(2,1)S(1)} collective-permute-done((bf16[160,128]{1,0:T(8,128)(2,1)S(1)}, bf16[160,128]{1,0:T(8,128)(2,1)S(1)}, u32[]{:S(2)}, u32[]{:S(2)}) %collective-permute-start.3) | collective-permute-done | bytes 40992 | tf_op jit(solution)/shard_map/ppermute | solution.py:493
  16.2 0.0 collective-permute-done.2.refs_1_
  16.2 1.3 %shard_map.92 = (f32[128,128]{1,0:T(8,128)S(1)}, bf16[128,128]{1,0:T(8,128)(2,1)S(1)}, bf16[128,128]{1,0:T(8,128)(2,1)S(1)}, bf16[128,128]{1,0:T(8,128)(2,1)S(1)}) custom-call(f32[9,128,128]{2,1,0:T(8,128)S(1)} %shard_map.91.taps_ref, bf16[27,512,128]{2,1,0:T(8,128)(2,1)S(1)} %get-tuple-element.33.refs_4_.w_ref, ...), custom_call_target="tpu_custom_call" | custom-call | flops 452984832 | bytes 4456448 | tf_op jit(solution)/shard_map/pallas_call | solution.py:33
  17.5 0.1 collective-permute-start.8
  17.6 1.6 %collective-permute-start.9 = (bf16[128,128]{1,0:T(8,128)(2,1)S(1)}, bf16[128,128]{1,0:T(8,128)(2,1)S(1)}, u32[]{:S(2)}, u32[]{:S(2)}) collective-permute-start(bf16[128,128]{1,0:T(8,128)(2,1)S(1)} %get-tuple-element.42), channel_id=1, source_target_pairs={{0,2},{1,3},{2,0},{3,1},{4,6},{5,7},{6,4},{7,5},{8,10},{9,11},{10,... | collective-permute-start | bytes 98312 | tf_op jit(solution)/shard_map/ppermute | solution.py:493
  19.2 0.3 collective-permute-start.10
  19.5 0.7 %shard_map.89 = (f32[128,128]{1,0:T(8,128)S(1)}, f32[128,128]{1,0:T(8,128)S(1)}, f32[2,128]{1,0:T(2,128)S(1)}, bf16[80,128]{1,0:T(8,128)(2,1)S(1)}) custom-call(bf16[160,128]{1,0:T(8,128)(2,1)S(1)} %get-tuple-element.28.refs_0_, bf16[160,128]{1,0:T(8,128)(2,1)S(1)} %collective-permute-done.2.refs_1_, bf16[160,128]{1,0:T(8,128)(2,1)S(1)} %collective-permute-done.3.refs_2_, ...), custom_call_target="tpu_custom_call" | custom-call | flops 25165824 | bytes 514048 | tf_op jit(solution)/shard_map/pallas_call | solution.py:33
  20.2 1.5 %collective-permute-start.7 = (bf16[80,128]{1,0:T(8,128)(2,1)S(1)}, bf16[80,128]{1,0:T(8,128)(2,1)S(1)}, u32[]{:S(2)}, u32[]{:S(2)}) collective-permute-start(bf16[80,128]{1,0:T(8,128)(2,1)S(1)} %get-tuple-element.32.refs_0_), channel_id=1, source_target_pairs={{0,3},{1,2},{2,1},{3,0},{4,7},{5,6},{6,5},{7,4},{8,11},{9,10},{10,... | collective-permute-start | bytes 61448 | tf_op jit(solution)/shard_map/ppermute | solution.py:493
  21.7 0.5 %collective-permute-start.6 = (bf16[80,128]{1,0:T(8,128)(2,1)S(1)}, bf16[80,128]{1,0:T(8,128)(2,1)S(1)}, u32[]{:S(2)}, u32[]{:S(2)}) collective-permute-start(bf16[80,128]{1,0:T(8,128)(2,1)S(1)} %get-tuple-element.32.refs_0_), channel_id=1, source_target_pairs={{0,2},{1,3},{2,0},{3,1},{4,6},{5,7},{6,4},{7,5},{8,10},{9,11},{10,... | collective-permute-start | bytes 61448 | tf_op jit(solution)/shard_map/ppermute | solution.py:493
  22.2 0.0 collective-permute-done.8.refs_5_
  22.2 0.0 collective-permute-start.5
  22.2 0.0 collective-permute-done.9.refs_6_
  22.2 0.3 %collective-permute-done.10.refs_7_ = bf16[128,128]{1,0:T(8,128)(2,1)S(1)} collective-permute-done((bf16[128,128]{1,0:T(8,128)(2,1)S(1)}, bf16[128,128]{1,0:T(8,128)(2,1)S(1)}, u32[]{:S(2)}, u32[]{:S(2)}) %collective-permute-start.10) | collective-permute-done | bytes 32800 | tf_op jit(solution)/shard_map/ppermute | solution.py:493
  22.6 0.4 %shard_map.93 = (bf16[32,128]{1,0:T(8,128)(2,1)S(1)}, bf16[32,128]{1,0:T(8,128)(2,1)S(1)}, bf16[32,128]{1,0:T(8,128)(2,1)S(1)}, bf16[32,128]{1,0:T(8,128)(2,1)S(1)}) custom-call(f32[128,128]{1,0:T(8,128)S(1)} %get-tuple-element.36.refs_0_, f32[128,128]{1,0:T(8,128)S(1)} %get-tuple-element.37.refs_1_, f32[128,128]{1,0:T(8,128)S(1)} %get-tuple-element.38.refs_2_, ...), custom_call_target="tpu_custom_call" | custom-call | bytes 361472 | tf_op jit(solution)/shard_map/pallas_call | solution.py:33
  22.9 0.1 collective-permute-start.11
  23.0 2.1 %collective-permute-start.12 = (bf16[32,128]{1,0:T(8,128)(2,1)S(1)}, bf16[32,128]{1,0:T(8,128)(2,1)S(1)}, u32[]{:S(2)}, u32[]{:S(2)}) collective-permute-start(bf16[32,128]{1,0:T(8,128)(2,1)S(1)} %get-tuple-element.46), channel_id=1, source_target_pairs={{0,16},{4,20},{8,24},{12,28},{16,0},{20,4},{24,8},{28,12},{1,17},{... | collective-permute-start | bytes 24584 | tf_op jit(solution)/shard_map/ppermute | solution.py:493
  25.1 0.0 collective-permute-done.7.refs_3_
  25.1 2.3 %collective-permute-start.13 = (bf16[32,128]{1,0:T(8,128)(2,1)S(1)}, bf16[32,128]{1,0:T(8,128)(2,1)S(1)}, u32[]{:S(2)}, u32[]{:S(2)}) collective-permute-start(bf16[32,128]{1,0:T(8,128)(2,1)S(1)} %get-tuple-element.47), channel_id=1, source_target_pairs={{0,24},{4,28},{8,16},{12,20},{16,8},{20,12},{24,0},{28,4},{1,25},{... | collective-permute-start | bytes 24584 | tf_op jit(solution)/shard_map/ppermute | solution.py:493
  27.4 0.0 collective-permute-done.6.refs_2_
  27.4 0.0 collective-permute-done.5.refs_1_
  27.4 1.5 %shard_map.90 = bf16[256,128]{1,0:T(8,128)(2,1)} custom-call(bf16[80,128]{1,0:T(8,128)(2,1)S(1)} %get-tuple-element.32.refs_0_, bf16[80,128]{1,0:T(8,128)(2,1)S(1)} %collective-permute-done.5.refs_1_, bf16[80,128]{1,0:T(8,128)(2,1)S(1)} %collective-permute-done.6.refs_2_, bf16[80,128]{1,0:T(8,128)(2,1)S(1)} %collective-permute-done.7.refs_3_, ...), custom_call_target="tpu_custom_call" | custom-call | flops 283115520 | bytes 3686912 | tf_op jit(solution)/shard_map/pallas_call | solution.py:33
  28.9 0.0 collective-permute-done.11.refs_1_
  28.9 0.0 collective-permute-done.12.refs_2_
  28.9 1.7 %collective-permute-done.13.refs_3_ = bf16[32,128]{1,0:T(8,128)(2,1)S(1)} collective-permute-done((bf16[32,128]{1,0:T(8,128)(2,1)S(1)}, bf16[32,128]{1,0:T(8,128)(2,1)S(1)}, u32[]{:S(2)}, u32[]{:S(2)}) %collective-permute-start.13) | collective-permute-done | bytes 8224 | tf_op jit(solution)/shard_map/ppermute | solution.py:493
  30.5 0.7 %shard_map.94 = bf16[64,128]{1,0:T(8,128)(2,1)} custom-call(bf16[64,128]{1,0:T(8,128)(2,1)S(1)} %get-tuple-element.27.after_ref.put_ref, bf16[32,128]{1,0:T(8,128)(2,1)S(1)} %get-tuple-element.44.refs_0_, bf16[32,128]{1,0:T(8,128)(2,1)S(1)} %collective-permute-done.11.refs_1_, bf16[32,128]{1,0:T(8,128)(2,1)S(1)} %collective-permute-done.12.refs_2_, ...), custom_call_target="tpu_custom_call" | custom-call | bytes 65536 | tf_op jit(solution)/shard_map/pallas_call | solution.py:33
  (1 shorter events, 0.0 us)
Async XLA Ops:
  0.6 7.0 %collective-permute-start.1 = (bf16[256,128]{1,0:T(8,128)(2,1)}, bf16[256,128]{1,0:T(8,128)(2,1)S(1)}, u32[]{:S(2)}, u32[]{:S(2)}) collective-permute-start(bf16[256,128]{1,0:T(8,128)(2,1)} %bitcast.6), channel_id=1, source_target_pairs={{0,4},{4,0},{8,12},{12,8},{16,20},{20,16},{24,28},{28,24},{1,5},{5... | collective-permute-start | bytes 196616 | tf_op jit(solution)/shard_map/ppermute | solution.py:493
  3.6 3.9 %collective-permute-start = (bf16[64,128]{1,0:T(8,128)(2,1)}, bf16[64,128]{1,0:T(8,128)(2,1)S(1)}, u32[]{:S(2)}, u32[]{:S(2)}) collective-permute-start(bf16[64,128]{1,0:T(8,128)(2,1)} %tokens_ref.1), channel_id=1, source_target_pairs={{0,4},{4,0},{8,12},{12,8},{16,20},{20,16},{24,28},{28,24},{1,5},{5... | collective-permute-start | bytes 49160 | tf_op jit(solution)/shard_map/ppermute | solution.py:493
  7.6 5.9 %collective-permute-start.4 = (bf16[160,128]{1,0:T(8,128)(2,1)S(1)}, bf16[160,128]{1,0:T(8,128)(2,1)S(1)}, u32[]{:S(2)}, u32[]{:S(2)}) collective-permute-start(bf16[160,128]{1,0:T(8,128)(2,1)S(1)} %get-tuple-element.28.refs_0_), channel_id=1, source_target_pairs={{0,24},{4,28},{8,16},{12,20},{16,8},{20,12},{24,0},{28,4},{1,25},{... | collective-permute-start | bytes 122888 | tf_op jit(solution)/shard_map/ppermute | solution.py:493
  11.3 4.9 %collective-permute-start.3 = (bf16[160,128]{1,0:T(8,128)(2,1)S(1)}, bf16[160,128]{1,0:T(8,128)(2,1)S(1)}, u32[]{:S(2)}, u32[]{:S(2)}) collective-permute-start(bf16[160,128]{1,0:T(8,128)(2,1)S(1)} %get-tuple-element.28.refs_0_), channel_id=1, source_target_pairs={{0,16},{4,20},{8,24},{12,28},{16,0},{20,4},{24,8},{28,12},{1,17},{... | collective-permute-start | bytes 122888 | tf_op jit(solution)/shard_map/ppermute | solution.py:493
  11.3 4.9 %collective-permute-start.2 = (bf16[160,128]{1,0:T(8,128)(2,1)S(1)}, bf16[160,128]{1,0:T(8,128)(2,1)S(1)}, u32[]{:S(2)}, u32[]{:S(2)}) collective-permute-start(bf16[160,128]{1,0:T(8,128)(2,1)S(1)} %get-tuple-element.28.refs_0_), channel_id=1, source_target_pairs={{0,8},{4,12},{8,0},{12,4},{16,24},{20,28},{24,16},{28,20},{1,9},{5... | collective-permute-start | bytes 122888 | tf_op jit(solution)/shard_map/ppermute | solution.py:493
  17.5 4.7 %collective-permute-start.8 = (bf16[128,128]{1,0:T(8,128)(2,1)S(1)}, bf16[128,128]{1,0:T(8,128)(2,1)S(1)}, u32[]{:S(2)}, u32[]{:S(2)}) collective-permute-start(bf16[128,128]{1,0:T(8,128)(2,1)S(1)} %get-tuple-element.41), channel_id=1, source_target_pairs={{0,1},{1,0},{2,3},{3,2},{4,5},{5,4},{6,7},{7,6},{8,9},{9,8},{10,11... | collective-permute-start | bytes 98312 | tf_op jit(solution)/shard_map/ppermute | solution.py:493
  17.6 4.6 %collective-permute-start.9 = (bf16[128,128]{1,0:T(8,128)(2,1)S(1)}, bf16[128,128]{1,0:T(8,128)(2,1)S(1)}, u32[]{:S(2)}, u32[]{:S(2)}) collective-permute-start(bf16[128,128]{1,0:T(8,128)(2,1)S(1)} %get-tuple-element.42), channel_id=1, source_target_pairs={{0,2},{1,3},{2,0},{3,1},{4,6},{5,7},{6,4},{7,5},{8,10},{9,11},{10,... | collective-permute-start | bytes 98312 | tf_op jit(solution)/shard_map/ppermute | solution.py:493
  19.2 3.3 %collective-permute-start.10 = (bf16[128,128]{1,0:T(8,128)(2,1)S(1)}, bf16[128,128]{1,0:T(8,128)(2,1)S(1)}, u32[]{:S(2)}, u32[]{:S(2)}) collective-permute-start(bf16[128,128]{1,0:T(8,128)(2,1)S(1)} %get-tuple-element.43), channel_id=1, source_target_pairs={{0,3},{1,2},{2,1},{3,0},{4,7},{5,6},{6,5},{7,4},{8,11},{9,10},{10,... | collective-permute-start | bytes 98312 | tf_op jit(solution)/shard_map/ppermute | solution.py:493
  20.2 4.9 %collective-permute-start.7 = (bf16[80,128]{1,0:T(8,128)(2,1)S(1)}, bf16[80,128]{1,0:T(8,128)(2,1)S(1)}, u32[]{:S(2)}, u32[]{:S(2)}) collective-permute-start(bf16[80,128]{1,0:T(8,128)(2,1)S(1)} %get-tuple-element.32.refs_0_), channel_id=1, source_target_pairs={{0,3},{1,2},{2,1},{3,0},{4,7},{5,6},{6,5},{7,4},{8,11},{9,10},{10,... | collective-permute-start | bytes 61448 | tf_op jit(solution)/shard_map/ppermute | solution.py:493
  21.7 5.7 %collective-permute-start.6 = (bf16[80,128]{1,0:T(8,128)(2,1)S(1)}, bf16[80,128]{1,0:T(8,128)(2,1)S(1)}, u32[]{:S(2)}, u32[]{:S(2)}) collective-permute-start(bf16[80,128]{1,0:T(8,128)(2,1)S(1)} %get-tuple-element.32.refs_0_), channel_id=1, source_target_pairs={{0,2},{1,3},{2,0},{3,1},{4,6},{5,7},{6,4},{7,5},{8,10},{9,11},{10,... | collective-permute-start | bytes 61448 | tf_op jit(solution)/shard_map/ppermute | solution.py:493
  22.2 5.2 %collective-permute-start.5 = (bf16[80,128]{1,0:T(8,128)(2,1)S(1)}, bf16[80,128]{1,0:T(8,128)(2,1)S(1)}, u32[]{:S(2)}, u32[]{:S(2)}) collective-permute-start(bf16[80,128]{1,0:T(8,128)(2,1)S(1)} %get-tuple-element.32.refs_0_), channel_id=1, source_target_pairs={{0,1},{1,0},{2,3},{3,2},{4,5},{5,4},{6,7},{7,6},{8,9},{9,8},{10,11... | collective-permute-start | bytes 61448 | tf_op jit(solution)/shard_map/ppermute | solution.py:493
  22.9 5.9 %collective-permute-start.11 = (bf16[32,128]{1,0:T(8,128)(2,1)S(1)}, bf16[32,128]{1,0:T(8,128)(2,1)S(1)}, u32[]{:S(2)}, u32[]{:S(2)}) collective-permute-start(bf16[32,128]{1,0:T(8,128)(2,1)S(1)} %get-tuple-element.45), channel_id=1, source_target_pairs={{0,8},{4,12},{8,0},{12,4},{16,24},{20,28},{24,16},{28,20},{1,9},{5... | collective-permute-start | bytes 24584 | tf_op jit(solution)/shard_map/ppermute | solution.py:493
  23.0 5.9 %collective-permute-start.12 = (bf16[32,128]{1,0:T(8,128)(2,1)S(1)}, bf16[32,128]{1,0:T(8,128)(2,1)S(1)}, u32[]{:S(2)}, u32[]{:S(2)}) collective-permute-start(bf16[32,128]{1,0:T(8,128)(2,1)S(1)} %get-tuple-element.46), channel_id=1, source_target_pairs={{0,16},{4,20},{8,24},{12,28},{16,0},{20,4},{24,8},{28,12},{1,17},{... | collective-permute-start | bytes 24584 | tf_op jit(solution)/shard_map/ppermute | solution.py:493
  25.1 5.4 %collective-permute-start.13 = (bf16[32,128]{1,0:T(8,128)(2,1)S(1)}, bf16[32,128]{1,0:T(8,128)(2,1)S(1)}, u32[]{:S(2)}, u32[]{:S(2)}) collective-permute-start(bf16[32,128]{1,0:T(8,128)(2,1)S(1)} %get-tuple-element.47), channel_id=1, source_target_pairs={{0,24},{4,28},{8,16},{12,20},{16,8},{20,12},{24,0},{28,4},{1,25},{... | collective-permute-start | bytes 24584 | tf_op jit(solution)/shard_map/ppermute | solution.py:493

commit v6 on v5

--- a/solution.py
+++ b/solution.py
@@ -16,6 +16,7 @@
 ROWS = FRAMES * TILE_H
 EPS = 1e-06
 VMEM_LIMIT = 12 * 2**20
+SPLIT = 240
 F32 = jnp.float32
 BF16 = jnp.bfloat16
 VMEM = pl.BlockSpec(memory_space=pltpu.VMEM)
@@ -309,28 +310,35 @@
         copy.wait()
 
 
-def early_kernel(tokens_ref, lines_ref, own_ref, grid_ref, space, sems):
+def early_kernel(tokens_ref, lines_ref, out_ref, *refs):
+    parts, (grid_ref, space, sems) = refs[:-3], refs[-3:]
+    own = tokens_ref.shape[0]
     fetch(
         [
-            pltpu.make_async_copy(tokens_ref, own_ref, sems.at[0]),
+            pltpu.make_async_copy(tokens_ref, out_ref.at[pl.ds(0, own)], sems.at[0]),
             pltpu.make_async_copy(lines_ref, space, sems.at[1]),
         ]
     )
+    size = parts[0].shape[0]
+    parts[0][...] = space[:size]
+    out_ref[own + 2 * ROWS :] = space[size:]
     grid_ref[...] = space[...].astype(F32)
-
-
-def join_kernel(own_ref, peer_ref, grid_ref, lines_ref, after_ref, out_ref, pair_ref):
-    own, area = own_ref.shape[0], grid_ref.shape[0]
-    odd = lax.axis_index("tile") % 2
     wide = 2 * TILE_W
-    out_ref[pl.ds(pl.multiple_of(odd * own, own), own), :] = own_ref[...]
-    out_ref[pl.ds(pl.multiple_of((1 - odd) * own, own), own), :] = peer_ref[...]
-    pair_ref[pl.ds(pl.multiple_of(odd * area, area), area), :] = grid_ref[...]
-    pair_ref[pl.ds(pl.multiple_of((1 - odd) * area, area), area), :] = lines_ref[...].astype(F32)
-    left = pair_ref[pl.ds(0, 2 * ROWS, stride=wide), :]
-    right = pair_ref[pl.ds(area + wide - 1, 2 * ROWS, stride=wide), :]
-    out_ref[2 * own : 2 * own + 2 * ROWS] = left.astype(BF16)
-    out_ref[2 * own + 2 * ROWS :] = right.astype(BF16)
+    first = grid_ref[pl.ds(0, 2 * ROWS, stride=wide), :]
+    last = grid_ref[pl.ds(wide - 1, 2 * ROWS, stride=wide), :]
+    odd = lax.axis_index("tile") % 2 == 1
+    out_ref[own : own + 2 * ROWS] = jnp.where(odd, last, first).astype(BF16)
+
+
+def join_kernel(mine_ref, peer_ref, after_ref, out_ref):
+    own = (out_ref.shape[0] - 4 * ROWS) // 2
+    odd = lax.axis_index("tile") % 2 == 1
+    mine, peer = mine_ref[...], peer_ref[...]
+    even_one, odd_one = jnp.where(odd, peer, mine), jnp.where(odd, mine, peer)
+    out_ref[:own] = even_one[:own]
+    out_ref[own : 2 * own] = odd_one[:own]
+    out_ref[2 * own : 2 * own + 2 * ROWS] = even_one[own : own + 2 * ROWS]
+    out_ref[2 * own + 2 * ROWS :] = odd_one[own : own + 2 * ROWS]
 
 
 def conv_kernel(multi, *refs):
@@ -481,8 +489,18 @@
         copy.wait()
 
 
-def pair_fold_kernel(pair_ref, taps_ref):
+def pair_fold_kernel(*refs):
+    taps_ref, pair_ref = refs[-2:]
+    mine, theirs = refs[:2], refs[2:4]
+    area = pair_ref.shape[0] // 2
+    size = mine[0].shape[0]
     wide = 2 * TILE_W
+    right = lax.axis_index("tile") % 2
+    for at, (head, tail) in ((right, mine), (1 - right, theirs)):
+        begin = pl.multiple_of(at * area, area)
+        pair_ref[pl.ds(begin, size), :] = head[...].astype(F32)
+        begin = pl.multiple_of(at * area + size, 16)
+        pair_ref[pl.ds(begin, area - size), :] = tail[size - area :].astype(F32)
     zero = jnp.zeros((ROWS, pair_ref.shape[1]), F32)
     columns = folded_columns(pair_ref, wide, 2 * wide, lambda p: zero, lambda p: zero)
     for tap, value in enumerate(fold_taps(columns)):
@@ -507,15 +525,19 @@
     capacity = max(2, own // (members // 2))
     slots = members * capacity
     area = lines.shape[0]
-    peer = swapped(tokens, "tile", 1)
-    other = swapped(lines, "tile", 1)
-    kept, grid = call(
+    early, *parts = call(
         early_kernel,
-        [shape(own, lanes), shape(area, lanes, F32)],
+        [shape(own + 2 * ROWS + area - SPLIT, lanes), shape(SPLIT, lanes)],
         [tokens, lines],
-        [pltpu.VMEM((area, lanes), BF16), pltpu.SemaphoreType.DMA((2,))],
+        [
+            pltpu.VMEM((area, lanes), F32),
+            pltpu.VMEM((area, lanes), BF16),
+            pltpu.SemaphoreType.DMA((2,)),
+        ],
         loose=(0, 1),
     )
+    peer = swapped(early, "tile", 1)
+    others = [swapped(part, "tile", 1) for part in parts]
     ins = [cell_source, weight] + [v.reshape(1, lanes) for v in (gain, shift, bias)]
     take, pack, put, weight, gain, shift, bias = call(
         functools.partial(pair_prep_kernel, own, capacity),
@@ -529,13 +551,14 @@
         [pltpu.VMEM(cell_source.shape, jnp.int32), pltpu.SemaphoreType.DMA((len(ins),))],
         loose=range(5),
     )
-    block, pair = call(
-        join_kernel,
-        [shape(2 * own + 4 * ROWS, lanes), shape(2 * area, lanes, F32)],
-        [kept, peer, grid, other, put],
-    )
+    (block,) = call(join_kernel, [shape(2 * own + 4 * ROWS, lanes)], [early, peer, put])
     pieces = [block] + [swapped(block, "tile", k) for k in (2, 4, 6)]
-    (taps,) = call(pair_fold_kernel, [jax.ShapeDtypeStruct((9, 2 * CELLS, lanes), F32)], [pair])
+    (taps,) = call(
+        pair_fold_kernel,
+        [jax.ShapeDtypeStruct((9, 2 * CELLS, lanes), F32)],
+        parts + [early] + others + [peer],
+        [pltpu.VMEM((2 * area, lanes), F32)],
+    )
     cell = shape(2 * CELLS, lanes, F32)
     mine, *sends = call(
         pair_adjoint_kernel,

time: 31.5 us -> 31.1 us (0.987)
  waiting for transfers between devices: 6.83 us -> 6.02 us
    ppermute x14, waiting for transfers between devices: 6.83 us -> 6.02 us  [swapped(): lax.ppermute(block, axis, [(i, i ^ k) for i in range(lax.axis_size(axis))])]
  transfers between devices with their start and end apart: 14 -> 14, of which waited for: 5 -> 4; matrix products, arithmetic and copies ran while one was open for 0% -> 0% of each run, Pallas kernels for 18% -> 16%
where the time goes in v6:
time: 31.1 us; the launch traced here: 30.8 us
  starting transfers between devices  16.3 us (52%)
  Pallas kernels  7.83 us (25%)
  waiting for transfers between devices  6.02 us (19%)
  between operations  0.72 us (2%)
    ppermute x14, starting transfers between devices, swapped(): lax.ppermute(block, axis, [(i, i ^ k) for i in range(lax.axis_size(axis))])  16.3 us
    pallas_call x9, Pallas kernels, call(): pl.pallas_call(kernel, out_shape=outs, in_specs=[FAR if i in loose else V...  7.83 us
    ppermute x14, waiting for transfers between devices, swapped(): lax.ppermute(block, axis, [(i, i ^ k) for i in range(lax.axis_size(axis))])  6.02 us
  transfers between devices with their start and end apart: 14, of which 4 were waited for; matrix products, arithmetic and copies ran while one was open for 0% of the time, Pallas kernels for 16%

profile of v6, /device:TPU:0, one launch (start us, length us, event | category | flops | bytes accessed | tf_op | source)
XLA Modules:
  0.0 30.8 jit_solution(16388200005189764956)
XLA Ops:
  0.6 0.9 %shard_map.86 = (bf16[96,128]{1,0:T(8,128)(2,1)S(1)}, bf16[240,128]{1,0:T(8,128)(2,1)S(1)}) custom-call(bf16[64,128]{1,0:T(8,128)(2,1)} %tokens_ref.1, bf16[256,128]{1,0:T(8,128)(2,1)} %bitcast.6), custom_call_target="tpu_custom_call" | custom-call | bytes 167936 | tf_op jit(solution)/shard_map/pallas_call | solution.py:34
  1.5 3.0 %collective-permute-start = (bf16[96,128]{1,0:T(8,128)(2,1)S(1)}, bf16[96,128]{1,0:T(8,128)(2,1)S(1)}, u32[]{:S(2)}, u32[]{:S(2)}) collective-permute-start(bf16[96,128]{1,0:T(8,128)(2,1)S(1)} %get-tuple-element.23.mine_ref.refs_1_), channel_id=1, source_target_pairs={{0,4},{4,0},{8,12},{12,8},{16,20},{20,16},{24,28},{28,24},{1,5},{5... | collective-permute-start | bytes 73736 | tf_op jit(solution)/shard_map/ppermute | solution.py:511
  4.5 0.1 collective-permute-start.7
  4.6 2.1 %shard_map.87 = (bf16[192,512]{1,0:T(8,128)(2,1)S(1)}, bf16[128,128]{1,0:T(8,128)(2,1)S(1)}, bf16[64,128]{1,0:T(8,128)(2,1)S(1)}, bf16[27,512,128]{2,1,0:T(8,128...) custom-call(s32[8,64]{1,0:T(8,128)} %refs_0_.1, bf16[27,512,128]{2,1,0:T(8,128)(2,1)} %refs_1_.1, ...), custom_call_target="tpu_custom_call" | custom-call | bytes 7328768 | tf_op jit(solution)/shard_map/pallas_call | solution.py:34
  6.7 0.0 collective-permute-done.peer_ref.refs_3_
  6.7 4.1 %collective-permute-start.3 = (bf16[160,128]{1,0:T(8,128)(2,1)S(1)}, bf16[160,128]{1,0:T(8,128)(2,1)S(1)}, u32[]{:S(2)}, u32[]{:S(2)}) collective-permute-start(bf16[160,128]{1,0:T(8,128)(2,1)S(1)} %shard_map.88.refs_0_), channel_id=1, source_target_pairs={{0,24},{4,28},{8,16},{12,20},{16,8},{20,12},{24,0},{28,4},{1,25},{... | collective-permute-start | bytes 122888 | tf_op jit(solution)/shard_map/ppermute | solution.py:511
  10.9 0.0 collective-permute-start.2
  10.9 0.6 %collective-permute-start.1 = (bf16[160,128]{1,0:T(8,128)(2,1)S(1)}, bf16[160,128]{1,0:T(8,128)(2,1)S(1)}, u32[]{:S(2)}, u32[]{:S(2)}) collective-permute-start(bf16[160,128]{1,0:T(8,128)(2,1)S(1)} %shard_map.88.refs_0_), channel_id=1, source_target_pairs={{0,8},{4,12},{8,0},{12,4},{16,24},{20,28},{24,16},{28,20},{1,9},{5... | collective-permute-start | bytes 122888 | tf_op jit(solution)/shard_map/ppermute | solution.py:511
  11.5 0.0 collective-permute-done.7.refs_2_
  11.5 0.3 shard_map.91.taps_ref
  11.8 1.5 %collective-permute-done.3.refs_3_ = bf16[160,128]{1,0:T(8,128)(2,1)S(1)} collective-permute-done((bf16[160,128]{1,0:T(8,128)(2,1)S(1)}, bf16[160,128]{1,0:T(8,128)(2,1)S(1)}, u32[]{:S(2)}, u32[]{:S(2)}) %collective-permute-start.3) | collective-permute-done | bytes 40992 | tf_op jit(solution)/shard_map/ppermute | solution.py:511
  13.3 2.5 %collective-permute-done.2.refs_2_ = bf16[160,128]{1,0:T(8,128)(2,1)S(1)} collective-permute-done((bf16[160,128]{1,0:T(8,128)(2,1)S(1)}, bf16[160,128]{1,0:T(8,128)(2,1)S(1)}, u32[]{:S(2)}, u32[]{:S(2)}) %collective-permute-start.2) | collective-permute-done | bytes 40992 | tf_op jit(solution)/shard_map/ppermute | solution.py:511
  15.8 0.0 collective-permute-done.1.refs_1_
  15.8 1.3 %shard_map.92 = (f32[128,128]{1,0:T(8,128)S(1)}, bf16[128,128]{1,0:T(8,128)(2,1)S(1)}, bf16[128,128]{1,0:T(8,128)(2,1)S(1)}, bf16[128,128]{1,0:T(8,128)(2,1)S(1)}) custom-call(f32[9,128,128]{2,1,0:T(8,128)S(1)} %shard_map.91.taps_ref, bf16[27,512,128]{2,1,0:T(8,128)(2,1)S(1)} %get-tuple-element.29.refs_4_.w_ref, bf16[160,128]{1,0:T(8,128)(2,1)S(1)} %shard_map.88.refs_0_, ...), custom_call_target="tpu_custom_call" | custom-call | flops 452984832 | bytes 4456448 | tf_op jit(solution)/shard_map/pallas_call | solution.py:34
  17.1 0.1 collective-permute-start.8
  17.2 1.6 %collective-permute-start.9 = (bf16[128,128]{1,0:T(8,128)(2,1)S(1)}, bf16[128,128]{1,0:T(8,128)(2,1)S(1)}, u32[]{:S(2)}, u32[]{:S(2)}) collective-permute-start(bf16[128,128]{1,0:T(8,128)(2,1)S(1)} %get-tuple-element.38), channel_id=1, source_target_pairs={{0,2},{1,3},{2,0},{3,1},{4,6},{5,7},{6,4},{7,5},{8,10},{9,11},{10,... | collective-permute-start | bytes 98312 | tf_op jit(solution)/shard_map/ppermute | solution.py:511
  18.8 0.3 collective-permute-start.10
  19.0 0.7 %shard_map.89 = (f32[128,128]{1,0:T(8,128)S(1)}, f32[128,128]{1,0:T(8,128)S(1)}, f32[2,128]{1,0:T(2,128)S(1)}, bf16[80,128]{1,0:T(8,128)(2,1)S(1)}) custom-call(bf16[160,128]{1,0:T(8,128)(2,1)S(1)} %shard_map.88.refs_0_, bf16[160,128]{1,0:T(8,128)(2,1)S(1)} %collective-permute-done.1.refs_1_, bf16[160,128]{1,0:T(8,128)(2,1)S(1)} %collective-permute-done.2.refs_2_, ...), custom_call_target="tpu_custom_call" | custom-call | flops 25165824 | bytes 514048 | tf_op jit(solution)/shard_map/pallas_call | solution.py:34
  19.7 1.5 %collective-permute-start.6 = (bf16[80,128]{1,0:T(8,128)(2,1)S(1)}, bf16[80,128]{1,0:T(8,128)(2,1)S(1)}, u32[]{:S(2)}, u32[]{:S(2)}) collective-permute-start(bf16[80,128]{1,0:T(8,128)(2,1)S(1)} %get-tuple-element.28.refs_0_), channel_id=1, source_target_pairs={{0,3},{1,2},{2,1},{3,0},{4,7},{5,6},{6,5},{7,4},{8,11},{9,10},{10,... | collective-permute-start | bytes 61448 | tf_op jit(solution)/shard_map/ppermute | solution.py:511
  21.3 0.5 %collective-permute-start.5 = (bf16[80,128]{1,0:T(8,128)(2,1)S(1)}, bf16[80,128]{1,0:T(8,128)(2,1)S(1)}, u32[]{:S(2)}, u32[]{:S(2)}) collective-permute-start(bf16[80,128]{1,0:T(8,128)(2,1)S(1)} %get-tuple-element.28.refs_0_), channel_id=1, source_target_pairs={{0,2},{1,3},{2,0},{3,1},{4,6},{5,7},{6,4},{7,5},{8,10},{9,11},{10,... | collective-permute-start | bytes 61448 | tf_op jit(solution)/shard_map/ppermute | solution.py:511
  21.8 0.0 collective-permute-done.8.refs_5_
  21.8 0.0 collective-permute-start.4
  21.8 0.0 collective-permute-done.9.refs_6_
  21.8 0.3 %collective-permute-done.10.refs_7_ = bf16[128,128]{1,0:T(8,128)(2,1)S(1)} collective-permute-done((bf16[128,128]{1,0:T(8,128)(2,1)S(1)}, bf16[128,128]{1,0:T(8,128)(2,1)S(1)}, u32[]{:S(2)}, u32[]{:S(2)}) %collective-permute-start.10) | collective-permute-done | bytes 32800 | tf_op jit(solution)/shard_map/ppermute | solution.py:511
  22.1 0.4 %shard_map.93 = (bf16[32,128]{1,0:T(8,128)(2,1)S(1)}, bf16[32,128]{1,0:T(8,128)(2,1)S(1)}, bf16[32,128]{1,0:T(8,128)(2,1)S(1)}, bf16[32,128]{1,0:T(8,128)(2,1)S(1)}) custom-call(f32[128,128]{1,0:T(8,128)S(1)} %get-tuple-element.32.refs_0_, f32[128,128]{1,0:T(8,128)S(1)} %get-tuple-element.33.refs_1_, f32[128,128]{1,0:T(8,128)S(1)} %get-tuple-element.34.refs_2_, ...), custom_call_target="tpu_custom_call" | custom-call | bytes 361472 | tf_op jit(solution)/shard_map/pallas_call | solution.py:34
  22.5 0.1 collective-permute-start.11
  22.6 2.1 %collective-permute-start.12 = (bf16[32,128]{1,0:T(8,128)(2,1)S(1)}, bf16[32,128]{1,0:T(8,128)(2,1)S(1)}, u32[]{:S(2)}, u32[]{:S(2)}) collective-permute-start(bf16[32,128]{1,0:T(8,128)(2,1)S(1)} %get-tuple-element.42), channel_id=1, source_target_pairs={{0,16},{4,20},{8,24},{12,28},{16,0},{20,4},{24,8},{28,12},{1,17},{... | collective-permute-start | bytes 24584 | tf_op jit(solution)/shard_map/ppermute | solution.py:511
  24.7 0.0 collective-permute-done.6.refs_3_
  24.7 2.3 %collective-permute-start.13 = (bf16[32,128]{1,0:T(8,128)(2,1)S(1)}, bf16[32,128]{1,0:T(8,128)(2,1)S(1)}, u32[]{:S(2)}, u32[]{:S(2)}) collective-permute-start(bf16[32,128]{1,0:T(8,128)(2,1)S(1)} %get-tuple-element.43), channel_id=1, source_target_pairs={{0,24},{4,28},{8,16},{12,20},{16,8},{20,12},{24,0},{28,4},{1,25},{... | collective-permute-start | bytes 24584 | tf_op jit(solution)/shard_map/ppermute | solution.py:511
  26.9 0.0 collective-permute-done.5.refs_2_
  26.9 0.0 collective-permute-done.4.refs_1_
  26.9 1.5 %shard_map.90 = bf16[256,128]{1,0:T(8,128)(2,1)} custom-call(bf16[80,128]{1,0:T(8,128)(2,1)S(1)} %get-tuple-element.28.refs_0_, bf16[80,128]{1,0:T(8,128)(2,1)S(1)} %collective-permute-done.4.refs_1_, bf16[80,128]{1,0:T(8,128)(2,1)S(1)} %collective-permute-done.5.refs_2_, bf16[80,128]{1,0:T(8,128)(2,1)S(1)} %collective-permute-done.6.refs_3_, ...), custom_call_target="tpu_custom_call" | custom-call | flops 283115520 | bytes 3686912 | tf_op jit(solution)/shard_map/pallas_call | solution.py:34
  28.4 0.0 collective-permute-done.11.refs_1_
  28.4 0.0 collective-permute-done.12.refs_2_
  28.4 1.7 %collective-permute-done.13.refs_3_ = bf16[32,128]{1,0:T(8,128)(2,1)S(1)} collective-permute-done((bf16[32,128]{1,0:T(8,128)(2,1)S(1)}, bf16[32,128]{1,0:T(8,128)(2,1)S(1)}, u32[]{:S(2)}, u32[]{:S(2)}) %collective-permute-start.13) | collective-permute-done | bytes 8224 | tf_op jit(solution)/shard_map/ppermute | solution.py:511
  30.1 0.7 %shard_map.94 = bf16[64,128]{1,0:T(8,128)(2,1)} custom-call(bf16[64,128]{1,0:T(8,128)(2,1)S(1)} %get-tuple-element.24.after_ref.put_ref, bf16[32,128]{1,0:T(8,128)(2,1)S(1)} %get-tuple-element.40.refs_0_, bf16[32,128]{1,0:T(8,128)(2,1)S(1)} %collective-permute-done.11.refs_1_, bf16[32,128]{1,0:T(8,128)(2,1)S(1)} %collective-permute-done.12.refs_2_, ...), custom_call_target="tpu_custom_call" | custom-call | bytes 65536 | tf_op jit(solution)/shard_map/pallas_call | solution.py:34
  (1 shorter events, 0.0 us)
Async XLA Ops:
  1.5 5.2 %collective-permute-start = (bf16[96,128]{1,0:T(8,128)(2,1)S(1)}, bf16[96,128]{1,0:T(8,128)(2,1)S(1)}, u32[]{:S(2)}, u32[]{:S(2)}) collective-permute-start(bf16[96,128]{1,0:T(8,128)(2,1)S(1)} %get-tuple-element.23.mine_ref.refs_1_), channel_id=1, source_target_pairs={{0,4},{4,0},{8,12},{12,8},{16,20},{20,16},{24,28},{28,24},{1,5},{5... | collective-permute-start | bytes 73736 | tf_op jit(solution)/shard_map/ppermute | solution.py:511
  4.5 7.0 %collective-permute-start.7 = (bf16[240,128]{1,0:T(8,128)(2,1)S(1)}, bf16[240,128]{1,0:T(8,128)(2,1)S(1)}, u32[]{:S(2)}, u32[]{:S(2)}) collective-permute-start(bf16[240,128]{1,0:T(8,128)(2,1)S(1)} %get-tuple-element.31.refs_0_), channel_id=1, source_target_pairs={{0,4},{4,0},{8,12},{12,8},{16,20},{20,16},{24,28},{28,24},{1,5},{5... | collective-permute-start | bytes 184328 | tf_op jit(solution)/shard_map/ppermute | solution.py:511
  6.7 6.6 %collective-permute-start.3 = (bf16[160,128]{1,0:T(8,128)(2,1)S(1)}, bf16[160,128]{1,0:T(8,128)(2,1)S(1)}, u32[]{:S(2)}, u32[]{:S(2)}) collective-permute-start(bf16[160,128]{1,0:T(8,128)(2,1)S(1)} %shard_map.88.refs_0_), channel_id=1, source_target_pairs={{0,24},{4,28},{8,16},{12,20},{16,8},{20,12},{24,0},{28,4},{1,25},{... | collective-permute-start | bytes 122888 | tf_op jit(solution)/shard_map/ppermute | solution.py:511
  10.9 4.9 %collective-permute-start.2 = (bf16[160,128]{1,0:T(8,128)(2,1)S(1)}, bf16[160,128]{1,0:T(8,128)(2,1)S(1)}, u32[]{:S(2)}, u32[]{:S(2)}) collective-permute-start(bf16[160,128]{1,0:T(8,128)(2,1)S(1)} %shard_map.88.refs_0_), channel_id=1, source_target_pairs={{0,16},{4,20},{8,24},{12,28},{16,0},{20,4},{24,8},{28,12},{1,17},{... | collective-permute-start | bytes 122888 | tf_op jit(solution)/shard_map/ppermute | solution.py:511
  10.9 4.9 %collective-permute-start.1 = (bf16[160,128]{1,0:T(8,128)(2,1)S(1)}, bf16[160,128]{1,0:T(8,128)(2,1)S(1)}, u32[]{:S(2)}, u32[]{:S(2)}) collective-permute-start(bf16[160,128]{1,0:T(8,128)(2,1)S(1)} %shard_map.88.refs_0_), channel_id=1, source_target_pairs={{0,8},{4,12},{8,0},{12,4},{16,24},{20,28},{24,16},{28,20},{1,9},{5... | collective-permute-start | bytes 122888 | tf_op jit(solution)/shard_map/ppermute | solution.py:511
  17.1 4.7 %collective-permute-start.8 = (bf16[128,128]{1,0:T(8,128)(2,1)S(1)}, bf16[128,128]{1,0:T(8,128)(2,1)S(1)}, u32[]{:S(2)}, u32[]{:S(2)}) collective-permute-start(bf16[128,128]{1,0:T(8,128)(2,1)S(1)} %get-tuple-element.37), channel_id=1, source_target_pairs={{0,1},{1,0},{2,3},{3,2},{4,5},{5,4},{6,7},{7,6},{8,9},{9,8},{10,11... | collective-permute-start | bytes 98312 | tf_op jit(solution)/shard_map/ppermute | solution.py:511
  17.2 4.6 %collective-permute-start.9 = (bf16[128,128]{1,0:T(8,128)(2,1)S(1)}, bf16[128,128]{1,0:T(8,128)(2,1)S(1)}, u32[]{:S(2)}, u32[]{:S(2)}) collective-permute-start(bf16[128,128]{1,0:T(8,128)(2,1)S(1)} %get-tuple-element.38), channel_id=1, source_target_pairs={{0,2},{1,3},{2,0},{3,1},{4,6},{5,7},{6,4},{7,5},{8,10},{9,11},{10,... | collective-permute-start | bytes 98312 | tf_op jit(solution)/shard_map/ppermute | solution.py:511
  18.8 3.3 %collective-permute-start.10 = (bf16[128,128]{1,0:T(8,128)(2,1)S(1)}, bf16[128,128]{1,0:T(8,128)(2,1)S(1)}, u32[]{:S(2)}, u32[]{:S(2)}) collective-permute-start(bf16[128,128]{1,0:T(8,128)(2,1)S(1)} %get-tuple-element.39), channel_id=1, source_target_pairs={{0,3},{1,2},{2,1},{3,0},{4,7},{5,6},{6,5},{7,4},{8,11},{9,10},{10,... | collective-permute-start | bytes 98312 | tf_op jit(solution)/shard_map/ppermute | solution.py:511
  19.7 4.9 %collective-permute-start.6 = (bf16[80,128]{1,0:T(8,128)(2,1)S(1)}, bf16[80,128]{1,0:T(8,128)(2,1)S(1)}, u32[]{:S(2)}, u32[]{:S(2)}) collective-permute-start(bf16[80,128]{1,0:T(8,128)(2,1)S(1)} %get-tuple-element.28.refs_0_), channel_id=1, source_target_pairs={{0,3},{1,2},{2,1},{3,0},{4,7},{5,6},{6,5},{7,4},{8,11},{9,10},{10,... | collective-permute-start | bytes 61448 | tf_op jit(solution)/shard_map/ppermute | solution.py:511
  21.3 5.7 %collective-permute-start.5 = (bf16[80,128]{1,0:T(8,128)(2,1)S(1)}, bf16[80,128]{1,0:T(8,128)(2,1)S(1)}, u32[]{:S(2)}, u32[]{:S(2)}) collective-permute-start(bf16[80,128]{1,0:T(8,128)(2,1)S(1)} %get-tuple-element.28.refs_0_), channel_id=1, source_target_pairs={{0,2},{1,3},{2,0},{3,1},{4,6},{5,7},{6,4},{7,5},{8,10},{9,11},{10,... | collective-permute-start | bytes 61448 | tf_op jit(solution)/shard_map/ppermute | solution.py:511
  21.8 5.2 %collective-permute-start.4 = (bf16[80,128]{1,0:T(8,128)(2,1)S(1)}, bf16[80,128]{1,0:T(8,128)(2,1)S(1)}, u32[]{:S(2)}, u32[]{:S(2)}) collective-permute-start(bf16[80,128]{1,0:T(8,128)(2,1)S(1)} %get-tuple-element.28.refs_0_), channel_id=1, source_target_pairs={{0,1},{1,0},{2,3},{3,2},{4,5},{5,4},{6,7},{7,6},{8,9},{9,8},{10,11... | collective-permute-start | bytes 61448 | tf_op jit(solution)/shard_map/ppermute | solution.py:511
  22.5 5.9 %collective-permute-start.11 = (bf16[32,128]{1,0:T(8,128)(2,1)S(1)}, bf16[32,128]{1,0:T(8,128)(2,1)S(1)}, u32[]{:S(2)}, u32[]{:S(2)}) collective-permute-start(bf16[32,128]{1,0:T(8,128)(2,1)S(1)} %get-tuple-element.41), channel_id=1, source_target_pairs={{0,8},{4,12},{8,0},{12,4},{16,24},{20,28},{24,16},{28,20},{1,9},{5... | collective-permute-start | bytes 24584 | tf_op jit(solution)/shard_map/ppermute | solution.py:511
  22.6 5.9 %collective-permute-start.12 = (bf16[32,128]{1,0:T(8,128)(2,1)S(1)}, bf16[32,128]{1,0:T(8,128)(2,1)S(1)}, u32[]{:S(2)}, u32[]{:S(2)}) collective-permute-start(bf16[32,128]{1,0:T(8,128)(2,1)S(1)} %get-tuple-element.42), channel_id=1, source_target_pairs={{0,16},{4,20},{8,24},{12,28},{16,0},{20,4},{24,8},{28,12},{1,17},{... | collective-permute-start | bytes 24584 | tf_op jit(solution)/shard_map/ppermute | solution.py:511
  24.7 5.4 %collective-permute-start.13 = (bf16[32,128]{1,0:T(8,128)(2,1)S(1)}, bf16[32,128]{1,0:T(8,128)(2,1)S(1)}, u32[]{:S(2)}, u32[]{:S(2)}) collective-permute-start(bf16[32,128]{1,0:T(8,128)(2,1)S(1)} %get-tuple-element.43), channel_id=1, source_target_pairs={{0,24},{4,28},{8,16},{12,20},{16,8},{20,12},{24,0},{28,4},{1,25},{... | collective-permute-start | bytes 24584 | tf_op jit(solution)/shard_map/ppermute | solution.py:511

commit v7 on v6

--- a/solution.py
+++ b/solution.py
@@ -297,10 +297,9 @@
         result.append(scale_ref[i : i + 1] * value)
     result = (jnp.concatenate(result, axis=0) if tiles > 1 else result[0]).astype(BF16)
     packed = jnp.dot(pack_ref[...], result, preferred_element_type=F32).astype(BF16)
-    begin = 0
-    for out in outs:
-        out[...] = packed[begin : begin + out.shape[0]]
-        begin += out.shape[0]
+    step = packed.shape[0] // len(outs)
+    for k, out in enumerate(outs):
+        out[:step] = packed[k * step : (k + 1) * step]
 
 
 def fetch(copies):
@@ -401,7 +400,8 @@
 
 def place_kernel(put_ref, *refs):
     returned, out_ref = refs[:-1], refs[-1]
-    values = [r[...] for r in returned]
+    step = put_ref.shape[1] // len(returned)
+    values = [r[:step] for r in returned]
     values = jnp.concatenate(values, axis=0) if len(values) > 1 else values[0]
     placed = jnp.dot(put_ref[...], values, preferred_element_type=F32)
     out_ref[...] = placed.astype(BF16)
@@ -577,7 +577,7 @@
     received = chan_swaps([cells] * 3)
     routed = call(
         back_kernel,
-        [shape(2 * capacity, lanes)] * 4,
+        [shape(2 * capacity + more, lanes) for more in (0, 16, 32, 0)],
         [mine, hat, slope, scale, pack] + sends,
     )
     returned = [routed[0]] + [swapped(r, "tile", 2 * k + 2) for k, r in enumerate(routed[1:])]

time: 31.1 us -> 30.8 us (level)
  waiting for transfers between devices: 6.02 us -> 5.69 us
    ppermute x14, waiting for transfers between devices: 6.02 us -> 5.69 us  [swapped(): lax.ppermute(block, axis, [(i, i ^ k) for i in range(lax.axis_size(axis))])]
where the time goes in v7:
time: 30.8 us; the launch traced here: 30.5 us
  starting transfers between devices  16.3 us (53%)
  Pallas kernels  7.83 us (25%)
  waiting for transfers between devices  5.69 us (18%)
  between operations  0.71 us (2%)
    ppermute x14, starting transfers between devices, swapped(): lax.ppermute(block, axis, [(i, i ^ k) for i in range(lax.axis_size(axis))])  16.3 us
    pallas_call x9, Pallas kernels, call(): pl.pallas_call(kernel, out_shape=outs, in_specs=[FAR if i in loose else V...  7.83 us
    ppermute x14, waiting for transfers between devices, swapped(): lax.ppermute(block, axis, [(i, i ^ k) for i in range(lax.axis_size(axis))])  5.69 us
  transfers between devices with their start and end apart: 14, of which 4 were waited for; matrix products, arithmetic and copies ran while one was open for 0% of the time, Pallas kernels for 16%

profile of v7, /device:TPU:0, one launch (start us, length us, event | category | flops | bytes accessed | tf_op | source)
XLA Modules:
  0.0 30.5 jit_solution(18350786013427984085)
XLA Ops:
  0.6 0.9 %shard_map.86 = (bf16[96,128]{1,0:T(8,128)(2,1)S(1)}, bf16[240,128]{1,0:T(8,128)(2,1)S(1)}) custom-call(bf16[64,128]{1,0:T(8,128)(2,1)} %tokens_ref.1, bf16[256,128]{1,0:T(8,128)(2,1)} %bitcast.6), custom_call_target="tpu_custom_call" | custom-call | bytes 167936 | tf_op jit(solution)/shard_map/pallas_call | solution.py:34
  1.5 3.0 %collective-permute-start = (bf16[96,128]{1,0:T(8,128)(2,1)S(1)}, bf16[96,128]{1,0:T(8,128)(2,1)S(1)}, u32[]{:S(2)}, u32[]{:S(2)}) collective-permute-start(bf16[96,128]{1,0:T(8,128)(2,1)S(1)} %get-tuple-element.23.mine_ref.refs_1_), channel_id=1, source_target_pairs={{0,4},{4,0},{8,12},{12,8},{16,20},{20,16},{24,28},{28,24},{1,5},{5... | collective-permute-start | bytes 73736 | tf_op jit(solution)/shard_map/ppermute | solution.py:511
  4.5 0.1 collective-permute-start.7
  4.6 2.1 %shard_map.87 = (bf16[192,512]{1,0:T(8,128)(2,1)S(1)}, bf16[128,128]{1,0:T(8,128)(2,1)S(1)}, bf16[64,128]{1,0:T(8,128)(2,1)S(1)}, bf16[27,512,128]{2,1,0:T(8,128...) custom-call(s32[8,64]{1,0:T(8,128)} %refs_0_.1, bf16[27,512,128]{2,1,0:T(8,128)(2,1)} %refs_1_.1, ...), custom_call_target="tpu_custom_call" | custom-call | bytes 7328768 | tf_op jit(solution)/shard_map/pallas_call | solution.py:34
  6.7 0.0 collective-permute-done.peer_ref.refs_3_
  6.7 4.1 %collective-permute-start.3 = (bf16[160,128]{1,0:T(8,128)(2,1)S(1)}, bf16[160,128]{1,0:T(8,128)(2,1)S(1)}, u32[]{:S(2)}, u32[]{:S(2)}) collective-permute-start(bf16[160,128]{1,0:T(8,128)(2,1)S(1)} %shard_map.88.refs_0_), channel_id=1, source_target_pairs={{0,24},{4,28},{8,16},{12,20},{16,8},{20,12},{24,0},{28,4},{1,25},{... | collective-permute-start | bytes 122888 | tf_op jit(solution)/shard_map/ppermute | solution.py:511
  10.9 0.0 collective-permute-start.2
  10.9 0.6 %collective-permute-start.1 = (bf16[160,128]{1,0:T(8,128)(2,1)S(1)}, bf16[160,128]{1,0:T(8,128)(2,1)S(1)}, u32[]{:S(2)}, u32[]{:S(2)}) collective-permute-start(bf16[160,128]{1,0:T(8,128)(2,1)S(1)} %shard_map.88.refs_0_), channel_id=1, source_target_pairs={{0,8},{4,12},{8,0},{12,4},{16,24},{20,28},{24,16},{28,20},{1,9},{5... | collective-permute-start | bytes 122888 | tf_op jit(solution)/shard_map/ppermute | solution.py:511
  11.5 0.0 collective-permute-done.7.refs_2_
  11.5 0.3 shard_map.91.taps_ref
  11.8 1.5 %collective-permute-done.3.refs_3_ = bf16[160,128]{1,0:T(8,128)(2,1)S(1)} collective-permute-done((bf16[160,128]{1,0:T(8,128)(2,1)S(1)}, bf16[160,128]{1,0:T(8,128)(2,1)S(1)}, u32[]{:S(2)}, u32[]{:S(2)}) %collective-permute-start.3) | collective-permute-done | bytes 40992 | tf_op jit(solution)/shard_map/ppermute | solution.py:511
  13.3 2.5 %collective-permute-done.2.refs_2_ = bf16[160,128]{1,0:T(8,128)(2,1)S(1)} collective-permute-done((bf16[160,128]{1,0:T(8,128)(2,1)S(1)}, bf16[160,128]{1,0:T(8,128)(2,1)S(1)}, u32[]{:S(2)}, u32[]{:S(2)}) %collective-permute-start.2) | collective-permute-done | bytes 40992 | tf_op jit(solution)/shard_map/ppermute | solution.py:511
  15.8 0.0 collective-permute-done.1.refs_1_
  15.8 1.3 %shard_map.92 = (f32[128,128]{1,0:T(8,128)S(1)}, bf16[128,128]{1,0:T(8,128)(2,1)S(1)}, bf16[128,128]{1,0:T(8,128)(2,1)S(1)}, bf16[128,128]{1,0:T(8,128)(2,1)S(1)}) custom-call(f32[9,128,128]{2,1,0:T(8,128)S(1)} %shard_map.91.taps_ref, bf16[27,512,128]{2,1,0:T(8,128)(2,1)S(1)} %get-tuple-element.29.refs_4_.w_ref, bf16[160,128]{1,0:T(8,128)(2,1)S(1)} %shard_map.88.refs_0_, ...), custom_call_target="tpu_custom_call" | custom-call | flops 452984832 | bytes 4456448 | tf_op jit(solution)/shard_map/pallas_call | solution.py:34
  17.1 0.1 collective-permute-start.8
  17.2 1.6 %collective-permute-start.9 = (bf16[128,128]{1,0:T(8,128)(2,1)S(1)}, bf16[128,128]{1,0:T(8,128)(2,1)S(1)}, u32[]{:S(2)}, u32[]{:S(2)}) collective-permute-start(bf16[128,128]{1,0:T(8,128)(2,1)S(1)} %get-tuple-element.38), channel_id=1, source_target_pairs={{0,2},{1,3},{2,0},{3,1},{4,6},{5,7},{6,4},{7,5},{8,10},{9,11},{10,... | collective-permute-start | bytes 98312 | tf_op jit(solution)/shard_map/ppermute | solution.py:511
  18.8 0.3 collective-permute-start.10
  19.0 0.7 %shard_map.89 = (f32[128,128]{1,0:T(8,128)S(1)}, f32[128,128]{1,0:T(8,128)S(1)}, f32[2,128]{1,0:T(2,128)S(1)}, bf16[80,128]{1,0:T(8,128)(2,1)S(1)}) custom-call(bf16[160,128]{1,0:T(8,128)(2,1)S(1)} %shard_map.88.refs_0_, bf16[160,128]{1,0:T(8,128)(2,1)S(1)} %collective-permute-done.1.refs_1_, bf16[160,128]{1,0:T(8,128)(2,1)S(1)} %collective-permute-done.2.refs_2_, ...), custom_call_target="tpu_custom_call" | custom-call | flops 25165824 | bytes 514048 | tf_op jit(solution)/shard_map/pallas_call | solution.py:34
  19.7 1.5 %collective-permute-start.6 = (bf16[80,128]{1,0:T(8,128)(2,1)S(1)}, bf16[80,128]{1,0:T(8,128)(2,1)S(1)}, u32[]{:S(2)}, u32[]{:S(2)}) collective-permute-start(bf16[80,128]{1,0:T(8,128)(2,1)S(1)} %get-tuple-element.28.refs_0_), channel_id=1, source_target_pairs={{0,3},{1,2},{2,1},{3,0},{4,7},{5,6},{6,5},{7,4},{8,11},{9,10},{10,... | collective-permute-start | bytes 61448 | tf_op jit(solution)/shard_map/ppermute | solution.py:511
  21.3 0.5 %collective-permute-start.5 = (bf16[80,128]{1,0:T(8,128)(2,1)S(1)}, bf16[80,128]{1,0:T(8,128)(2,1)S(1)}, u32[]{:S(2)}, u32[]{:S(2)}) collective-permute-start(bf16[80,128]{1,0:T(8,128)(2,1)S(1)} %get-tuple-element.28.refs_0_), channel_id=1, source_target_pairs={{0,2},{1,3},{2,0},{3,1},{4,6},{5,7},{6,4},{7,5},{8,10},{9,11},{10,... | collective-permute-start | bytes 61448 | tf_op jit(solution)/shard_map/ppermute | solution.py:511
  21.8 0.0 collective-permute-done.8.refs_5_
  21.8 0.0 collective-permute-start.4
  21.8 0.0 collective-permute-done.9.refs_6_
  21.8 0.3 %collective-permute-done.10.refs_7_ = bf16[128,128]{1,0:T(8,128)(2,1)S(1)} collective-permute-done((bf16[128,128]{1,0:T(8,128)(2,1)S(1)}, bf16[128,128]{1,0:T(8,128)(2,1)S(1)}, u32[]{:S(2)}, u32[]{:S(2)}) %collective-permute-start.10) | collective-permute-done | bytes 32800 | tf_op jit(solution)/shard_map/ppermute | solution.py:511
  22.1 0.4 %shard_map.93 = (bf16[32,128]{1,0:T(8,128)(2,1)S(1)}, bf16[48,128]{1,0:T(8,128)(2,1)S(1)}, bf16[64,128]{1,0:T(8,128)(2,1)S(1)}, bf16[32,128]{1,0:T(8,128)(2,1)S(1)}) custom-call(f32[128,128]{1,0:T(8,128)S(1)} %get-tuple-element.32.refs_0_, f32[128,128]{1,0:T(8,128)S(1)} %get-tuple-element.33.refs_1_, f32[128,128]{1,0:T(8,128)S(1)} %get-tuple-element.34.refs_2_, ...), custom_call_target="tpu_custom_call" | custom-call | bytes 373760 | tf_op jit(solution)/shard_map/pallas_call | solution.py:34
  22.5 1.5 %collective-permute-start.13 = (bf16[32,128]{1,0:T(8,128)(2,1)S(1)}, bf16[32,128]{1,0:T(8,128)(2,1)S(1)}, u32[]{:S(2)}, u32[]{:S(2)}) collective-permute-start(bf16[32,128]{1,0:T(8,128)(2,1)S(1)} %get-tuple-element.43), channel_id=1, source_target_pairs={{0,24},{4,28},{8,16},{12,20},{16,8},{20,12},{24,0},{28,4},{1,25},{... | collective-permute-start | bytes 24584 | tf_op jit(solution)/shard_map/ppermute | solution.py:511
  24.0 1.1 %collective-permute-start.11 = (bf16[48,128]{1,0:T(8,128)(2,1)S(1)}, bf16[48,128]{1,0:T(8,128)(2,1)S(1)}, u32[]{:S(2)}, u32[]{:S(2)}) collective-permute-start(bf16[48,128]{1,0:T(8,128)(2,1)S(1)} %get-tuple-element.41), channel_id=1, source_target_pairs={{0,8},{4,12},{8,0},{12,4},{16,24},{20,28},{24,16},{28,20},{1,9},{5... | collective-permute-start | bytes 36872 | tf_op jit(solution)/shard_map/ppermute | solution.py:511
  25.1 0.0 collective-permute-done.6.refs_3_
  25.1 1.8 %collective-permute-start.12 = (bf16[64,128]{1,0:T(8,128)(2,1)S(1)}, bf16[64,128]{1,0:T(8,128)(2,1)S(1)}, u32[]{:S(2)}, u32[]{:S(2)}) collective-permute-start(bf16[64,128]{1,0:T(8,128)(2,1)S(1)} %get-tuple-element.42), channel_id=1, source_target_pairs={{0,16},{4,20},{8,24},{12,28},{16,0},{20,4},{24,8},{28,12},{1,17},{... | collective-permute-start | bytes 49160 | tf_op jit(solution)/shard_map/ppermute | solution.py:511
  26.9 0.0 collective-permute-done.5.refs_2_
  26.9 0.0 collective-permute-done.4.refs_1_
  26.9 1.5 %shard_map.90 = bf16[256,128]{1,0:T(8,128)(2,1)} custom-call(bf16[80,128]{1,0:T(8,128)(2,1)S(1)} %get-tuple-element.28.refs_0_, bf16[80,128]{1,0:T(8,128)(2,1)S(1)} %collective-permute-done.4.refs_1_, bf16[80,128]{1,0:T(8,128)(2,1)S(1)} %collective-permute-done.5.refs_2_, bf16[80,128]{1,0:T(8,128)(2,1)S(1)} %collective-permute-done.6.refs_3_, ...), custom_call_target="tpu_custom_call" | custom-call | flops 283115520 | bytes 3686912 | tf_op jit(solution)/shard_map/pallas_call | solution.py:34
  28.4 0.0 collective-permute-done.13.refs_3_
  28.4 0.0 collective-permute-done.11.refs_1_
  28.4 1.4 %collective-permute-done.12.refs_2_ = bf16[64,128]{1,0:T(8,128)(2,1)S(1)} collective-permute-done((bf16[64,128]{1,0:T(8,128)(2,1)S(1)}, bf16[64,128]{1,0:T(8,128)(2,1)S(1)}, u32[]{:S(2)}, u32[]{:S(2)}) %collective-permute-start.12) | collective-permute-done | bytes 16416 | tf_op jit(solution)/shard_map/ppermute | solution.py:511
  29.8 0.7 %shard_map.94 = bf16[64,128]{1,0:T(8,128)(2,1)} custom-call(bf16[64,128]{1,0:T(8,128)(2,1)S(1)} %get-tuple-element.24.after_ref.put_ref, bf16[32,128]{1,0:T(8,128)(2,1)S(1)} %get-tuple-element.40.refs_0_, bf16[48,128]{1,0:T(8,128)(2,1)S(1)} %collective-permute-done.11.refs_1_, bf16[64,128]{1,0:T(8,128)(2,1)S(1)} %collective-permute-done.12.refs_2_, ...), custom_call_target="tpu_custom_call" | custom-call | bytes 77824 | tf_op jit(solution)/shard_map/pallas_call | solution.py:34
  (1 shorter events, 0.0 us)
Async XLA Ops:
  1.5 5.2 %collective-permute-start = (bf16[96,128]{1,0:T(8,128)(2,1)S(1)}, bf16[96,128]{1,0:T(8,128)(2,1)S(1)}, u32[]{:S(2)}, u32[]{:S(2)}) collective-permute-start(bf16[96,128]{1,0:T(8,128)(2,1)S(1)} %get-tuple-element.23.mine_ref.refs_1_), channel_id=1, source_target_pairs={{0,4},{4,0},{8,12},{12,8},{16,20},{20,16},{24,28},{28,24},{1,5},{5... | collective-permute-start | bytes 73736 | tf_op jit(solution)/shard_map/ppermute | solution.py:511
  4.5 7.0 %collective-permute-start.7 = (bf16[240,128]{1,0:T(8,128)(2,1)S(1)}, bf16[240,128]{1,0:T(8,128)(2,1)S(1)}, u32[]{:S(2)}, u32[]{:S(2)}) collective-permute-start(bf16[240,128]{1,0:T(8,128)(2,1)S(1)} %get-tuple-element.31.refs_0_), channel_id=1, source_target_pairs={{0,4},{4,0},{8,12},{12,8},{16,20},{20,16},{24,28},{28,24},{1,5},{5... | collective-permute-start | bytes 184328 | tf_op jit(solution)/shard_map/ppermute | solution.py:511
  6.7 6.6 %collective-permute-start.3 = (bf16[160,128]{1,0:T(8,128)(2,1)S(1)}, bf16[160,128]{1,0:T(8,128)(2,1)S(1)}, u32[]{:S(2)}, u32[]{:S(2)}) collective-permute-start(bf16[160,128]{1,0:T(8,128)(2,1)S(1)} %shard_map.88.refs_0_), channel_id=1, source_target_pairs={{0,24},{4,28},{8,16},{12,20},{16,8},{20,12},{24,0},{28,4},{1,25},{... | collective-permute-start | bytes 122888 | tf_op jit(solution)/shard_map/ppermute | solution.py:511
  10.9 4.9 %collective-permute-start.2 = (bf16[160,128]{1,0:T(8,128)(2,1)S(1)}, bf16[160,128]{1,0:T(8,128)(2,1)S(1)}, u32[]{:S(2)}, u32[]{:S(2)}) collective-permute-start(bf16[160,128]{1,0:T(8,128)(2,1)S(1)} %shard_map.88.refs_0_), channel_id=1, source_target_pairs={{0,16},{4,20},{8,24},{12,28},{16,0},{20,4},{24,8},{28,12},{1,17},{... | collective-permute-start | bytes 122888 | tf_op jit(solution)/shard_map/ppermute | solution.py:511
  10.9 4.9 %collective-permute-start.1 = (bf16[160,128]{1,0:T(8,128)(2,1)S(1)}, bf16[160,128]{1,0:T(8,128)(2,1)S(1)}, u32[]{:S(2)}, u32[]{:S(2)}) collective-permute-start(bf16[160,128]{1,0:T(8,128)(2,1)S(1)} %shard_map.88.refs_0_), channel_id=1, source_target_pairs={{0,8},{4,12},{8,0},{12,4},{16,24},{20,28},{24,16},{28,20},{1,9},{5... | collective-permute-start | bytes 122888 | tf_op jit(solution)/shard_map/ppermute | solution.py:511
  17.1 4.7 %collective-permute-start.8 = (bf16[128,128]{1,0:T(8,128)(2,1)S(1)}, bf16[128,128]{1,0:T(8,128)(2,1)S(1)}, u32[]{:S(2)}, u32[]{:S(2)}) collective-permute-start(bf16[128,128]{1,0:T(8,128)(2,1)S(1)} %get-tuple-element.37), channel_id=1, source_target_pairs={{0,1},{1,0},{2,3},{3,2},{4,5},{5,4},{6,7},{7,6},{8,9},{9,8},{10,11... | collective-permute-start | bytes 98312 | tf_op jit(solution)/shard_map/ppermute | solution.py:511
  17.2 4.6 %collective-permute-start.9 = (bf16[128,128]{1,0:T(8,128)(2,1)S(1)}, bf16[128,128]{1,0:T(8,128)(2,1)S(1)}, u32[]{:S(2)}, u32[]{:S(2)}) collective-permute-start(bf16[128,128]{1,0:T(8,128)(2,1)S(1)} %get-tuple-element.38), channel_id=1, source_target_pairs={{0,2},{1,3},{2,0},{3,1},{4,6},{5,7},{6,4},{7,5},{8,10},{9,11},{10,... | collective-permute-start | bytes 98312 | tf_op jit(solution)/shard_map/ppermute | solution.py:511
  18.8 3.3 %collective-permute-start.10 = (bf16[128,128]{1,0:T(8,128)(2,1)S(1)}, bf16[128,128]{1,0:T(8,128)(2,1)S(1)}, u32[]{:S(2)}, u32[]{:S(2)}) collective-permute-start(bf16[128,128]{1,0:T(8,128)(2,1)S(1)} %get-tuple-element.39), channel_id=1, source_target_pairs={{0,3},{1,2},{2,1},{3,0},{4,7},{5,6},{6,5},{7,4},{8,11},{9,10},{10,... | collective-permute-start | bytes 98312 | tf_op jit(solution)/shard_map/ppermute | solution.py:511
  19.7 5.4 %collective-permute-start.6 = (bf16[80,128]{1,0:T(8,128)(2,1)S(1)}, bf16[80,128]{1,0:T(8,128)(2,1)S(1)}, u32[]{:S(2)}, u32[]{:S(2)}) collective-permute-start(bf16[80,128]{1,0:T(8,128)(2,1)S(1)} %get-tuple-element.28.refs_0_), channel_id=1, source_target_pairs={{0,3},{1,2},{2,1},{3,0},{4,7},{5,6},{6,5},{7,4},{8,11},{9,10},{10,... | collective-permute-start | bytes 61448 | tf_op jit(solution)/shard_map/ppermute | solution.py:511
  21.3 5.7 %collective-permute-start.5 = (bf16[80,128]{1,0:T(8,128)(2,1)S(1)}, bf16[80,128]{1,0:T(8,128)(2,1)S(1)}, u32[]{:S(2)}, u32[]{:S(2)}) collective-permute-start(bf16[80,128]{1,0:T(8,128)(2,1)S(1)} %get-tuple-element.28.refs_0_), channel_id=1, source_target_pairs={{0,2},{1,3},{2,0},{3,1},{4,6},{5,7},{6,4},{7,5},{8,10},{9,11},{10,... | collective-permute-start | bytes 61448 | tf_op jit(solution)/shard_map/ppermute | solution.py:511
  21.8 5.2 %collective-permute-start.4 = (bf16[80,128]{1,0:T(8,128)(2,1)S(1)}, bf16[80,128]{1,0:T(8,128)(2,1)S(1)}, u32[]{:S(2)}, u32[]{:S(2)}) collective-permute-start(bf16[80,128]{1,0:T(8,128)(2,1)S(1)} %get-tuple-element.28.refs_0_), channel_id=1, source_target_pairs={{0,1},{1,0},{2,3},{3,2},{4,5},{5,4},{6,7},{7,6},{8,9},{9,8},{10,11... | collective-permute-start | bytes 61448 | tf_op jit(solution)/shard_map/ppermute | solution.py:511
  22.5 5.9 %collective-permute-start.13 = (bf16[32,128]{1,0:T(8,128)(2,1)S(1)}, bf16[32,128]{1,0:T(8,128)(2,1)S(1)}, u32[]{:S(2)}, u32[]{:S(2)}) collective-permute-start(bf16[32,128]{1,0:T(8,128)(2,1)S(1)} %get-tuple-element.43), channel_id=1, source_target_pairs={{0,24},{4,28},{8,16},{12,20},{16,8},{20,12},{24,0},{28,4},{1,25},{... | collective-permute-start | bytes 24584 | tf_op jit(solution)/shard_map/ppermute | solution.py:511
  24.0 4.4 %collective-permute-start.11 = (bf16[48,128]{1,0:T(8,128)(2,1)S(1)}, bf16[48,128]{1,0:T(8,128)(2,1)S(1)}, u32[]{:S(2)}, u32[]{:S(2)}) collective-permute-start(bf16[48,128]{1,0:T(8,128)(2,1)S(1)} %get-tuple-element.41), channel_id=1, source_target_pairs={{0,8},{4,12},{8,0},{12,4},{16,24},{20,28},{24,16},{28,20},{1,9},{5... | collective-permute-start | bytes 36872 | tf_op jit(solution)/shard_map/ppermute | solution.py:511
  25.1 4.6 %collective-permute-start.12 = (bf16[64,128]{1,0:T(8,128)(2,1)S(1)}, bf16[64,128]{1,0:T(8,128)(2,1)S(1)}, u32[]{:S(2)}, u32[]{:S(2)}) collective-permute-start(bf16[64,128]{1,0:T(8,128)(2,1)S(1)} %get-tuple-element.42), channel_id=1, source_target_pairs={{0,16},{4,20},{8,24},{12,28},{16,0},{20,4},{24,8},{28,12},{1,17},{... | collective-permute-start | bytes 49160 | tf_op jit(solution)/shard_map/ppermute | solution.py:511

commit v8 on v7

--- a/solution.py
+++ b/solution.py
@@ -101,25 +101,24 @@
     return taps
 
 
-def adjoint(taps, w_ref):
+def operands(taps):
     rows = taps[0].shape[0]
-    total = jnp.zeros((rows, CHANNELS), F32)
     first = row_index(taps[0].shape) % ROWS < TILE_H
-    latest = []
-    for tap, value in enumerate(taps):
-        both = value + pltpu.roll(value, rows - TILE_H, 0)
-        both = jnp.where(first, both, 0.0).astype(BF16)
-        latest.append((value.astype(BF16), tap + 18))
-        total = total + contract(both, tap, both, tap + 9, w_ref)
-        if len(latest) == 2:
-            (x, i), (y, j) = latest
-            total = total + contract(x, i, y, j, w_ref)
-            latest = []
-    for x, i in latest:
-        total = total + lax.dot_general(
-            x, w_ref[i], (((1,), (1,)), ((), ())), preferred_element_type=F32
-        )
-    return total
+    both = [jnp.where(first, v + pltpu.roll(v, rows - TILE_H, 0), 0.0).astype(BF16) for v in taps]
+    return both, [v.astype(BF16) for v in taps]
+
+
+def adjoint(both, single, w_ref, begin, width):
+    total = jnp.zeros((both[0].shape[0], width), F32)
+    some = pl.ds(begin, width)
+    pairs = [(both[t], t, both[t], t + 9) for t in range(9)]
+    pairs += [(single[t], t + 18, single[t + 1], t + 19) for t in range(0, 8, 2)]
+    for x, i, y, j in pairs:
+        total = total + contract(x, i, y, j, w_ref, some)
+    last = w_ref[26, some, :]
+    return total + lax.dot_general(
+        single[8], last, (((1,), (1,)), ((), ())), preferred_element_type=F32
+    )
 
 
 def share(partial_ref, outs):
@@ -130,9 +129,9 @@
         out[...] = partial_ref[:, pl.ds(begin, lanes)].astype(out.dtype)
 
 
-def contract(x, i, y, j, w_ref):
+def contract(x, i, y, j, w_ref, some):
     left = jnp.concatenate([x, y], axis=1)
-    right = jnp.concatenate([w_ref[i], w_ref[j]], axis=1)
+    right = jnp.concatenate([w_ref[i, some, :], w_ref[j, some, :]], axis=1)
     return lax.dot_general(left, right, (((1,), (1,)), ((), ())), preferred_element_type=F32)
 
 
@@ -175,7 +174,7 @@
         lambda p: sides[pl.ds(p, ROWS, stride=2), :],
         lambda p: sides[pl.ds(2 * ROWS + p, ROWS, stride=2), :],
     )
-    partial_ref[...] = adjoint(fold_taps(columns, rims), w_ref)
+    partial_ref[...] = adjoint(*operands(fold_taps(columns, rims)), w_ref, 0, CHANNELS)
     share(partial_ref, outs)
 
 
@@ -215,8 +214,24 @@
     own_ref[...] = jnp.concatenate(parts, axis=0).astype(BF16)
 
 
-def pair_adjoint_kernel(taps_ref, w_ref, *refs):
-    pieces, outs, (partial_ref, sides) = refs[:4], refs[4:8], refs[8:]
+def half_adjoint(both, single, w_ref, half, partial_ref, outs):
+    lanes = outs[0].shape[1]
+    begin = pl.multiple_of(half * (2 * lanes), 256)
+    partial_ref[...] = adjoint(both, single, w_ref, begin, 2 * lanes)
+    like = lax.axis_index("chan") % 2
+    for k, out in enumerate(outs):
+        begin = pl.multiple_of((like ^ k) * lanes, 128)
+        out[...] = partial_ref[:, pl.ds(begin, lanes)].astype(out.dtype)
+
+
+def near_adjoint_kernel(left_ref, w_ref, mine_ref, send_ref, partial_ref):
+    both, single = [[left_ref[i, t] for t in range(9)] for i in range(2)]
+    half = lax.axis_index("chan") // 2
+    half_adjoint(both, single, w_ref, half, partial_ref, [mine_ref, send_ref])
+
+
+def far_adjoint_kernel(taps_ref, w_ref, *refs):
+    pieces, outs, left_ref, (partial_ref, sides) = refs[:4], refs[4:6], refs[6], refs[7:]
     place = lax.axis_index("tile") // 2
     zero = jnp.zeros((2 * ROWS, taps_ref.shape[2]), BF16)
     left, right = zero, zero
@@ -239,8 +254,11 @@
         if e == 2:
             value = jnp.concatenate([value[:ROWS] + rims[0][b], value[ROWS:]], axis=0)
         taps.append(value)
-    partial_ref[...] = adjoint(taps, w_ref)
-    share(partial_ref, outs)
+    both, single = operands(taps)
+    for t in range(9):
+        left_ref[0, t] = both[t]
+        left_ref[1, t] = single[t]
+    half_adjoint(both, single, w_ref, 1 - lax.axis_index("chan") // 2, partial_ref, outs)
 
 
 def pair_norm_kernel(*refs):
@@ -465,7 +483,9 @@
 
 
 def pair_prep_kernel(own, capacity, *refs):
-    ins, (take_ref, pack_ref, put_ref, *outs) = refs[:5], refs[5:-2]
+    lines_ref, refs = refs[0], refs[1:]
+    ins, (take_ref, pack_ref, put_ref, after_ref, *outs) = refs[:4], refs[4:-2]
+    after_ref[...] = lines_ref[...]
     source_ref, sems = refs[-2:]
     copies = load_all(ins, [source_ref] + outs, sems)
     copies[0].wait()
@@ -489,8 +509,18 @@
         copy.wait()
 
 
+def weight_copies(weight_ref, w_ref, sems):
+    return [
+        pltpu.make_async_copy(weight_ref.at[pl.ds(3 * k, 3)], w_ref.at[pl.ds(3 * k, 3)], sems.at[k])
+        for k in range(9)
+    ]
+
+
 def pair_fold_kernel(*refs):
-    taps_ref, pair_ref = refs[-2:]
+    weight_ref, taps_ref, w_ref, pair_ref, sems = refs[4:]
+    weights = weight_copies(weight_ref, w_ref, sems)
+    for copy in weights:
+        copy.start()
     mine, theirs = refs[:2], refs[2:4]
     area = pair_ref.shape[0] // 2
     size = mine[0].shape[0]
@@ -505,6 +535,8 @@
     columns = folded_columns(pair_ref, wide, 2 * wide, lambda p: zero, lambda p: zero)
     for tap, value in enumerate(fold_taps(columns)):
         taps_ref[tap] = value
+    for copy in weights:
+        copy.wait()
 
 
 def swapped(block, axis, k):
@@ -537,37 +569,51 @@
         loose=(0, 1),
     )
     peer = swapped(early, "tile", 1)
-    others = [swapped(part, "tile", 1) for part in parts]
-    ins = [cell_source, weight] + [v.reshape(1, lanes) for v in (gain, shift, bias)]
-    take, pack, put, weight, gain, shift, bias = call(
+    ins = [cell_source] + [v.reshape(1, lanes) for v in (gain, shift, bias)]
+    take, pack, put, parts[0], gain, shift, bias = call(
         functools.partial(pair_prep_kernel, own, capacity),
         [
             shape(3 * CELLS, members * own),
             shape(slots, 2 * CELLS),
             shape(own, slots),
+            shape(SPLIT, lanes),
         ]
         + [jax.ShapeDtypeStruct(v.shape, v.dtype) for v in ins[1:]],
-        ins,
+        parts[:1] + ins,
         [pltpu.VMEM(cell_source.shape, jnp.int32), pltpu.SemaphoreType.DMA((len(ins),))],
-        loose=range(5),
-    )
+        loose=range(1, 5),
+    )
+    others = [swapped(part, "tile", 1) for part in parts]
     (block,) = call(join_kernel, [shape(2 * own + 4 * ROWS, lanes)], [early, peer, put])
     pieces = [block] + [swapped(block, "tile", k) for k in (2, 4, 6)]
-    (taps,) = call(
+    taps, weight = call(
         pair_fold_kernel,
-        [jax.ShapeDtypeStruct((9, 2 * CELLS, lanes), F32)],
-        parts + [early] + others + [peer],
-        [pltpu.VMEM((2 * area, lanes), F32)],
+        [
+            jax.ShapeDtypeStruct((9, 2 * CELLS, lanes), F32),
+            jax.ShapeDtypeStruct(weight.shape, BF16),
+        ],
+        parts + [early] + others + [peer, weight],
+        [pltpu.VMEM((2 * area, lanes), F32), pltpu.SemaphoreType.DMA((9,))],
+        loose=(4,),
     )
     cell = shape(2 * CELLS, lanes, F32)
-    mine, *sends = call(
-        pair_adjoint_kernel,
-        [cell] + [shape(2 * CELLS, lanes)] * 3,
+    part = pltpu.VMEM((2 * CELLS, 2 * lanes), F32)
+    work = 2 * 27 * CELLS * lanes * CHANNELS
+    straight, crossed, left = call(
+        far_adjoint_kernel,
+        [shape(2 * CELLS, lanes)] * 2 + [jax.ShapeDtypeStruct((2, 9, 2 * CELLS, lanes), BF16)],
         [taps, weight] + pieces,
-        [pltpu.VMEM((2 * CELLS, CHANNELS), F32), pltpu.VMEM((4 * ROWS, lanes), F32)],
-        flops=4 * 27 * CELLS * lanes * CHANNELS,
-    )
-    sends = chan_swaps(sends)
+        [part, pltpu.VMEM((4 * ROWS, lanes), F32)],
+        flops=work,
+    )
+    mine, twin = call(
+        near_adjoint_kernel,
+        [cell, shape(2 * CELLS, lanes)],
+        [left, weight],
+        [part],
+        flops=work,
+    )
+    sends = chan_swaps([twin, straight, crossed])
     hat, slope, scale, cells = call(
         pair_norm_kernel,
         [cell, cell, shape(2, lanes, F32), shape(CELLS + 2 * ROWS, lanes)],

time: 30.8 us -> 30.7 us (level)
  waiting for transfers between devices: 5.69 us -> 4.68 us
  Pallas kernels: 7.83 us -> 8.64 us
    ppermute x14, waiting for transfers between devices: 5.69 us -> 4.68 us  [swapped(): lax.ppermute(block, axis, [(i, i ^ k) for i in range(lax.axis_size(axis))])]
    pallas_call x9 -> x10, Pallas kernels: 7.83 us -> 8.64 us  [call(): pl.pallas_call(kernel, out_shape=outs, in_specs=[FAR if i in loose else V...]
  transfers between devices with their start and end apart: 14 -> 14, of which waited for: 4 -> 4; matrix products, arithmetic and copies ran while one was open for 0% -> 0% of each run, Pallas kernels for 16% -> 18%
where the time goes in v8:
time: 30.7 us; the launch traced here: 30.4 us
  starting transfers between devices  16.4 us (53%)
  Pallas kernels  8.64 us (28%)
  waiting for transfers between devices  4.68 us (15%)
  between operations  0.71 us (2%)
    ppermute x14, starting transfers between devices, swapped(): lax.ppermute(block, axis, [(i, i ^ k) for i in range(lax.axis_size(axis))])  16.4 us
    pallas_call x10, Pallas kernels, call(): pl.pallas_call(kernel, out_shape=outs, in_specs=[FAR if i in loose else V...  8.64 us
    ppermute x14, waiting for transfers between devices, swapped(): lax.ppermute(block, axis, [(i, i ^ k) for i in range(lax.axis_size(axis))])  4.68 us
  transfers between devices with their start and end apart: 14, of which 4 were waited for; matrix products, arithmetic and copies ran while one was open for 0% of the time, Pallas kernels for 18%

profile of v8, /device:TPU:0, one launch (start us, length us, event | category | flops | bytes accessed | tf_op | source)
XLA Modules:
  0.0 30.4 jit_solution(5861846989040638611)
XLA Ops:
  0.6 0.9 %shard_map.86 = (bf16[96,128]{1,0:T(8,128)(2,1)S(1)}, bf16[240,128]{1,0:T(8,128)(2,1)S(1)}) custom-call(bf16[64,128]{1,0:T(8,128)(2,1)} %tokens_ref.1, bf16[256,128]{1,0:T(8,128)(2,1)} %bitcast.6), custom_call_target="tpu_custom_call" | custom-call | bytes 167936 | tf_op jit(solution)/shard_map/pallas_call | solution.py:34
  1.5 3.0 %collective-permute-start = (bf16[96,128]{1,0:T(8,128)(2,1)S(1)}, bf16[96,128]{1,0:T(8,128)(2,1)S(1)}, u32[]{:S(2)}, u32[]{:S(2)}) collective-permute-start(bf16[96,128]{1,0:T(8,128)(2,1)S(1)} %get-tuple-element.26.mine_ref.refs_1_), channel_id=1, source_target_pairs={{0,4},{4,0},{8,12},{12,8},{16,20},{20,16},{24,28},{28,24},{1,5},{5... | collective-permute-start | bytes 73736 | tf_op jit(solution)/shard_map/ppermute | solution.py:543
  4.5 1.0 %shard_map.87 = (bf16[192,512]{1,0:T(8,128)(2,1)S(1)}, bf16[128,128]{1,0:T(8,128)(2,1)S(1)}, bf16[64,128]{1,0:T(8,128)(2,1)S(1)}, bf16[240,128]{1,0:T(8,128)(2,1...) custom-call(bf16[240,128]{1,0:T(8,128)(2,1)S(1)} %get-tuple-element.27.refs_0_, ...), custom_call_target="tpu_custom_call" | custom-call | bytes 373760 | tf_op jit(solution)/shard_map/pallas_call | solution.py:34
  5.5 0.1 collective-permute-start.7
  5.6 0.8 %collective-permute-done.peer_ref.refs_3_ = bf16[96,128]{1,0:T(8,128)(2,1)S(1)} collective-permute-done((bf16[96,128]{1,0:T(8,128)(2,1)S(1)}, bf16[96,128]{1,0:T(8,128)(2,1)S(1)}, u32[]{:S(2)}, u32[]{:S(2)}) %collective-permute-start) | collective-permute-done | bytes 24608 | tf_op jit(solution)/shard_map/ppermute | solution.py:543
  6.4 4.2 %collective-permute-start.3 = (bf16[160,128]{1,0:T(8,128)(2,1)S(1)}, bf16[160,128]{1,0:T(8,128)(2,1)S(1)}, u32[]{:S(2)}, u32[]{:S(2)}) collective-permute-start(bf16[160,128]{1,0:T(8,128)(2,1)S(1)} %shard_map.88.refs_0_), channel_id=1, source_target_pairs={{0,24},{4,28},{8,16},{12,20},{16,8},{20,12},{24,0},{28,4},{1,25},{... | collective-permute-start | bytes 122888 | tf_op jit(solution)/shard_map/ppermute | solution.py:543
  10.6 0.0 collective-permute-start.2
  10.6 0.6 %collective-permute-start.1 = (bf16[160,128]{1,0:T(8,128)(2,1)S(1)}, bf16[160,128]{1,0:T(8,128)(2,1)S(1)}, u32[]{:S(2)}, u32[]{:S(2)}) collective-permute-start(bf16[160,128]{1,0:T(8,128)(2,1)S(1)} %shard_map.88.refs_0_), channel_id=1, source_target_pairs={{0,8},{4,12},{8,0},{12,4},{16,24},{20,28},{24,16},{28,20},{1,9},{5... | collective-permute-start | bytes 122888 | tf_op jit(solution)/shard_map/ppermute | solution.py:543
  11.2 0.0 collective-permute-done.7.refs_2_
  11.2 2.0 %shard_map.90 = (f32[9,128,128]{2,1,0:T(8,128)S(1)}, bf16[27,512,128]{2,1,0:T(8,128)(2,1)S(1)}) custom-call(bf16[240,128]{1,0:T(8,128)(2,1)S(1)} %get-tuple-element.33.refs_0_, bf16[96,128]{1,0:T(8,128)(2,1)S(1)} %get-tuple-element.26.mine_ref.refs_1_, bf16[240,128]{1,0:T(8,128)(2,1)S(1)} %collective-permute-done.7.refs_2_, ...), custom_call_target="tpu_custom_call" | custom-call | bytes 7839744 | tf_op jit(solution)/shard_map/pallas_call | solution.py:34
  13.2 0.0 collective-permute-done.3.refs_3_
  13.2 2.2 %collective-permute-done.2.refs_2_ = bf16[160,128]{1,0:T(8,128)(2,1)S(1)} collective-permute-done((bf16[160,128]{1,0:T(8,128)(2,1)S(1)}, bf16[160,128]{1,0:T(8,128)(2,1)S(1)}, u32[]{:S(2)}, u32[]{:S(2)}) %collective-permute-start.2) | collective-permute-done | bytes 40992 | tf_op jit(solution)/shard_map/ppermute | solution.py:543
  15.5 0.0 collective-permute-done.1.refs_1_
  15.5 0.7 %shard_map.92 = (bf16[128,128]{1,0:T(8,128)(2,1)S(1)}, bf16[128,128]{1,0:T(8,128)(2,1)S(1)}, bf16[2,9,128,128]{3,2,1,0:T(8,128)(2,1)S(1)}) custom-call(f32[9,128,128]{2,1,0:T(8,128)S(1)} %get-tuple-element.36.taps_ref, bf16[27,512,128]{2,1,0:T(8,128)(2,1)S(1)} %get-tuple-element.34.refs_4_.w_ref, bf16[160,128]{1,0:T(8,128)(2,1)S(1)} %shard_map.88.refs_0_, ...), custom_call_target="tpu_custom_call" | custom-call | flops 226492416 | bytes 4947968 | tf_op jit(solution)/shard_map/pallas_call | solution.py:34
  16.2 0.8 %shard_map.93 = (f32[128,128]{1,0:T(8,128)S(1)}, bf16[128,128]{1,0:T(8,128)(2,1)S(1)}) custom-call(bf16[2,9,128,128]{3,2,1,0:T(8,128)(2,1)S(1)} %get-tuple-element.37.left_ref, bf16[27,512,128]{2,1,0:T(8,128)(2,1)S(1)} %get-tuple-element.34.refs_4_.w_ref), custom_call_target="tpu_custom_call" | custom-call | flops 226492416 | bytes 4227072 | tf_op jit(solution)/shard_map/pallas_call | solution.py:34
  17.0 0.1 collective-permute-start.8
  17.0 1.6 %collective-permute-start.9 = (bf16[128,128]{1,0:T(8,128)(2,1)S(1)}, bf16[128,128]{1,0:T(8,128)(2,1)S(1)}, u32[]{:S(2)}, u32[]{:S(2)}) collective-permute-start(bf16[128,128]{1,0:T(8,128)(2,1)S(1)} %get-tuple-element.44), channel_id=1, source_target_pairs={{0,2},{1,3},{2,0},{3,1},{4,6},{5,7},{6,4},{7,5},{8,10},{9,11},{10,... | collective-permute-start | bytes 98312 | tf_op jit(solution)/shard_map/ppermute | solution.py:543
  18.6 0.3 collective-permute-start.10
  18.9 0.7 %shard_map.89 = (f32[128,128]{1,0:T(8,128)S(1)}, f32[128,128]{1,0:T(8,128)S(1)}, f32[2,128]{1,0:T(2,128)S(1)}, bf16[80,128]{1,0:T(8,128)(2,1)S(1)}) custom-call(bf16[160,128]{1,0:T(8,128)(2,1)S(1)} %shard_map.88.refs_0_, bf16[160,128]{1,0:T(8,128)(2,1)S(1)} %collective-permute-done.1.refs_1_, bf16[160,128]{1,0:T(8,128)(2,1)S(1)} %collective-permute-done.2.refs_2_, ...), custom_call_target="tpu_custom_call" | custom-call | flops 25165824 | bytes 514048 | tf_op jit(solution)/shard_map/pallas_call | solution.py:34
  19.6 1.5 %collective-permute-start.6 = (bf16[80,128]{1,0:T(8,128)(2,1)S(1)}, bf16[80,128]{1,0:T(8,128)(2,1)S(1)}, u32[]{:S(2)}, u32[]{:S(2)}) collective-permute-start(bf16[80,128]{1,0:T(8,128)(2,1)S(1)} %get-tuple-element.32.refs_0_), channel_id=1, source_target_pairs={{0,3},{1,2},{2,1},{3,0},{4,7},{5,6},{6,5},{7,4},{8,11},{9,10},{10,... | collective-permute-start | bytes 61448 | tf_op jit(solution)/shard_map/ppermute | solution.py:543
  21.1 0.5 %collective-permute-start.5 = (bf16[80,128]{1,0:T(8,128)(2,1)S(1)}, bf16[80,128]{1,0:T(8,128)(2,1)S(1)}, u32[]{:S(2)}, u32[]{:S(2)}) collective-permute-start(bf16[80,128]{1,0:T(8,128)(2,1)S(1)} %get-tuple-element.32.refs_0_), channel_id=1, source_target_pairs={{0,2},{1,3},{2,0},{3,1},{4,6},{5,7},{6,4},{7,5},{8,10},{9,11},{10,... | collective-permute-start | bytes 61448 | tf_op jit(solution)/shard_map/ppermute | solution.py:543
  21.6 0.0 collective-permute-done.8.refs_5_
  21.6 0.0 collective-permute-start.4
  21.7 0.0 collective-permute-done.9.refs_6_
  21.7 0.3 %collective-permute-done.10.refs_7_ = bf16[128,128]{1,0:T(8,128)(2,1)S(1)} collective-permute-done((bf16[128,128]{1,0:T(8,128)(2,1)S(1)}, bf16[128,128]{1,0:T(8,128)(2,1)S(1)}, u32[]{:S(2)}, u32[]{:S(2)}) %collective-permute-start.10) | collective-permute-done | bytes 32800 | tf_op jit(solution)/shard_map/ppermute | solution.py:543
  22.0 0.4 %shard_map.94 = (bf16[32,128]{1,0:T(8,128)(2,1)S(1)}, bf16[48,128]{1,0:T(8,128)(2,1)S(1)}, bf16[64,128]{1,0:T(8,128)(2,1)S(1)}, bf16[32,128]{1,0:T(8,128)(2,1)S(1)}) custom-call(f32[128,128]{1,0:T(8,128)S(1)} %get-tuple-element.38.refs_0_, f32[128,128]{1,0:T(8,128)S(1)} %get-tuple-element.39.refs_1_, f32[128,128]{1,0:T(8,128)S(1)} %get-tuple-element.40.refs_2_, ...), custom_call_target="tpu_custom_call" | custom-call | bytes 373760 | tf_op jit(solution)/shard_map/pallas_call | solution.py:34
  22.4 1.6 %collective-permute-start.13 = (bf16[32,128]{1,0:T(8,128)(2,1)S(1)}, bf16[32,128]{1,0:T(8,128)(2,1)S(1)}, u32[]{:S(2)}, u32[]{:S(2)}) collective-permute-start(bf16[32,128]{1,0:T(8,128)(2,1)S(1)} %get-tuple-element.49), channel_id=1, source_target_pairs={{0,24},{4,28},{8,16},{12,20},{16,8},{20,12},{24,0},{28,4},{1,25},{... | collective-permute-start | bytes 24584 | tf_op jit(solution)/shard_map/ppermute | solution.py:543
  24.0 1.0 %collective-permute-start.11 = (bf16[48,128]{1,0:T(8,128)(2,1)S(1)}, bf16[48,128]{1,0:T(8,128)(2,1)S(1)}, u32[]{:S(2)}, u32[]{:S(2)}) collective-permute-start(bf16[48,128]{1,0:T(8,128)(2,1)S(1)} %get-tuple-element.47), channel_id=1, source_target_pairs={{0,8},{4,12},{8,0},{12,4},{16,24},{20,28},{24,16},{28,20},{1,9},{5... | collective-permute-start | bytes 36872 | tf_op jit(solution)/shard_map/ppermute | solution.py:543
  25.0 0.0 collective-permute-done.6.refs_3_
  25.0 1.8 %collective-permute-start.12 = (bf16[64,128]{1,0:T(8,128)(2,1)S(1)}, bf16[64,128]{1,0:T(8,128)(2,1)S(1)}, u32[]{:S(2)}, u32[]{:S(2)}) collective-permute-start(bf16[64,128]{1,0:T(8,128)(2,1)S(1)} %get-tuple-element.48), channel_id=1, source_target_pairs={{0,16},{4,20},{8,24},{12,28},{16,0},{20,4},{24,8},{28,12},{1,17},{... | collective-permute-start | bytes 49160 | tf_op jit(solution)/shard_map/ppermute | solution.py:543
  26.8 0.0 collective-permute-done.5.refs_2_
  26.8 0.0 collective-permute-done.4.refs_1_
  26.8 1.5 %shard_map.91 = bf16[256,128]{1,0:T(8,128)(2,1)} custom-call(bf16[80,128]{1,0:T(8,128)(2,1)S(1)} %get-tuple-element.32.refs_0_, bf16[80,128]{1,0:T(8,128)(2,1)S(1)} %collective-permute-done.4.refs_1_, bf16[80,128]{1,0:T(8,128)(2,1)S(1)} %collective-permute-done.5.refs_2_, bf16[80,128]{1,0:T(8,128)(2,1)S(1)} %collective-permute-done.6.refs_3_, ...), custom_call_target="tpu_custom_call" | custom-call | flops 283115520 | bytes 3686912 | tf_op jit(solution)/shard_map/pallas_call | solution.py:34
  28.3 0.0 collective-permute-done.13.refs_3_
  28.3 0.0 collective-permute-done.11.refs_1_
  28.3 1.4 %collective-permute-done.12.refs_2_ = bf16[64,128]{1,0:T(8,128)(2,1)S(1)} collective-permute-done((bf16[64,128]{1,0:T(8,128)(2,1)S(1)}, bf16[64,128]{1,0:T(8,128)(2,1)S(1)}, u32[]{:S(2)}, u32[]{:S(2)}) %collective-permute-start.12) | collective-permute-done | bytes 16416 | tf_op jit(solution)/shard_map/ppermute | solution.py:543
  29.6 0.7 %shard_map.95 = bf16[64,128]{1,0:T(8,128)(2,1)} custom-call(bf16[64,128]{1,0:T(8,128)(2,1)S(1)} %get-tuple-element.28.after_ref.put_ref, bf16[32,128]{1,0:T(8,128)(2,1)S(1)} %get-tuple-element.46.refs_0_, bf16[48,128]{1,0:T(8,128)(2,1)S(1)} %collective-permute-done.11.refs_1_, bf16[64,128]{1,0:T(8,128)(2,1)S(1)} %collective-permute-done.12.refs_2_, ...), custom_call_target="tpu_custom_call" | custom-call | bytes 77824 | tf_op jit(solution)/shard_map/pallas_call | solution.py:34
  (1 shorter events, 0.0 us)
Async XLA Ops:
  1.5 4.8 %collective-permute-start = (bf16[96,128]{1,0:T(8,128)(2,1)S(1)}, bf16[96,128]{1,0:T(8,128)(2,1)S(1)}, u32[]{:S(2)}, u32[]{:S(2)}) collective-permute-start(bf16[96,128]{1,0:T(8,128)(2,1)S(1)} %get-tuple-element.26.mine_ref.refs_1_), channel_id=1, source_target_pairs={{0,4},{4,0},{8,12},{12,8},{16,20},{20,16},{24,28},{28,24},{1,5},{5... | collective-permute-start | bytes 73736 | tf_op jit(solution)/shard_map/ppermute | solution.py:543
  5.5 5.7 %collective-permute-start.7 = (bf16[240,128]{1,0:T(8,128)(2,1)S(1)}, bf16[240,128]{1,0:T(8,128)(2,1)S(1)}, u32[]{:S(2)}, u32[]{:S(2)}) collective-permute-start(bf16[240,128]{1,0:T(8,128)(2,1)S(1)} %get-tuple-element.33.refs_0_), channel_id=1, source_target_pairs={{0,4},{4,0},{8,12},{12,8},{16,20},{20,16},{24,28},{28,24},{1,5},{5... | collective-permute-start | bytes 184328 | tf_op jit(solution)/shard_map/ppermute | solution.py:543
  6.4 6.9 %collective-permute-start.3 = (bf16[160,128]{1,0:T(8,128)(2,1)S(1)}, bf16[160,128]{1,0:T(8,128)(2,1)S(1)}, u32[]{:S(2)}, u32[]{:S(2)}) collective-permute-start(bf16[160,128]{1,0:T(8,128)(2,1)S(1)} %shard_map.88.refs_0_), channel_id=1, source_target_pairs={{0,24},{4,28},{8,16},{12,20},{16,8},{20,12},{24,0},{28,4},{1,25},{... | collective-permute-start | bytes 122888 | tf_op jit(solution)/shard_map/ppermute | solution.py:543
  10.6 4.9 %collective-permute-start.2 = (bf16[160,128]{1,0:T(8,128)(2,1)S(1)}, bf16[160,128]{1,0:T(8,128)(2,1)S(1)}, u32[]{:S(2)}, u32[]{:S(2)}) collective-permute-start(bf16[160,128]{1,0:T(8,128)(2,1)S(1)} %shard_map.88.refs_0_), channel_id=1, source_target_pairs={{0,16},{4,20},{8,24},{12,28},{16,0},{20,4},{24,8},{28,12},{1,17},{... | collective-permute-start | bytes 122888 | tf_op jit(solution)/shard_map/ppermute | solution.py:543
  10.6 4.9 %collective-permute-start.1 = (bf16[160,128]{1,0:T(8,128)(2,1)S(1)}, bf16[160,128]{1,0:T(8,128)(2,1)S(1)}, u32[]{:S(2)}, u32[]{:S(2)}) collective-permute-start(bf16[160,128]{1,0:T(8,128)(2,1)S(1)} %shard_map.88.refs_0_), channel_id=1, source_target_pairs={{0,8},{4,12},{8,0},{12,4},{16,24},{20,28},{24,16},{28,20},{1,9},{5... | collective-permute-start | bytes 122888 | tf_op jit(solution)/shard_map/ppermute | solution.py:543
  17.0 4.7 %collective-permute-start.8 = (bf16[128,128]{1,0:T(8,128)(2,1)S(1)}, bf16[128,128]{1,0:T(8,128)(2,1)S(1)}, u32[]{:S(2)}, u32[]{:S(2)}) collective-permute-start(bf16[128,128]{1,0:T(8,128)(2,1)S(1)} %get-tuple-element.43), channel_id=1, source_target_pairs={{0,1},{1,0},{2,3},{3,2},{4,5},{5,4},{6,7},{7,6},{8,9},{9,8},{10,11... | collective-permute-start | bytes 98312 | tf_op jit(solution)/shard_map/ppermute | solution.py:543
  17.0 4.6 %collective-permute-start.9 = (bf16[128,128]{1,0:T(8,128)(2,1)S(1)}, bf16[128,128]{1,0:T(8,128)(2,1)S(1)}, u32[]{:S(2)}, u32[]{:S(2)}) collective-permute-start(bf16[128,128]{1,0:T(8,128)(2,1)S(1)} %get-tuple-element.44), channel_id=1, source_target_pairs={{0,2},{1,3},{2,0},{3,1},{4,6},{5,7},{6,4},{7,5},{8,10},{9,11},{10,... | collective-permute-start | bytes 98312 | tf_op jit(solution)/shard_map/ppermute | solution.py:543
  18.6 3.3 %collective-permute-start.10 = (bf16[128,128]{1,0:T(8,128)(2,1)S(1)}, bf16[128,128]{1,0:T(8,128)(2,1)S(1)}, u32[]{:S(2)}, u32[]{:S(2)}) collective-permute-start(bf16[128,128]{1,0:T(8,128)(2,1)S(1)} %get-tuple-element.45), channel_id=1, source_target_pairs={{0,3},{1,2},{2,1},{3,0},{4,7},{5,6},{6,5},{7,4},{8,11},{9,10},{10,... | collective-permute-start | bytes 98312 | tf_op jit(solution)/shard_map/ppermute | solution.py:543
  19.6 5.4 %collective-permute-start.6 = (bf16[80,128]{1,0:T(8,128)(2,1)S(1)}, bf16[80,128]{1,0:T(8,128)(2,1)S(1)}, u32[]{:S(2)}, u32[]{:S(2)}) collective-permute-start(bf16[80,128]{1,0:T(8,128)(2,1)S(1)} %get-tuple-element.32.refs_0_), channel_id=1, source_target_pairs={{0,3},{1,2},{2,1},{3,0},{4,7},{5,6},{6,5},{7,4},{8,11},{9,10},{10,... | collective-permute-start | bytes 61448 | tf_op jit(solution)/shard_map/ppermute | solution.py:543
  21.1 5.7 %collective-permute-start.5 = (bf16[80,128]{1,0:T(8,128)(2,1)S(1)}, bf16[80,128]{1,0:T(8,128)(2,1)S(1)}, u32[]{:S(2)}, u32[]{:S(2)}) collective-permute-start(bf16[80,128]{1,0:T(8,128)(2,1)S(1)} %get-tuple-element.32.refs_0_), channel_id=1, source_target_pairs={{0,2},{1,3},{2,0},{3,1},{4,6},{5,7},{6,4},{7,5},{8,10},{9,11},{10,... | collective-permute-start | bytes 61448 | tf_op jit(solution)/shard_map/ppermute | solution.py:543
  21.6 5.2 %collective-permute-start.4 = (bf16[80,128]{1,0:T(8,128)(2,1)S(1)}, bf16[80,128]{1,0:T(8,128)(2,1)S(1)}, u32[]{:S(2)}, u32[]{:S(2)}) collective-permute-start(bf16[80,128]{1,0:T(8,128)(2,1)S(1)} %get-tuple-element.32.refs_0_), channel_id=1, source_target_pairs={{0,1},{1,0},{2,3},{3,2},{4,5},{5,4},{6,7},{7,6},{8,9},{9,8},{10,11... | collective-permute-start | bytes 61448 | tf_op jit(solution)/shard_map/ppermute | solution.py:543
  22.4 5.9 %collective-permute-start.13 = (bf16[32,128]{1,0:T(8,128)(2,1)S(1)}, bf16[32,128]{1,0:T(8,128)(2,1)S(1)}, u32[]{:S(2)}, u32[]{:S(2)}) collective-permute-start(bf16[32,128]{1,0:T(8,128)(2,1)S(1)} %get-tuple-element.49), channel_id=1, source_target_pairs={{0,24},{4,28},{8,16},{12,20},{16,8},{20,12},{24,0},{28,4},{1,25},{... | collective-permute-start | bytes 24584 | tf_op jit(solution)/shard_map/ppermute | solution.py:543
  24.0 4.3 %collective-permute-start.11 = (bf16[48,128]{1,0:T(8,128)(2,1)S(1)}, bf16[48,128]{1,0:T(8,128)(2,1)S(1)}, u32[]{:S(2)}, u32[]{:S(2)}) collective-permute-start(bf16[48,128]{1,0:T(8,128)(2,1)S(1)} %get-tuple-element.47), channel_id=1, source_target_pairs={{0,8},{4,12},{8,0},{12,4},{16,24},{20,28},{24,16},{28,20},{1,9},{5... | collective-permute-start | bytes 36872 | tf_op jit(solution)/shard_map/ppermute | solution.py:543
  25.0 4.6 %collective-permute-start.12 = (bf16[64,128]{1,0:T(8,128)(2,1)S(1)}, bf16[64,128]{1,0:T(8,128)(2,1)S(1)}, u32[]{:S(2)}, u32[]{:S(2)}) collective-permute-start(bf16[64,128]{1,0:T(8,128)(2,1)S(1)} %get-tuple-element.48), channel_id=1, source_target_pairs={{0,16},{4,20},{8,24},{12,28},{16,0},{20,4},{24,8},{28,12},{1,17},{... | collective-permute-start | bytes 49160 | tf_op jit(solution)/shard_map/ppermute | solution.py:543
